TPU v7x, 512 devices: a whole 4x8x8 slice. The times are simulated.
512 devices in a mesh: section: 8 (over y_hi, core), dp: 64 (over y_lo, z, x).
Axes of the slice: x: 4, y: 8 (y_hi: 4, y_lo: 2; y = y_hi * 2 + y_lo), z: 8, core: 2. Of those that a mesh axis runs over, the one named last changes fastest.
Arguments:
- token_ids: int32 [8192], P('dp'), may hold values from 0 to 65535
- embed_table: bfloat16 [65536, 8192], P('section', 'dp'), may hold values from -6 to 6
- norm_gain: float32 [8192], replicated, may hold values from 0.1 to 1.9
- cotangent: bfloat16 [8192, 8192], P('dp', 'section'), may hold values from -6 to 6
Outputs:
- grad_table: bfloat16 [65536, 8192], P('section', 'dp')
- input_grad: bfloat16 [8192, 8192], P('dp', 'section')
All inputs are finite; a program needn't handle non-finite values.
Results may differ from a plain program's by a relative error of at most 0.0044.
Values may be sent and summed in bfloat16 or wider, within the bound.
No kernel may reach another device: no remote copies, remote signals or barrier semaphores. Data moves between devices by JAX's collectives and lax.ppermute only.
A program may use at most 64 MiB of HBM per device.

v0:
```python
import jax
import jax.numpy as jnp
from jax import lax
from jax.sharding import Mesh
from jax.sharding import PartitionSpec as P

SECTION = ("section_0", "section_1")


epsilon = 1e-05


def from_everyone(array, axis):
    count = lax.axis_size(axis)
    return lax.all_to_all(
        jnp.broadcast_to(array[None], (count, *array.shape)), axis, 0, 0, tiled=True
    )


def laid_out(tiles, dim):
    lengths = list(tiles.shape[1:])
    lengths[dim] *= tiles.shape[0]
    return jnp.moveaxis(tiles, 0, dim).reshape(lengths)


def gathered_copies(array, axis, dim):
    tiles = from_everyone(array, axis)
    return laid_out(tiles, dim)


def cut_along(array, dim, count):
    before, after = (array.shape[:dim], array.shape[dim + 1 :])
    return jnp.moveaxis(array.reshape(*before, count, -1, *after), dim, 0)


def exchange_in_order(tiles, axes, turns):
    lengths = [lax.axis_size(a) for a in axes]
    tiles = tiles.reshape(*lengths, *tiles.shape[1:])
    for k in turns:
        tiles = lax.all_to_all(tiles, axes[k], split_axis=k, concat_axis=k, tiled=True)
    return tiles.reshape(-1, *tiles.shape[len(axes) :])


def core_and_chips(array, groups, turns, split_dim, concat_dim):
    count = lax.axis_size(groups[0]) * lax.axis_size(groups[1])
    tiles = cut_along(array, split_dim, count)
    return laid_out(exchange_in_order(tiles, groups, turns), concat_dim)


def norm_backward(full_rows, own_cotangent, norm_gain):
    embedded = full_rows.astype(jnp.float32)
    square_mean = jnp.mean(embedded * embedded, axis=1, keepdims=True)
    inverse = lax.rsqrt(square_mean + epsilon)
    scaled = own_cotangent.astype(jnp.float32) * norm_gain[None, :]
    inner = jnp.mean(scaled * embedded, axis=1, keepdims=True)
    return (inverse * scaled - embedded * inverse * inverse * inverse * inner).astype(jnp.bfloat16)


def on_device(token_ids, embed_table, norm_gain, cotangent):
    section_index = lax.axis_index(SECTION)
    section_count = lax.axis_size(SECTION)
    replica_count = lax.axis_size("dp")
    vocab_section, columns = embed_table.shape
    local_tokens = cotangent.shape[0]
    section_width = cotangent.shape[1]
    share_tokens = local_tokens // section_count
    all_ids = gathered_copies(token_ids, "dp", 0)
    full_cotangent = lax.all_gather(cotangent, SECTION, axis=1, tiled=True)
    local_ids = all_ids - section_index * vocab_section
    inside = (local_ids >= 0) & (local_ids < vocab_section)
    clipped = jnp.clip(local_ids, 0, vocab_section - 1)
    picked = jnp.take(embed_table, clipped, axis=0).astype(jnp.float32)
    partial_rows = jnp.where(inside[:, None], picked, jnp.zeros_like(picked))
    stacked = partial_rows.reshape(replica_count, local_tokens, columns)
    column_share = lax.psum_scatter(
        stacked.astype(jnp.bfloat16), SECTION, scatter_dimension=1, tiled=True
    )
    full_rows = lax.all_to_all(column_share, "dp", split_axis=0, concat_axis=2, tiled=True)[0]
    own_cotangent = lax.dynamic_slice_in_dim(
        full_cotangent, section_index * share_tokens, share_tokens, 0
    )
    input_grad = norm_backward(full_rows, own_cotangent, norm_gain)
    split_grad = input_grad.reshape(share_tokens, section_count, section_width)
    own_grad = core_and_chips(split_grad, ("section_0", "section_1"), (1, 0), 1, 0).reshape(
        local_tokens, section_width
    )
    small_back = lax.all_to_all(input_grad[None], "dp", split_axis=2, concat_axis=0, tiled=True)
    returned = lax.all_gather(small_back, SECTION, axis=1, tiled=True)
    grad_tokens = returned.reshape(all_ids.shape[0], columns).astype(jnp.float32)
    masked = jnp.where(inside[:, None], grad_tokens, jnp.zeros_like(grad_tokens))
    summed = jnp.zeros((vocab_section, columns), jnp.float32).at[clipped].add(masked)
    return (summed.astype(jnp.bfloat16), own_grad)


def solution(mesh):
    split = Mesh(mesh.devices.reshape(4, 2, mesh.shape["dp"]), ("section_0", "section_1", "dp"))
    return jax.shard_map(
        on_device,
        mesh=split,
        in_specs=(P("dp"), P(SECTION, "dp"), P(), P("dp", SECTION)),
        out_specs=(P(SECTION, "dp"), P("dp", SECTION)),
        check_vma=False,
    )
```

profile of v0, /device:TPU:6, one launch (start us, length us, event | category | flops | bytes accessed | tf_op | source)
XLA Modules:
  0.0 353.9 jit_solution(14496536936811350758)
XLA Ops:
  7.2 0.0 copy-start
  7.2 1.4 broadcast_in_dim.38
  8.6 14.8 %all-to-all-start = ((s32[64,1,128]{2,1,0:T(1,128)}), s32[64,1,128]{2,1,0:T(1,128)S(1)}, u32[]{:S(2)}, u32[]{:S(2)}) async-start(s32[64,1,128]{2,1,0:T(1,128)} %broadcast_in_dim.38), calls=%async_computation | async-start | bytes 65536 | tf_op jit(solution)/shard_map/all_to_all | solution.py:15
  23.4 0.0 reduce-scatter.2.cloned.1.call-start
  23.5 8.9 %all-to-all-done = s32[64,1,128]{2,1,0:T(1,128)S(1)} async-done(((s32[64,1,128]{2,1,0:T(1,128)}), s32[64,1,128]{2,1,0:T(1,128)S(1)}, u32[]{:S(2)}, u32[]{:S(2)}) %all-to-all-start) | async-done | bytes 32800 | tf_op jit(solution)/shard_map/all_to_all | solution.py:15
  32.5 0.0 copy-done
  32.5 29.5 %gather_fusion = bf16[8192,128]{1,0:T(8,128)(2,1)} fusion(bf16[8192,128]{1,0:T(8,128)(2,1)S(1)} %copy-done, s32[8192]{0:T(1024)S(1)} %broadcast_clamp_fusion), kind=kCustom, calls=%fused_computation | custom fusion | bytes 4227072 | tf_op jit(solution)/shard_map/jit(_take)/gather | solution.py:72
  62.0 0.0 copy-start.1
  62.0 6.9 %select_convert_fusion = bf16[64,128,128]{2,1,0:T(8,128)(2,1)} fusion(bf16[64,128,128]{2,1,0:T(8,128)(2,1)} %bitcast.58, pred[64,128]{1,0:T(8,128)(4,1)S(1)} %get-tuple-element.2, pred[64,128]{1,0:T(8,128)(4,1)S(1)} %fusion.10), kind=kLoop, calls=%fused_computation.3 | loop fusion | flops 4194304 | bytes 4210688 | tf_op jit(solution)/shard_map/convert_element_type | solution.py:76
  68.9 0.0 reduce-scatter.2.cloned.1.call-update
  68.9 0.0 all-gather.4.cloned.1.call-start
  68.9 0.7 all-gather.4.cloned.1.call-update
  69.6 40.2 %reduce-scatter.2.cloned.1.call-done = bf16[64,16,128]{2,1,0:T(8,128)(2,1)} async-done(((bf16[64,128,128]{2,1,0:T(8,128)(2,1)}), bf16[64,16,128]{2,1,0:T(8,128)(2,1)}) %reduce-scatter.2.cloned.1.call-update) | async-done | bytes 262160 | tf_op jit(solution)/shard_map/reduce_scatter | solution.py:75
  109.8 10.6 %all-to-all-start.1 = ((bf16[64,16,128]{2,1,0:T(8,128)(2,1)}), bf16[64,16,128]{2,1,0:T(8,128)(2,1)S(1)}, u32[]{:S(2)}, u32[]{:S(2)}) async-start(bf16[64,16,128]{2,1,0:T(8,128)(2,1)} %reduce-scatter.2.cloned.1.call-done), calls=%async_computation.2 | async-start | bytes 524288 | tf_op jit(solution)/shard_map/all_to_all | solution.py:78
  120.5 0.0 all-gather.6.cloned.1.call-start
  120.5 10.5 %all-to-all-done.1 = bf16[64,16,128]{2,1,0:T(8,128)(2,1)S(1)} async-done(((bf16[64,16,128]{2,1,0:T(8,128)(2,1)}), bf16[64,16,128]{2,1,0:T(8,128)(2,1)S(1)}, u32[]{:S(2)}, u32[]{:S(2)}) %all-to-all-start.1) | async-done | bytes 262176 | tf_op jit(solution)/shard_map/all_to_all | solution.py:78
  131.1 0.2 copy.25
  131.2 0.2 fusion.2
  131.4 19.2 %all-gather.4.cloned.1.call-done = bf16[128,8192]{1,0:T(8,128)(2,1)} async-done(((bf16[128,1024]{1,0:T(8,128)(2,1)}), bf16[128,8192]{1,0:T(8,128)(2,1)}) %all-gather.4.cloned.1.call-update) | async-done | bytes 2097168 | tf_op jit(solution)/shard_map/all_gather | solution.py:68
  150.6 0.0 copy-done.1
  150.6 1.4 fusion.8
  152.0 1.3 fusion.7
  153.3 6.7 %copy.26 = bf16[1,16,8192]{1,0,2:T(2,128)(2,1)} copy(bf16[1,16,8192]{2,1,0:T(8,128)(2,1)S(1)} %bitcast.61) | data formatting | bytes 524288 | tf_op jit(solution)/shard_map/broadcast_in_dim | solution.py:87
  160.0 0.5 broadcast.164
  160.5 46.5 %reduce.3 = bf16[8192,16]{1,0:T(8,128)(2,1)} reduce(bf16[8192,1,16]{2,1,0:T(2,128)(2,1)} %bitcast.56, bf16[]{:T(256)} %broadcast.164), dimensions={1}, to_apply=%bitcast.51.reduce_sub_computation | reduce | bytes 524290
  207.0 3.8 %reshape.134 = bf16[64,2,1024]{2,1,0:T(2,128)(2,1)S(1)} reshape(bf16[8192,16]{1,0:T(8,128)(2,1)} %reduce.3) | data formatting | bytes 524288
  210.8 22.0 %all_to_all.43 = bf16[64,2,1024]{2,1,0:T(2,128)(2,1)S(1)} all-to-all(bf16[64,2,1024]{2,1,0:T(2,128)(2,1)S(1)} %reshape.134), channel_id=1, replica_groups=mesh['section_0'=4,'section_1'=2,'dp'=64] {'dp'}, dimensions={0} | all-to-all | bytes 524288 | tf_op jit(solution)/shard_map/all_to_all | solution.py:87
  232.8 7.6 %reshape.135 = bf16[8192,1,16]{2,1,0:T(2,128)(2,1)} reshape(bf16[64,2,1024]{2,1,0:T(2,128)(2,1)S(1)} %all_to_all.43) | data formatting | bytes 524288
  240.4 7.9 %copy.27 = bf16[1,16,8192]{2,1,0:T(8,128)(2,1)S(1)} copy(bf16[1,16,8192]{1,0,2:T(2,128)(2,1)} %bitcast.57) | data formatting | bytes 524288 | tf_op jit(solution)/shard_map/all_to_all | solution.py:87
  248.4 0.7 bitcast_bitcast_fusion
  249.1 0.0 all-gather.6.cloned.1.call-update
  249.1 0.2 copy.35
  249.3 0.2 copy.30
  249.5 3.9 %all_to_all.44 = bf16[4,2,16,1,1024]{4,2,0,3,1:T(8,128)(2,1)S(1)} all-to-all(bf16[4,2,16,1,1024]{4,2,0,3,1:T(8,128)(2,1)S(1)} %copy.31), channel_id=1, replica_groups=mesh['section_0'=4,'section_1'=2,'dp'=64] {'section_1'}, dimensions={1} | all-to-all | bytes 524288 | tf_op jit(solution)/shard_map/all_to_all | solution.py:40
  253.4 0.7 copy.32
  254.1 4.2 %all-to-all-start.4 = ((bf16[4,2,16,1,1024]{4,2,1,3,0:T(8,128)(2,1)}), bf16[4,2,16,1,1024]{4,2,1,3,0:T(8,128)(2,1)S(1)}, u32[]{:S(2)}, u32[]{:S(2)}) async-start(bf16[4,2,16,1,1024]{4,2,1,3,0:T(8,128)(2,1)} %copy.32), calls=%async_computation.5 | async-start | bytes 524288 | tf_op jit(solution)/shard_map/all_to_all | solution.py:40
  258.4 17.7 %all-to-all-done.4 = bf16[4,2,16,1,1024]{4,2,1,3,0:T(8,128)(2,1)S(1)} async-done(((bf16[4,2,16,1,1024]{4,2,1,3,0:T(8,128)(2,1)}), bf16[4,2,16,1,1024]{4,2,1,3,0:T(8,128)(2,1)S(1)}, u32[]{:S(2)}, u32[]{:S(2)}) %all-to-all-start.4) | async-done | bytes 262176 | tf_op jit(solution)/shard_map/all_to_all | solution.py:40
  276.1 11.6 %all-gather.6.cloned.1.call-done = bf16[64,1,128,128]{3,0,1,2:T(8,128)(2,1)} async-done(((bf16[64,1,16,128]{3,0,1,2:T(8,128)(2,1)}), bf16[64,1,128,128]{3,0,1,2:T(8,128)(2,1)}) %all-gather.6.cloned.1.call-update) | async-done | bytes 2097168 | tf_op jit(solution)/shard_map/all_gather | solution.py:88
  287.6 2.8 copy.29
  290.5 5.4 %bitcast_select_fusion = f32[8192,128]{1,0:T(8,128)} fusion(f32[64,1,128,128]{3,2,0,1:T(8,128)S(1)} %copy.29, pred[8192]{0:T(1024)(128)(4,1)S(1)} %fusion.9), kind=kLoop, calls=%fused_computation.2 | loop fusion | flops 1048576 | bytes 8396800 | tf_op jit(solution)/shard_map/jit(_where)/select_n | solution.py:90
  295.9 47.1 %scatter_custom_fusion = f32[8192,128]{1,0:T(8,128)} fusion(s32[8192]{0:T(1024)S(1)} %bitcast.73, f32[8192,128]{1,0:T(8,128)} %bitcast_select_fusion, f32[]{:T(128)} %constant.14.clone.1), kind=kCustom, calls=%fused_computation.4 | custom fusion | flops 1048576 | bytes 4194816 | tf_op jit(solution)/shard_map/scatter-add | solution.py:91
  343.0 3.7 %convert_element_type.50 = bf16[8192,128]{1,0:T(8,128)(2,1)} convert(f32[8192,128]{1,0:T(8,128)} %scatter_custom_fusion) | non-fusion elementwise | flops 1048576 | bytes 6291456 | tf_op jit(solution)/shard_map/convert_element_type | solution.py:92
  346.7 0.7 copy.39
  (10 shorter events, 0.2 us)
Async XLA Ops:
  7.2 25.4 %copy-start = (bf16[8192,128]{1,0:T(8,128)(2,1)S(1)}, bf16[8192,128]{1,0:T(8,128)(2,1)}, u32[]{:S(2)}) copy-start(bf16[8192,128]{1,0:T(8,128)(2,1)} %param.5) | copy-start | bytes 6291460
  8.6 23.8 %all-to-all-start = ((s32[64,1,128]{2,1,0:T(1,128)}), s32[64,1,128]{2,1,0:T(1,128)S(1)}, u32[]{:S(2)}, u32[]{:S(2)}) async-start(s32[64,1,128]{2,1,0:T(1,128)} %broadcast_in_dim.38), calls=%async_computation | async-start | bytes 65536 | tf_op jit(solution)/shard_map/all_to_all | solution.py:15
  23.4 86.4 %reduce-scatter.2.cloned.1.call-start = ((), (), s32[]{:S(2)}) async-start(), calls=%async_computation.6 | async-start | bytes 2359296 | tf_op jit(solution)/shard_map/reduce_scatter | solution.py:75
  62.0 88.6 %copy-start.1 = (f32[8192]{0:T(1024)S(1)}, f32[8192]{0:T(1024)}, u32[]{:S(2)}) copy-start(f32[8192]{0:T(1024)} %param.6) | copy-start | bytes 98308
  68.9 81.7 %all-gather.4.cloned.1.call-start = ((), (), s32[]{:S(2)}) async-start(), calls=%async_computation.7 | async-start | bytes 2359296 | tf_op jit(solution)/shard_map/all_gather | solution.py:68
  109.8 21.2 %all-to-all-start.1 = ((bf16[64,16,128]{2,1,0:T(8,128)(2,1)}), bf16[64,16,128]{2,1,0:T(8,128)(2,1)S(1)}, u32[]{:S(2)}, u32[]{:S(2)}) async-start(bf16[64,16,128]{2,1,0:T(8,128)(2,1)} %reduce-scatter.2.cloned.1.call-done), calls=%async_computation.2 | async-start | bytes 524288 | tf_op jit(solution)/shard_map/all_to_all | solution.py:78
  120.5 167.2 %all-gather.6.cloned.1.call-start = ((), (), s32[]{:S(2)}) async-start(), calls=%async_computation.8 | async-start | bytes 2359296 | tf_op jit(solution)/shard_map/all_gather | solution.py:88
  254.1 21.9 %all-to-all-start.4 = ((bf16[4,2,16,1,1024]{4,2,1,3,0:T(8,128)(2,1)}), bf16[4,2,16,1,1024]{4,2,1,3,0:T(8,128)(2,1)S(1)}, u32[]{:S(2)}, u32[]{:S(2)}) async-start(bf16[4,2,16,1,1024]{4,2,1,3,0:T(8,128)(2,1)} %copy.32), calls=%async_computation.5 | async-start | bytes 524288 | tf_op jit(solution)/shard_map/all_to_all | solution.py:40
Sparse Core Ops, SparseCore 0:
  69.0 40.7 reduce-scatter.1
  111.9 38.6 all-gather.3
  249.2 38.3 all-gather.5
where the time goes:
time: 360 us; the launch traced here: 354 us
  other arithmetic  113 us (31%)
  waiting for transfers between devices  109 us (30%)
  local copies, waits for them, and re-layouts  62.9 us (17%)
  starting transfers between devices  29.8 us (8%)
  blocking collectives  26 us (7%)
  between operations  13.9 us (4%)
    scatter-add x1, other arithmetic, on_device(): jnp.zeros((vocab_section, columns), jnp.float32).at[clipped].add(masked)  47.1 us
    unnamed x1, other arithmetic  46.5 us
    reduce_scatter x1, waiting for transfers between devices, on_device(): lax.psum_scatter(stacked.astype(jnp.bfloat16), SECTION, scatter_dimension...  40.2 us
    gather x1, local copies, waits for them, and re-layouts, on_device(): picked = jnp.take(embed_table, clipped, axis=0).astype(jnp.float32)  29.5 us
    all_to_all x1, blocking collectives, on_device(): lax.all_to_all(input_grad[None], 'dp', split_axis=2, concat_axis=0, tiled...  22 us
    all_gather x1, waiting for transfers between devices, on_device(): full_cotangent = lax.all_gather(cotangent, SECTION, axis=1, tiled=True)  19.2 us
    all_to_all x1, waiting for transfers between devices, exchange_in_order(): lax.all_to_all(tiles, axes[k], split_axis=k, concat_axis=k, tiled=True)  17.7 us
    all_to_all x1, starting transfers between devices, from_everyone(): lax.all_to_all(jnp.broadcast_to(array[None], (count, *array.shape)), axis...  14.8 us
  transfers between devices with their start and end apart: 6, of which 6 were waited for; matrix products, arithmetic and copies ran while one was open for 0% of the time, Pallas kernels for 0%

commit v1 on v0

v1 whole, which is shorter than its diff:
```python
import functools

import jax
import jax.numpy as jnp
from jax import lax
from jax.experimental import pallas as pl
from jax.experimental.pallas import tpu as pltpu
from jax.sharding import PartitionSpec as P

epsilon = 1e-05
SLOTS = 48
LANES = 128


def whole(shape, space=pltpu.VMEM):
    return pl.BlockSpec(shape, lambda *_: (0,) * len(shape), memory_space=space)


def plan_kernel(section_ref, ids_ref, index_ref, count_ref, *, slots, vocab_section):
    ids = ids_ref[...].astype(jnp.float32)
    ids = jnp.concatenate([ids, ids], axis=0)
    ids = ids.T.astype(jnp.int32)
    local = ids - section_ref[0] * vocab_section
    inside = (local >= 0) & (local < vocab_section)
    before = (
        lax.broadcasted_iota(jnp.int32, (LANES, LANES), 1)
        < lax.broadcasted_iota(jnp.int32, (LANES, LANES), 0)
    )
    ones = jnp.where(inside, 1.0, 0.0)
    rank = jnp.dot(
        jnp.where(before, 1.0, 0.0).astype(jnp.bfloat16),
        ones.astype(jnp.bfloat16),
        preferred_element_type=jnp.float32,
    ).astype(jnp.int32)
    rank = jnp.where(inside, rank, -1)
    for c in range(slots):
        index_ref[pl.ds(c, 1), :] = jnp.sum(jnp.where(rank == c, local, 0), axis=0, keepdims=True)
    count_ref[...] = jnp.broadcast_to(
        jnp.sum(ones, axis=0, keepdims=True).astype(jnp.int32), count_ref.shape
    )


def pick_kernel(index_ref, table_ref, rows_ref, wide_ref, picked_ref, *, slots, groups):
    step = 256

    def widen(i, carry):
        wide_ref[pl.ds(i * step, step), :] = table_ref[pl.ds(i * step, step), :].astype(jnp.float32)
        return carry

    lax.fori_loop(0, table_ref.shape[0] // step, widen, 0)

    def group(g, carry):
        for c in range(slots):
            picked_ref[pl.ds(c, 1), :] = wide_ref[pl.ds(index_ref[c, g], 1), :]
        rows_ref[g] = picked_ref[...].astype(jnp.bfloat16)
        return carry

    lax.fori_loop(0, groups, group, 0)


def slot_of(ids_row, slots, vocab_section):
    wide = jnp.broadcast_to(ids_row // vocab_section, (LANES, LANES))
    tall = wide.astype(jnp.float32).T.astype(jnp.int32)
    first = lax.broadcasted_iota(jnp.int32, (LANES, LANES), 0)
    second = lax.broadcasted_iota(jnp.int32, (LANES, LANES), 1)
    same = wide == tall
    as_row = jnp.sum(jnp.where(same & (first < second), 1, 0), axis=0, keepdims=True)
    as_column = jnp.sum(jnp.where(same & (second < first), 1.0, 0.0), axis=1, keepdims=True)
    row_slot = jnp.where(as_row < slots, wide[:1] * slots + as_row, -1)
    as_column = as_column.astype(jnp.int32)
    column_slot = jnp.where(as_column < slots, tall[:, :1] * slots + as_column, -1)
    return row_slot, column_slot


def deal_kernel(ids_ref, cotangent_ref, dealt_ref, *, slots, sections, vocab_section):
    row_slot, _ = slot_of(ids_ref[...], slots, vocab_section)
    cotangent = cotangent_ref[...]
    for s in range(sections):
        wanted = lax.broadcasted_iota(jnp.int32, (slots, LANES), 0) + s * slots == row_slot
        dealt_ref[s] = jnp.dot(
            jnp.where(wanted, 1.0, 0.0).astype(jnp.bfloat16),
            cotangent,
            preferred_element_type=jnp.float32,
        ).astype(jnp.bfloat16)


def collect_kernel(ids_ref, dealt_ref, own_ref, *, slots, sections, vocab_section):
    _, column_slot = slot_of(ids_ref[...], slots, vocab_section)
    total = jnp.zeros(own_ref.shape, jnp.float32)
    for s in range(sections):
        wanted = lax.broadcasted_iota(jnp.int32, (LANES, slots), 1) + s * slots == column_slot
        total = total + jnp.dot(
            jnp.where(wanted, 1.0, 0.0).astype(jnp.bfloat16),
            dealt_ref[s],
            preferred_element_type=jnp.float32,
        )
    own_ref[...] = total.astype(jnp.bfloat16)


def norm_kernel(rows_ref, cotangent_ref, gain_ref, by_column_ref, by_feature_ref):
    pieces, slots, columns = rows_ref.shape
    per = cotangent_ref.shape[2] // columns
    width = pieces * columns

    def parts(k, j):
        embedded = rows_ref[k * per + j].astype(jnp.float32)
        own = cotangent_ref[k, :, j * columns : (j + 1) * columns].astype(jnp.float32)
        return embedded, own * gain_ref[pl.ds(k * per + j, 1), :]

    def sums(k, carry):
        squares, inners = carry
        for j in range(per):
            embedded, scaled = parts(k, j)
            squares = squares + embedded * embedded
            inners = inners + scaled * embedded
        return squares, inners

    zeros = jnp.zeros((slots, columns), jnp.float32)
    squares, inners = lax.fori_loop(0, pieces // per, sums, (zeros, zeros))
    square_mean = jnp.sum(squares, axis=1, keepdims=True) * (1.0 / width)
    inner = jnp.sum(inners, axis=1, keepdims=True) * (1.0 / width)
    inverse = lax.rsqrt(square_mean + epsilon)
    pull = inverse * inverse * inverse * inner

    def grads(k, carry):
        for j in range(per):
            embedded, scaled = parts(k, j)
            grad = (inverse * scaled - embedded * pull).astype(jnp.bfloat16)
            by_column_ref[k * per + j] = grad
            by_feature_ref[k, :, j * columns : (j + 1) * columns] = grad
        return carry

    lax.fori_loop(0, pieces // per, grads, 0)


def add_kernel(index_ref, count_ref, grads_ref, table_ref, total_ref, wide_ref, *, groups):
    step = 256
    slots = grads_ref.shape[1]

    def clear(i, carry):
        total_ref[pl.ds(i * step, step), :] = jnp.zeros((step, LANES), jnp.float32)
        return carry

    lax.fori_loop(0, total_ref.shape[0] // step, clear, 0)

    def group(g, carry):
        wide_ref[...] = grads_ref[g].astype(jnp.float32)

        def one(c, carry):
            row = pl.ds(index_ref[c, g], 1)
            total_ref[row, :] = total_ref[row, :] + wide_ref[pl.ds(c, 1), :]
            return carry

        lax.fori_loop(0, jnp.minimum(count_ref[0, g], slots), one, 0)
        return carry

    lax.fori_loop(0, groups, group, 0)

    def narrow(i, carry):
        table_ref[pl.ds(i * step, step), :] = total_ref[pl.ds(i * step, step), :].astype(jnp.bfloat16)
        return carry

    lax.fori_loop(0, total_ref.shape[0] // step, narrow, 0)


def call(kernel, operands, spaces, outs, scratch=()):
    return pl.pallas_call(
        kernel,
        in_specs=[whole(o.shape, s) for o, s in zip(operands, spaces)],
        out_specs=[whole(o.shape) for o in outs],
        out_shape=outs,
        scratch_shapes=list(scratch),
    )(*operands)


def passage(slots, section, all_ids, own_ids, embed_table, norm_gain, cotangent):
    vocab_section, columns = embed_table.shape
    groups = all_ids.shape[0]
    tokens, features = cotangent.shape
    sections = lax.axis_size("section")
    V, S = pltpu.VMEM, pltpu.SMEM
    bf16 = functools.partial(jax.ShapeDtypeStruct, dtype=jnp.bfloat16)
    i32 = functools.partial(jax.ShapeDtypeStruct, dtype=jnp.int32)
    (dealt,) = call(
        functools.partial(deal_kernel, slots=slots, sections=sections, vocab_section=vocab_section),
        (own_ids, cotangent), (V, V), [bf16((sections, slots, features))],
    )
    their_cotangent = lax.all_to_all(dealt, "section", 0, 0, tiled=True)
    index, count = call(
        functools.partial(plan_kernel, slots=slots, vocab_section=vocab_section),
        (section, all_ids), (S, V), [i32((slots, LANES)), i32((8, LANES))],
    )
    (rows,) = call(
        functools.partial(pick_kernel, slots=slots, groups=groups),
        (index, embed_table), (S, V), [bf16((groups, slots, columns))],
        [pltpu.VMEM((vocab_section, columns), jnp.float32), pltpu.VMEM((slots, columns), jnp.float32)],
    )
    full_rows = lax.all_to_all(rows, "dp", 0, 0, tiled=True)
    gain = norm_gain.reshape(groups, columns)
    by_column, by_feature = call(
        norm_kernel, (full_rows, their_cotangent, gain), (V, V, V),
        [bf16(full_rows.shape), bf16(their_cotangent.shape)],
    )
    back = lax.all_to_all(by_column, "dp", 0, 0, tiled=True)
    home = lax.all_to_all(by_feature, "section", 0, 0, tiled=True)
    (grad_table,) = call(
        functools.partial(add_kernel, groups=groups),
        (index, count, back), (S, S, V), [bf16((vocab_section, columns))],
        [pltpu.VMEM((vocab_section, columns), jnp.float32), pltpu.VMEM((slots, columns), jnp.float32)],
    )
    (own_grad,) = call(
        functools.partial(collect_kernel, slots=slots, sections=sections, vocab_section=vocab_section),
        (own_ids, home), (V, V), [bf16((tokens, features))],
    )
    return grad_table, own_grad


def on_device(token_ids, embed_table, norm_gain, cotangent):
    vocab_section = embed_table.shape[0]
    groups = lax.axis_size("dp")
    tokens = token_ids.shape[0]
    section = lax.axis_index("section").reshape(1)
    own_ids = token_ids.reshape(1, tokens)
    all_ids = lax.all_to_all(
        jnp.broadcast_to(own_ids[None], (groups, 1, tokens)), "dp", 0, 0, tiled=True
    ).reshape(groups, tokens)
    sections = jnp.arange(lax.axis_size("section"))
    counts = jnp.sum(all_ids[:, :, None] // vocab_section == sections, axis=1)
    fits = jnp.max(counts) <= SLOTS
    return lax.cond(
        fits,
        functools.partial(passage, SLOTS),
        functools.partial(passage, tokens),
        section, all_ids, own_ids, embed_table, norm_gain, cotangent,
    )


def solution(mesh):
    return jax.shard_map(
        on_device,
        mesh=mesh,
        in_specs=(P("dp"), P("section", "dp"), P(), P("dp", "section")),
        out_specs=(P("section", "dp"), P("dp", "section")),
        check_vma=False,
    )
```

time: 360 us -> 160 us (0.44); the launches traced: 354 us -> 158 us
  other arithmetic: 113 us -> 1.82 us
  waiting for transfers between devices: 109 us -> 43 us
  local copies, waits for them, and re-layouts: 62.9 us -> 2.19 us
  Pallas kernels: 0 us -> 27.1 us
  blocking collectives: 26 us -> 49.8 us
  between operations: 13.9 us -> 1.3 us
    scatter-add x1 -> x0, other arithmetic: 47.1 us -> none  [on_device(): jnp.zeros((vocab_section, columns), jnp.float32).at[clipped].add(masked)]
    unnamed x1 -> x0, other arithmetic: 46.5 us -> none
    reduce_scatter x1 -> x0, waiting for transfers between devices: 40.2 us -> none  [on_device(): lax.psum_scatter(stacked.astype(jnp.bfloat16), SECTION, scatter_dimension...]
    all_gather x2 -> x0, waiting for transfers between devices: 30.7 us -> none  [the longest x1 19.2 us: on_device(): full_cotangent = lax.all_gather(cotangent, SECTION, axis=1, tiled=True)]
    gather x1 -> x0, local copies, waits for them, and re-layouts: 29.5 us -> none  [on_device(): picked = jnp.take(embed_table, clipped, axis=0).astype(jnp.float32)]
    pallas_call x0 -> x6, Pallas kernels: none -> 27.1 us  [call(): pl.pallas_call(kernel, in_specs=[whole(o.shape, s) for o, s in zip(operan...]
    all_to_all x2, blocking collectives: 26 us -> 49.8 us  [the longest x1 26.3 us: passage(): full_rows = lax.all_to_all(rows, 'dp', 0, 0, tiled=True)]
    unnamed x10 -> x0, local copies, waits for them, and re-layouts: 12.8 us -> none
  transfers between devices with their start and end apart: 6 -> 3, of which waited for: 6 -> 3; matrix products, arithmetic and copies ran while one was open for 0% -> 0% of each run, Pallas kernels for 0% -> 6%
where the time goes in v1:
time: 160 us; the launch traced here: 158 us
  blocking collectives  49.8 us (31%)
  waiting for transfers between devices  43 us (27%)
  starting transfers between devices  32.8 us (20%)
  Pallas kernels  27.1 us (17%)
  local copies, waits for them, and re-layouts  2.19 us (1%)
  other arithmetic  1.82 us (1%)
    pallas_call x6, Pallas kernels, call(): pl.pallas_call(kernel, in_specs=[whole(o.shape, s) for o, s in zip(operan...  27.1 us
    all_to_all x1, blocking collectives, passage(): full_rows = lax.all_to_all(rows, 'dp', 0, 0, tiled=True)  26.3 us
    all_to_all x1, blocking collectives, passage(): home = lax.all_to_all(by_feature, 'section', 0, 0, tiled=True)  23.5 us
    all_to_all x1, waiting for transfers between devices, passage(): back = lax.all_to_all(by_column, 'dp', 0, 0, tiled=True)  18.4 us
    all_to_all x1, waiting for transfers between devices, passage(): their_cotangent = lax.all_to_all(dealt, 'section', 0, 0, tiled=True)  15.7 us
    all_to_all x1, starting transfers between devices, on_device(): lax.all_to_all(jnp.broadcast_to(own_ids[None], (groups, 1, tokens)), 'dp'...  14.8 us
    all_to_all x1, starting transfers between devices, passage(): back = lax.all_to_all(by_column, 'dp', 0, 0, tiled=True)  11.8 us
    all_to_all x1, waiting for transfers between devices, on_device(): lax.all_to_all(jnp.broadcast_to(own_ids[None], (groups, 1, tokens)), 'dp'...  8.96 us
  transfers between devices with their start and end apart: 3, of which 3 were waited for; matrix products, arithmetic and copies ran while one was open for 0% of the time, Pallas kernels for 6%

profile of v1, /device:TPU:6, one launch (start us, length us, event | category | flops | bytes accessed | tf_op | source)
XLA Modules:
  0.0 158.1 jit_solution(173677746208600257)
XLA Ops:
  0.6 1.3 broadcast_in_dim.2
  1.9 14.8 %all-to-all-start.8 = ((s32[64,1,128]{2,1,0:T(1,128)}), s32[64,1,128]{2,1,0:T(1,128)S(1)}, u32[]{:S(2)}, u32[]{:S(2)}) async-start(s32[64,1,128]{2,1,0:T(1,128)} %broadcast_in_dim.2), calls=%async_computation.8 | async-start | bytes 65536 | tf_op jit(solution)/shard_map/all_to_all | solution.py:224
  16.8 9.0 %all-to-all-done.8 = s32[64,1,128]{2,1,0:T(1,128)S(1)} async-done(((s32[64,1,128]{2,1,0:T(1,128)}), s32[64,1,128]{2,1,0:T(1,128)S(1)}, u32[]{:S(2)}, u32[]{:S(2)}) %all-to-all-start.8) | async-done | bytes 32800 | tf_op jit(solution)/shard_map/all_to_all | solution.py:224
  25.7 1.2 convert_reduce_fusion
  26.9 0.6 reduce_max.9
  28.2 129.9 %conditional.1 = (bf16[8192,128]{1,0:T(8,128)(2,1)}, bf16[128,1024]{1,0:T(8,128)(2,1)}) conditional(s32[]{:T(128)} %convert_element_type.7, (s32[]{:T(128)}, s32[64,128]{1,0:T(8,128)S(1)}, bf16[8192,128]{1,0:T(8,128)(2,1)}, s32[128]{0:T(128)}, bf16[128,1024]{1,0:T(8,128)(2,1)}, /*index=5*/f32[8192]{0:T(1024)}) %tuple.22, (s32[]{:T(128)}, ...), branch_computations={%region_2.3_spmd, %region_3.4_spmd} | conditional | bytes 37882048 | solution.py:230
  28.2 0.0 copy-start.2
  28.2 2.5 %branch_1_fun.8 = bf16[8,48,1024]{2,1,0:T(8,128)(2,1)} custom-call(s32[1,128]{1,0:T(1,128)} %bitcast.14, bf16[128,1024]{1,0:T(8,128)(2,1)} %get-tuple-element.61.cotangent_ref), custom_call_target="tpu_custom_call" | custom-call | tf_op jit(solution)/shard_map/cond/branch_1_fun/pallas_call | solution.py:167
  30.8 6.2 %all-to-all-start.5 = ((bf16[8,48,1024]{2,1,0:T(8,128)(2,1)}), bf16[8,48,1024]{2,1,0:T(8,128)(2,1)S(1)}, u32[]{:S(2)}, u32[]{:S(2)}) async-start(bf16[8,48,1024]{2,1,0:T(8,128)(2,1)} %branch_1_fun.8), calls=%async_computation.5 | async-start | bytes 1572864 | tf_op jit(solution)/shard_map/cond/branch_1_fun/all_to_all | solution.py:188
  37.0 1.2 branch_1_fun.6
  38.1 0.0 copy-done.2
  38.1 0.0 copy-start.6
  38.1 6.3 %branch_1_fun.7 = bf16[64,48,128]{2,1,0:T(8,128)(2,1)} custom-call(s32[48,128]{1,0:T(8,128)} %get-tuple-element.36.index_ref, bf16[8192,128]{1,0:T(8,128)(2,1)S(1)} %copy-done.2), custom_call_target="tpu_custom_call" | custom-call | tf_op jit(solution)/shard_map/cond/branch_1_fun/pallas_call | solution.py:167
  44.4 15.7 %all-to-all-done.5.cotangent_ref = bf16[8,48,1024]{2,1,0:T(8,128)(2,1)S(1)} async-done(((bf16[8,48,1024]{2,1,0:T(8,128)(2,1)}), bf16[8,48,1024]{2,1,0:T(8,128)(2,1)S(1)}, u32[]{:S(2)}, u32[]{:S(2)}) %all-to-all-start.5) | async-done | bytes 786464 | tf_op jit(solution)/shard_map/cond/branch_1_fun/all_to_all | solution.py:188
  60.1 0.0 copy-start.3
  60.1 26.3 %all_to_all.39.rows_ref = bf16[64,48,128]{2,1,0:T(8,128)(2,1)} all-to-all(bf16[64,48,128]{2,1,0:T(8,128)(2,1)} %branch_1_fun.7), channel_id=1, replica_groups=mesh['section'=8,'dp'=64] {'dp'}, dimensions={0} | all-to-all | bytes 1572864 | tf_op jit(solution)/shard_map/cond/branch_1_fun/all_to_all | solution.py:198
  86.4 0.0 copy-done.3
  86.4 0.0 copy-done.6
  86.4 0.0 copy-start.8
  86.4 3.4 %branch_1_fun.9 = (bf16[64,48,128]{2,1,0:T(8,128)(2,1)}, bf16[8,48,1024]{2,1,0:T(8,128)(2,1)}) custom-call(bf16[64,48,128]{2,1,0:T(8,128)(2,1)} %all_to_all.39.rows_ref, bf16[8,48,1024]{2,1,0:T(8,128)(2,1)} %copy-done.3, f32[64,128]{1,0:T(8,128)S(1)} %bitcast.11), custom_call_target="tpu_custom_call" | custom-call | tf_op jit(solution)/shard_map/cond/branch_1_fun/pallas_call | solution.py:167
  89.8 23.5 %all_to_all.40.dealt_ref = bf16[8,48,1024]{2,1,0:T(8,128)(2,1)} all-to-all(bf16[8,48,1024]{2,1,0:T(8,128)(2,1)} %get-tuple-element.43), channel_id=1, replica_groups=mesh['section'=8,'dp'=64] {'section'}, dimensions={0} | all-to-all | bytes 1572864 | tf_op jit(solution)/shard_map/cond/branch_1_fun/all_to_all | solution.py:205
  113.4 11.8 %all-to-all-start.6 = ((bf16[64,48,128]{2,1,0:T(8,128)(2,1)}), bf16[64,48,128]{2,1,0:T(8,128)(2,1)S(1)}, u32[]{:S(2)}, u32[]{:S(2)}) async-start(bf16[64,48,128]{2,1,0:T(8,128)(2,1)} %get-tuple-element.42), calls=%async_computation.6 | async-start | bytes 1572864 | tf_op jit(solution)/shard_map/cond/branch_1_fun/all_to_all | solution.py:204
  125.1 0.0 copy-done.8
  125.1 2.7 %branch_1_fun.11 = bf16[128,1024]{1,0:T(8,128)(2,1)} custom-call(s32[1,128]{1,0:T(1,128)S(1)} %bitcast.15, bf16[8,48,1024]{2,1,0:T(8,128)(2,1)} %all_to_all.40.dealt_ref), custom_call_target="tpu_custom_call" | custom-call | tf_op jit(solution)/shard_map/cond/branch_1_fun/pallas_call | solution.py:167
  127.9 18.4 %all-to-all-done.6.grads_ref = bf16[64,48,128]{2,1,0:T(8,128)(2,1)S(1)} async-done(((bf16[64,48,128]{2,1,0:T(8,128)(2,1)}), bf16[64,48,128]{2,1,0:T(8,128)(2,1)S(1)}, u32[]{:S(2)}, u32[]{:S(2)}) %all-to-all-start.6) | async-done | bytes 786464 | tf_op jit(solution)/shard_map/cond/branch_1_fun/all_to_all | solution.py:204
  146.3 0.0 copy-start.4
  146.3 0.9 copy-done.4
  147.2 11.0 %branch_1_fun.10 = bf16[8192,128]{1,0:T(8,128)(2,1)} custom-call(s32[48,128]{1,0:T(8,128)} %get-tuple-element.36.index_ref, s32[8,128]{1,0:T(8,128)} %get-tuple-element.37.count_ref, bf16[64,48,128]{2,1,0:T(8,128)(2,1)} %copy-done.4), custom_call_target="tpu_custom_call" | custom-call | tf_op jit(solution)/shard_map/cond/branch_1_fun/pallas_call | solution.py:167
  (1 shorter events, 0.0 us)
Async XLA Ops:
  1.9 23.8 %all-to-all-start.8 = ((s32[64,1,128]{2,1,0:T(1,128)}), s32[64,1,128]{2,1,0:T(1,128)S(1)}, u32[]{:S(2)}, u32[]{:S(2)}) async-start(s32[64,1,128]{2,1,0:T(1,128)} %broadcast_in_dim.2), calls=%async_computation.8 | async-start | bytes 65536 | tf_op jit(solution)/shard_map/all_to_all | solution.py:224
  28.2 9.9 %copy-start.2 = (bf16[8192,128]{1,0:T(8,128)(2,1)S(1)}, bf16[8192,128]{1,0:T(8,128)(2,1)}, u32[]{:S(2)}) copy-start(bf16[8192,128]{1,0:T(8,128)(2,1)} %get-tuple-element.59.table_ref) | copy-start | bytes 6291460 | tf_op jit(solution)/shard_map/cond
  30.8 29.3 %all-to-all-start.5 = ((bf16[8,48,1024]{2,1,0:T(8,128)(2,1)}), bf16[8,48,1024]{2,1,0:T(8,128)(2,1)S(1)}, u32[]{:S(2)}, u32[]{:S(2)}) async-start(bf16[8,48,1024]{2,1,0:T(8,128)(2,1)} %branch_1_fun.8), calls=%async_computation.5 | async-start | bytes 1572864 | tf_op jit(solution)/shard_map/cond/branch_1_fun/all_to_all | solution.py:188
  38.1 48.3 %copy-start.6 = (f32[8192]{0:T(1024)S(1)}, f32[8192]{0:T(1024)}, u32[]{:S(2)}) copy-start(f32[8192]{0:T(1024)} %get-tuple-element.63) | copy-start | bytes 98308 | tf_op jit(solution)/shard_map/cond
  60.1 26.3 %copy-start.3 = (bf16[8,48,1024]{2,1,0:T(8,128)(2,1)}, bf16[8,48,1024]{2,1,0:T(8,128)(2,1)S(1)}, u32[]{:S(2)}) copy-start(bf16[8,48,1024]{2,1,0:T(8,128)(2,1)S(1)} %all-to-all-done.5.cotangent_ref) | copy-start | bytes 2359300 | tf_op jit(solution)/shard_map/cond
  86.4 38.7 %copy-start.8 = (s32[128]{0:T(128)S(1)}, s32[128]{0:T(128)}, u32[]{:S(2)}) copy-start(s32[128]{0:T(128)} %get-tuple-element.53) | copy-start | bytes 1540 | tf_op jit(solution)/shard_map/cond
  113.4 32.9 %all-to-all-start.6 = ((bf16[64,48,128]{2,1,0:T(8,128)(2,1)}), bf16[64,48,128]{2,1,0:T(8,128)(2,1)S(1)}, u32[]{:S(2)}, u32[]{:S(2)}) async-start(bf16[64,48,128]{2,1,0:T(8,128)(2,1)} %get-tuple-element.42), calls=%async_computation.6 | async-start | bytes 1572864 | tf_op jit(solution)/shard_map/cond/branch_1_fun/all_to_all | solution.py:204
  146.3 0.9 copy-start.4

commit v2 on v1

--- a/solution.py
+++ b/solution.py
@@ -97,10 +97,39 @@
     own_ref[...] = total.astype(jnp.bfloat16)
 
 
-def norm_kernel(rows_ref, cotangent_ref, gain_ref, by_column_ref, by_feature_ref):
+def own_slots(ids_row, section, slots, vocab_section):
+    wide = jnp.broadcast_to(ids_row // vocab_section, (LANES, LANES))
+    tall = wide.astype(jnp.float32).T.astype(jnp.int32)
+    first = lax.broadcasted_iota(jnp.int32, (LANES, LANES), 0)
+    second = lax.broadcasted_iota(jnp.int32, (LANES, LANES), 1)
+    as_row = jnp.sum(jnp.where((tall == section) & (first < second), 1, 0), axis=0, keepdims=True)
+    as_column = jnp.sum(jnp.where((wide == section) & (second < first), 1.0, 0.0), axis=1, keepdims=True)
+    row_slot = jnp.where(wide[:1] == section, as_row, -1)
+    column_slot = jnp.where(tall[:, :1] == section, as_column.astype(jnp.int32), -1)
+    return row_slot, column_slot
+
+
+def select_kernel(section_ref, ids_ref, cotangent_ref, own_ref, *, slots, vocab_section):
+    row_slot, _ = own_slots(ids_ref[...], section_ref[0], slots, vocab_section)
+    wanted = lax.broadcasted_iota(jnp.int32, (slots, LANES), 0) == row_slot
+    wanted = jnp.where(wanted, 1.0, 0.0).astype(jnp.bfloat16)
+    for s in range(cotangent_ref.shape[0]):
+        own_ref[s] = jnp.dot(
+            wanted, cotangent_ref[s], preferred_element_type=jnp.float32
+        ).astype(jnp.bfloat16)
+
+
+def norm_kernel(*refs, spread, vocab_section):
+    if spread:
+        section_ref, ids_ref, *refs = refs
+    rows_ref, cotangent_ref, gain_ref, by_column_ref, by_feature_ref, *scratch = refs
     pieces, slots, columns = rows_ref.shape
     per = cotangent_ref.shape[2] // columns
     width = pieces * columns
+    if spread:
+        _, column_slot = own_slots(ids_ref[...], section_ref[0], slots, vocab_section)
+        wanted = lax.broadcasted_iota(jnp.int32, (LANES, slots), 1) == column_slot
+        wanted = jnp.where(wanted, 1.0, 0.0).astype(jnp.bfloat16)
 
     def parts(k, j):
         embedded = rows_ref[k * per + j].astype(jnp.float32)
@@ -127,7 +156,14 @@
             embedded, scaled = parts(k, j)
             grad = (inverse * scaled - embedded * pull).astype(jnp.bfloat16)
             by_column_ref[k * per + j] = grad
-            by_feature_ref[k, :, j * columns : (j + 1) * columns] = grad
+            if spread:
+                scratch[0][:, j * columns : (j + 1) * columns] = grad
+            else:
+                by_feature_ref[k, :, j * columns : (j + 1) * columns] = grad
+        if spread:
+            by_feature_ref[k] = jnp.dot(
+                wanted, scratch[0][...], preferred_element_type=jnp.float32
+            ).astype(jnp.bfloat16)
         return carry
 
     lax.fori_loop(0, pieces // per, grads, 0)
@@ -198,7 +234,8 @@
     full_rows = lax.all_to_all(rows, "dp", 0, 0, tiled=True)
     gain = norm_gain.reshape(groups, columns)
     by_column, by_feature = call(
-        norm_kernel, (full_rows, their_cotangent, gain), (V, V, V),
+        functools.partial(norm_kernel, spread=False, vocab_section=vocab_section),
+        (full_rows, their_cotangent, gain), (V, V, V),
         [bf16(full_rows.shape), bf16(their_cotangent.shape)],
     )
     back = lax.all_to_all(by_column, "dp", 0, 0, tiled=True)
@@ -216,23 +253,62 @@
 
 
 def on_device(token_ids, embed_table, norm_gain, cotangent):
-    vocab_section = embed_table.shape[0]
+    vocab_section, columns = embed_table.shape
     groups = lax.axis_size("dp")
-    tokens = token_ids.shape[0]
+    sections = lax.axis_size("section")
+    tokens, features = cotangent.shape
+    V, S = pltpu.VMEM, pltpu.SMEM
+    bf16 = functools.partial(jax.ShapeDtypeStruct, dtype=jnp.bfloat16)
+    i32 = functools.partial(jax.ShapeDtypeStruct, dtype=jnp.int32)
     section = lax.axis_index("section").reshape(1)
     own_ids = token_ids.reshape(1, tokens)
+    all_cotangent = lax.all_gather(cotangent, "section", axis=0)
     all_ids = lax.all_to_all(
         jnp.broadcast_to(own_ids[None], (groups, 1, tokens)), "dp", 0, 0, tiled=True
     ).reshape(groups, tokens)
-    sections = jnp.arange(lax.axis_size("section"))
-    counts = jnp.sum(all_ids[:, :, None] // vocab_section == sections, axis=1)
+    counts = jnp.sum(all_ids[:, :, None] // vocab_section == jnp.arange(sections), axis=1)
     fits = jnp.max(counts) <= SLOTS
-    return lax.cond(
-        fits,
-        functools.partial(passage, SLOTS),
-        functools.partial(passage, tokens),
+
+    index, count = call(
+        functools.partial(plan_kernel, slots=SLOTS, vocab_section=vocab_section),
+        (section, all_ids), (S, V), [i32((SLOTS, LANES)), i32((8, LANES))],
+    )
+    (rows,) = call(
+        functools.partial(pick_kernel, slots=SLOTS, groups=groups),
+        (index, embed_table), (S, V), [bf16((groups, SLOTS, columns))],
+        [pltpu.VMEM((vocab_section, columns), jnp.float32), pltpu.VMEM((SLOTS, columns), jnp.float32)],
+    )
+    full_rows = lax.all_to_all(rows, "dp", 0, 0, tiled=True)
+    (slot_cotangent,) = call(
+        functools.partial(select_kernel, slots=SLOTS, vocab_section=vocab_section),
+        (section, own_ids, all_cotangent), (S, V, V), [bf16((sections, SLOTS, features))],
+    )
+    by_column, spread = call(
+        functools.partial(norm_kernel, spread=True, vocab_section=vocab_section),
+        (section, own_ids, full_rows, slot_cotangent, norm_gain.reshape(groups, columns)),
+        (S, V, V, V, V),
+        [bf16(full_rows.shape), bf16((sections, tokens, features))],
+        [pltpu.VMEM((SLOTS, features), jnp.bfloat16)],
+    )
+    fast_grad = lax.psum_scatter(spread, "section", scatter_dimension=0, tiled=True)[0]
+    back = lax.all_to_all(by_column, "dp", 0, 0, tiled=True)
+
+    def fast(index, count, back, *_):
+        (grad_table,) = call(
+            functools.partial(add_kernel, groups=groups),
+            (index, count, back), (S, S, V), [bf16((vocab_section, columns))],
+            [pltpu.VMEM((vocab_section, columns), jnp.float32), pltpu.VMEM((SLOTS, columns), jnp.float32)],
+        )
+        return grad_table, jnp.zeros((tokens, features), jnp.bfloat16)
+
+    def slow(index, count, back, *operands):
+        return passage(tokens, *operands)
+
+    grad_table, slow_grad = lax.cond(
+        fits, fast, slow, index, count, back,
         section, all_ids, own_ids, embed_table, norm_gain, cotangent,
     )
+    return grad_table, jnp.where(fits, fast_grad, slow_grad)
 
 
 def solution(mesh):

time: 160 us -> 128 us (0.80)
  blocking collectives: 49.8 us -> 0 us
  between operations: 1.3 us -> 14.8 us
  waiting for transfers between devices: 43 us -> 49.1 us
  starting transfers between devices: 32.8 us -> 29.7 us
  other arithmetic: 1.82 us -> 3.5 us
    all_to_all x2 -> x0, blocking collectives: 49.8 us -> none  [the longest x1 26.3 us: passage(): full_rows = lax.all_to_all(rows, 'dp', 0, 0, tiled=True)]
    all_gather x0 -> x1, waiting for transfers between devices: none -> 8.25 us  [on_device(): all_cotangent = lax.all_gather(cotangent, 'section', axis=0)]
    all_to_all x2, waiting for transfers between devices: 34 us -> 26.2 us  [the longest x1 17.3 us: on_device(): back = lax.all_to_all(by_column, 'dp', 0, 0, tiled=True)]
    reduce_scatter x0 -> x1, waiting for transfers between devices: none -> 4.98 us  [on_device(): lax.psum_scatter(spread, 'section', scatter_dimension=0, tiled=True)[0]]
    all_to_all x2, starting transfers between devices: 18 us -> 14.8 us  [the longest x1 8.69 us: on_device(): back = lax.all_to_all(by_column, 'dp', 0, 0, tiled=True)]
    select_n x1 -> x2, other arithmetic: 0.02 us -> 1.7 us  [the longest x1 1.68 us: on_device(): return (grad_table, jnp.where(fits, fast_grad, slow_grad))]
    pallas_call x6 -> x5, Pallas kernels: 27.1 us -> 26.5 us  [call(): pl.pallas_call(kernel, in_specs=[whole(o.shape, s) for o, s in zip(operan...]
  transfers between devices with their start and end apart: 3 -> 5, of which waited for: 3 -> 5; matrix products, arithmetic and copies ran while one was open for 0% -> 2% of each run, Pallas kernels for 6% -> 17%
where the time goes in v2:
time: 128 us; the launch traced here: 126 us
  waiting for transfers between devices  49.1 us (38%)
  starting transfers between devices  29.7 us (23%)
  Pallas kernels  26.5 us (21%)
  between operations  14.8 us (12%)
  other arithmetic  3.5 us (3%)
  local copies, waits for them, and re-layouts  2.21 us (2%)
    pallas_call x5, Pallas kernels, call(): pl.pallas_call(kernel, in_specs=[whole(o.shape, s) for o, s in zip(operan...  26.5 us
    all_to_all x1, waiting for transfers between devices, on_device(): back = lax.all_to_all(by_column, 'dp', 0, 0, tiled=True)  17.3 us
    all_to_all x1, starting transfers between devices, on_device(): lax.all_to_all(jnp.broadcast_to(own_ids[None], (groups, 1, tokens)), 'dp'...  14.8 us
    all_to_all x1, waiting for transfers between devices, on_device(): lax.all_to_all(jnp.broadcast_to(own_ids[None], (groups, 1, tokens)), 'dp'...  8.96 us
    all_to_all x1, waiting for transfers between devices, on_device(): full_rows = lax.all_to_all(rows, 'dp', 0, 0, tiled=True)  8.9 us
    all_to_all x1, starting transfers between devices, on_device(): back = lax.all_to_all(by_column, 'dp', 0, 0, tiled=True)  8.69 us
    all_gather x1, waiting for transfers between devices, on_device(): all_cotangent = lax.all_gather(cotangent, 'section', axis=0)  8.25 us
    all_to_all x1, starting transfers between devices, on_device(): full_rows = lax.all_to_all(rows, 'dp', 0, 0, tiled=True)  6.14 us
  transfers between devices with their start and end apart: 5, of which 5 were waited for; matrix products, arithmetic and copies ran while one was open for 2% of the time, Pallas kernels for 17%

profile of v2, /device:TPU:6, one launch (start us, length us, event | category | flops | bytes accessed | tf_op | source)
XLA Modules:
  0.0 125.7 jit_solution(9339500607533936516)
XLA Ops:
  7.2 0.0 all-gather.3.cloned.1.call-start
  7.2 0.7 all-gather.3.cloned.1.call-update
  7.9 1.3 %broadcast_in_dim.2 = s32[64,1,128]{2,1,0:T(1,128)} broadcast(s32[128]{0:T(128)} %param.6), dimensions={2} | broadcast | bytes 33280 | tf_op jit(solution)/shard_map/broadcast_in_dim | solution.py:267
  9.2 14.8 %all-to-all-start.4 = ((s32[64,1,128]{2,1,0:T(1,128)}), s32[64,1,128]{2,1,0:T(1,128)S(1)}, u32[]{:S(2)}, u32[]{:S(2)}) async-start(s32[64,1,128]{2,1,0:T(1,128)} %broadcast_in_dim.2), calls=%async_computation.4 | async-start | bytes 65536 | tf_op jit(solution)/shard_map/all_to_all | solution.py:266
  24.0 9.0 %all-to-all-done.4 = s32[64,1,128]{2,1,0:T(1,128)S(1)} async-done(((s32[64,1,128]{2,1,0:T(1,128)}), s32[64,1,128]{2,1,0:T(1,128)S(1)}, u32[]{:S(2)}, u32[]{:S(2)}) %all-to-all-start.4) | async-done | bytes 32800 | tf_op jit(solution)/shard_map/all_to_all | solution.py:266
  33.0 0.6 shard_map.59
  33.6 0.0 copy-start.5
  33.6 6.7 %shard_map.60 = bf16[64,48,128]{2,1,0:T(8,128)(2,1)} custom-call(s32[48,128]{1,0:T(8,128)S(1)} %get-tuple-element.39.index_ref, bf16[8192,128]{1,0:T(8,128)(2,1)} %table_ref.1), custom_call_target="tpu_custom_call" | custom-call | tf_op jit(solution)/shard_map/pallas_call | solution.py:203
  40.3 0.0 copy-start.4
  40.3 6.1 %all-to-all-start.5 = ((bf16[64,48,128]{2,1,0:T(8,128)(2,1)}), bf16[64,48,128]{2,1,0:T(8,128)(2,1)S(1)}, u32[]{:S(2)}, u32[]{:S(2)}) async-start(bf16[64,48,128]{2,1,0:T(8,128)(2,1)} %shard_map.60), calls=%async_computation.5 | async-start | bytes 1572864 | tf_op jit(solution)/shard_map/all_to_all | solution.py:281
  46.4 0.0 reduce-scatter.2.cloned.1.call-start
  46.5 8.2 %all-gather.3.cloned.1.call-done = bf16[1024,1024]{1,0:T(8,128)(2,1)} async-done(((bf16[128,1024]{1,0:T(8,128)(2,1)}), bf16[1024,1024]{1,0:T(8,128)(2,1)}) %all-gather.3.cloned.1.call-update) | async-done | bytes 2097168 | tf_op jit(solution)/shard_map/all_gather | solution.py:265
  54.7 0.0 copy-done.5
  54.7 3.0 %shard_map.61.refs_3_ = bf16[8,48,1024]{2,1,0:T(8,128)(2,1)} custom-call(s32[1]{0:T(128)} %bitcast.2.section_ref.refs_0_, s32[1,128]{1,0:T(1,128)S(1)} %bitcast.14, bf16[8,128,1024]{2,1,0:T(8,128)(2,1)} %bitcast.8), custom_call_target="tpu_custom_call" | custom-call | tf_op jit(solution)/shard_map/pallas_call | solution.py:203
  57.7 8.9 %all-to-all-done.5.refs_2_ = bf16[64,48,128]{2,1,0:T(8,128)(2,1)S(1)} async-done(((bf16[64,48,128]{2,1,0:T(8,128)(2,1)}), bf16[64,48,128]{2,1,0:T(8,128)(2,1)S(1)}, u32[]{:S(2)}, u32[]{:S(2)}) %all-to-all-start.5) | async-done | bytes 786464 | tf_op jit(solution)/shard_map/all_to_all | solution.py:281
  66.6 0.0 copy-start.2
  66.6 0.9 copy-done.2
  67.5 0.0 copy-done.4
  67.5 5.4 %shard_map.62 = (bf16[64,48,128]{2,1,0:T(8,128)(2,1)}, bf16[8,128,1024]{2,1,0:T(8,128)(2,1)}) custom-call(s32[1]{0:T(128)} %bitcast.2.section_ref.refs_0_, s32[1,128]{1,0:T(1,128)S(1)} %bitcast.15, bf16[64,48,128]{2,1,0:T(8,128)(2,1)} %copy-done.2, bf16[8,48,1024]{2,1,0:T(8,128)(2,1)} %shard_map.61.refs_3_, f32[64,128]{1,0:T(8,128)S(1)} %bitcast.12), custom_call_target="tpu_custom_call" | custom-call | tf_op jit(solution)/shard_map/pallas_call | solution.py:203
  72.9 0.0 copy-start.1
  72.9 0.0 copy-start.3
  72.9 0.0 reduce-scatter.2.cloned.1.call-update
  72.9 8.7 %all-to-all-start.6 = ((bf16[64,48,128]{2,1,0:T(8,128)(2,1)}), bf16[64,48,128]{2,1,0:T(8,128)(2,1)S(1)}, u32[]{:S(2)}, u32[]{:S(2)}) async-start(bf16[64,48,128]{2,1,0:T(8,128)(2,1)} %get-tuple-element.41), calls=%async_computation.6 | async-start | bytes 1572864 | tf_op jit(solution)/shard_map/all_to_all | solution.py:294
  81.7 1.2 convert_reduce_fusion
  82.8 0.6 reduce_max.9
  84.1 17.3 %all-to-all-done.6 = bf16[64,48,128]{2,1,0:T(8,128)(2,1)S(1)} async-done(((bf16[64,48,128]{2,1,0:T(8,128)(2,1)}), bf16[64,48,128]{2,1,0:T(8,128)(2,1)S(1)}, u32[]{:S(2)}, u32[]{:S(2)}) %all-to-all-start.6) | async-done | bytes 786464 | tf_op jit(solution)/shard_map/all_to_all | solution.py:294
  101.4 0.0 copy-done.1
  101.4 0.0 copy-done.3
  101.4 10.8 %conditional.1 = (bf16[8192,128]{1,0:T(8,128)(2,1)}, bf16[128,1024]{1,0:T(8,128)(2,1)S(1)}) conditional(s32[]{:T(128)} %convert_element_type.7, (s32[1]{0:T(128)}, s32[64,128]{1,0:T(8,128)S(1)}, bf16[8192,128]{1,0:T(8,128)(2,1)S(1)}, s32[1,128]{1,0:T(1,128)S(1)}, bf16[128,1024]{1,0:T(8,128)(2,1)S(1)}, /*index=5*/f32[8192]{0:T(1024)S(1)}) %tuple.29, ...), branch_computations={%region_2.3_spmd, %region_3.4_spmd} | conditional | bytes 29360236 | solution.py:307
  101.4 10.8 %branch_1_fun.1 = bf16[8192,128]{1,0:T(8,128)(2,1)} custom-call(s32[48,128]{1,0:T(8,128)S(1)} %get-tuple-element.28.index_ref, s32[8,128]{1,0:T(8,128)S(1)} %get-tuple-element.29.count_ref, bf16[64,48,128]{2,1,0:T(8,128)(2,1)S(1)} %get-tuple-element.30.grads_ref), custom_call_target="tpu_custom_call" | custom-call | tf_op jit(solution)/shard_map/cond/branch_1_fun/pallas_call | solution.py:203
  112.2 5.0 %reduce-scatter.2.cloned.1.call-done = bf16[1,128,1024]{2,1,0:T(8,128)(2,1)} async-done(((bf16[8,128,1024]{2,1,0:T(8,128)(2,1)}), bf16[1,128,1024]{2,1,0:T(8,128)(2,1)}) %reduce-scatter.2.cloned.1.call-update) | async-done | bytes 262160 | tf_op jit(solution)/shard_map/reduce_scatter | solution.py:293
  117.2 1.7 %bitcast_select_fusion = bf16[128,1024]{1,0:T(8,128)(2,1)} fusion(bf16[128,1024]{1,0:T(8,128)(2,1)S(1)} %get-tuple-element.44, bf16[1,128,1024]{2,1,0:T(8,128)(2,1)} %reduce-scatter.2.cloned.1.call-done, pred[]{:T(512)S(6)} %le.3), kind=kLoop, calls=%fused_computation | loop fusion | flops 131072 | bytes 786433 | tf_op jit(solution)/shard_map/jit(_where)/select_n | solution.py:311
  (2 shorter events, 0.0 us)
Async XLA Ops:
  7.2 47.6 %all-gather.3.cloned.1.call-start = ((), (), s32[]{:S(2)}) async-start(), calls=%async_computation.9 | async-start | bytes 2359296 | tf_op jit(solution)/shard_map/all_gather | solution.py:265
  9.2 23.8 %all-to-all-start.4 = ((s32[64,1,128]{2,1,0:T(1,128)}), s32[64,1,128]{2,1,0:T(1,128)S(1)}, u32[]{:S(2)}, u32[]{:S(2)}) async-start(s32[64,1,128]{2,1,0:T(1,128)} %broadcast_in_dim.2), calls=%async_computation.4 | async-start | bytes 65536 | tf_op jit(solution)/shard_map/all_to_all | solution.py:266
  33.6 21.2 %copy-start.5 = (s32[128]{0:T(128)S(1)}, s32[128]{0:T(128)}, u32[]{:S(2)}) copy-start(s32[128]{0:T(128)} %param.6) | copy-start | bytes 1540
  40.3 27.2 %copy-start.4 = (f32[8192]{0:T(1024)S(1)}, f32[8192]{0:T(1024)}, u32[]{:S(2)}) copy-start(f32[8192]{0:T(1024)} %param.8) | copy-start | bytes 98308
  40.3 26.3 %all-to-all-start.5 = ((bf16[64,48,128]{2,1,0:T(8,128)(2,1)}), bf16[64,48,128]{2,1,0:T(8,128)(2,1)S(1)}, u32[]{:S(2)}, u32[]{:S(2)}) async-start(bf16[64,48,128]{2,1,0:T(8,128)(2,1)} %shard_map.60), calls=%async_computation.5 | async-start | bytes 1572864 | tf_op jit(solution)/shard_map/all_to_all | solution.py:281
  46.4 70.8 %reduce-scatter.2.cloned.1.call-start = ((), (), s32[]{:S(2)}) async-start(), calls=%async_computation.8 | async-start | bytes 2359296 | tf_op jit(solution)/shard_map/reduce_scatter | solution.py:293
  66.6 0.9 copy-start.2
  72.9 28.5 %copy-start.1 = (bf16[8192,128]{1,0:T(8,128)(2,1)S(1)}, bf16[8192,128]{1,0:T(8,128)(2,1)}, u32[]{:S(2)}) copy-start(bf16[8192,128]{1,0:T(8,128)(2,1)} %table_ref.1) | copy-start | bytes 6291460
  72.9 28.5 %copy-start.3 = (bf16[128,1024]{1,0:T(8,128)(2,1)S(1)}, bf16[128,1024]{1,0:T(8,128)(2,1)}, u32[]{:S(2)}) copy-start(bf16[128,1024]{1,0:T(8,128)(2,1)} %param.9) | copy-start | bytes 786436
  72.9 28.5 %all-to-all-start.6 = ((bf16[64,48,128]{2,1,0:T(8,128)(2,1)}), bf16[64,48,128]{2,1,0:T(8,128)(2,1)S(1)}, u32[]{:S(2)}, u32[]{:S(2)}) async-start(bf16[64,48,128]{2,1,0:T(8,128)(2,1)} %get-tuple-element.41), calls=%async_computation.6 | async-start | bytes 1572864 | tf_op jit(solution)/shard_map/all_to_all | solution.py:294
Sparse Core Ops, SparseCore 0:
  10.1 44.5 all-gather.2
  73.1 44.0 reduce-scatter.1

commit v3 on v1

--- a/solution.py
+++ b/solution.py
@@ -1,14 +1,22 @@
 import functools
+import math
 
 import jax
 import jax.numpy as jnp
 from jax import lax
 from jax.experimental import pallas as pl
 from jax.experimental.pallas import tpu as pltpu
+from jax.sharding import Mesh
 from jax.sharding import PartitionSpec as P
 
 epsilon = 1e-05
-SLOTS = 48
+TOKEN_SLOTS = 48
+ROW_SLOTS = 32
+CHUNK = 8
+REPEATED = 1 << 16
+CHIPS = "section_0"
+CORES = "section_1"
+SECTION = (CHIPS, CORES)
 LANES = 128
 
 
@@ -164,12 +172,14 @@
 
 
 def call(kernel, operands, spaces, outs, scratch=()):
+    held = sum(math.prod(a.shape) * a.dtype.itemsize for a in (*operands, *outs, *scratch))
     return pl.pallas_call(
         kernel,
         in_specs=[whole(o.shape, s) for o, s in zip(operands, spaces)],
         out_specs=[whole(o.shape) for o in outs],
         out_shape=outs,
         scratch_shapes=list(scratch),
+        compiler_params=pltpu.CompilerParams(vmem_limit_bytes=2 * held + (6 << 20)),
     )(*operands)
 
 
@@ -177,7 +187,7 @@
     vocab_section, columns = embed_table.shape
     groups = all_ids.shape[0]
     tokens, features = cotangent.shape
-    sections = lax.axis_size("section")
+    sections = lax.axis_size(SECTION)
     V, S = pltpu.VMEM, pltpu.SMEM
     bf16 = functools.partial(jax.ShapeDtypeStruct, dtype=jnp.bfloat16)
     i32 = functools.partial(jax.ShapeDtypeStruct, dtype=jnp.int32)
@@ -185,7 +195,7 @@
         functools.partial(deal_kernel, slots=slots, sections=sections, vocab_section=vocab_section),
         (own_ids, cotangent), (V, V), [bf16((sections, slots, features))],
     )
-    their_cotangent = lax.all_to_all(dealt, "section", 0, 0, tiled=True)
+    their_cotangent = lax.all_to_all(dealt, SECTION, 0, 0, tiled=True)
     index, count = call(
         functools.partial(plan_kernel, slots=slots, vocab_section=vocab_section),
         (section, all_ids), (S, V), [i32((slots, LANES)), i32((8, LANES))],
@@ -202,7 +212,7 @@
         [bf16(full_rows.shape), bf16(their_cotangent.shape)],
     )
     back = lax.all_to_all(by_column, "dp", 0, 0, tiled=True)
-    home = lax.all_to_all(by_feature, "section", 0, 0, tiled=True)
+    home = lax.all_to_all(by_feature, SECTION, 0, 0, tiled=True)
     (grad_table,) = call(
         functools.partial(add_kernel, groups=groups),
         (index, count, back), (S, S, V), [bf16((vocab_section, columns))],
@@ -215,31 +225,316 @@
     return grad_table, own_grad
 
 
+def row_plan_kernel(section_ref, ids_ref, index_ref, count_ref, *, vocab_section):
+    slots = index_ref.shape[0]
+    ids = ids_ref[...].astype(jnp.float32)
+    ids = jnp.concatenate([ids, ids], axis=0)
+    ids = ids.T.astype(jnp.int32)
+    local = ids - section_ref[0] * vocab_section
+    inside = (local >= 0) & (local < vocab_section) & (ids < REPEATED)
+    before = (
+        lax.broadcasted_iota(jnp.int32, (LANES, LANES), 1)
+        < lax.broadcasted_iota(jnp.int32, (LANES, LANES), 0)
+    )
+    ones = jnp.where(inside, 1.0, 0.0)
+    rank = jnp.dot(
+        jnp.where(before, 1.0, 0.0).astype(jnp.bfloat16),
+        ones.astype(jnp.bfloat16),
+        preferred_element_type=jnp.float32,
+    ).astype(jnp.int32)
+    rank = jnp.where(inside, rank, -1)
+    short = local - vocab_section
+    for c in range(slots):
+        index_ref[pl.ds(c, 1), :] = vocab_section + jnp.sum(
+            jnp.where(rank == c, short, 0), axis=0, keepdims=True
+        )
+    count = jnp.minimum(jnp.sum(ones, axis=0, keepdims=True).astype(jnp.int32), slots)
+    count_ref[...] = jnp.broadcast_to((count + (CHUNK - 1)) // CHUNK, count_ref.shape)
+
+
+def row_pick_kernel(index_ref, count_ref, table_ref, rows_ref, wide_ref, picked_ref):
+    groups, slots, columns = rows_ref.shape
+    entries = table_ref.shape[0]
+    step = 512
+    picked_ref[...] = jnp.zeros(picked_ref.shape, jnp.float32)
+    wide_ref[pl.ds(entries, CHUNK), :] = jnp.zeros((CHUNK, columns), jnp.float32)
+
+    def widen(i, carry):
+        wide_ref[pl.ds(i * step, step), :] = table_ref[pl.ds(i * step, step), :].astype(jnp.float32)
+        return carry
+
+    lax.fori_loop(0, entries // step, widen, 0)
+
+    def group(g, carry):
+        def chunk(i, carry):
+            for j in range(CHUNK):
+                c = i * CHUNK + j
+                picked_ref[pl.ds(c, 1), :] = wide_ref[pl.ds(index_ref[c, g], 1), :]
+            return carry
+
+        lax.fori_loop(0, count_ref[0, g], chunk, 0)
+        rows_ref[g] = picked_ref[...].astype(jnp.bfloat16)
+        return carry
+
+    lax.fori_loop(0, groups, group, 0)
+
+
+def row_add_kernel(index_ref, count_ref, grads_ref, table_ref, total_ref, wide_ref):
+    groups, slots, columns = grads_ref.shape
+    entries = table_ref.shape[0]
+    step = 512
+
+    def clear(i, carry):
+        total_ref[pl.ds(i * step, step), :] = jnp.zeros((step, columns), jnp.float32)
+        return carry
+
+    lax.fori_loop(0, entries // step, clear, 0)
+    total_ref[pl.ds(entries, CHUNK), :] = jnp.zeros((CHUNK, columns), jnp.float32)
+
+    def group(g, carry):
+        wide_ref[...] = grads_ref[g].astype(jnp.float32)
+
+        def chunk(i, carry):
+            rows = [pl.ds(index_ref[i * CHUNK + j, g], 1) for j in range(CHUNK)]
+            sums = [
+                total_ref[row, :] + wide_ref[pl.ds(i * CHUNK + j, 1), :]
+                for j, row in enumerate(rows)
+            ]
+            for row, value in zip(rows, sums):
+                total_ref[row, :] = value
+            return carry
+
+        lax.fori_loop(0, count_ref[0, g], chunk, 0)
+        return carry
+
+    lax.fori_loop(0, groups, group, 0)
+
+    def narrow(i, carry):
+        table_ref[pl.ds(i * step, step), :] = total_ref[pl.ds(i * step, step), :].astype(jnp.bfloat16)
+        return carry
+
+    lax.fori_loop(0, entries // step, narrow, 0)
+
+
+def both_ways(ids_row):
+    wide = jnp.broadcast_to(ids_row, (LANES, LANES))
+    tall = wide.astype(jnp.float32).T.astype(jnp.int32)
+    down = lax.broadcasted_iota(jnp.int32, (LANES, LANES), 0)
+    along = lax.broadcasted_iota(jnp.int32, (LANES, LANES), 1)
+    return wide, tall, down < along, along < down
+
+
+def mark_kernel(ids_ref, marked_ref):
+    wide, tall, row_first, _ = both_ways(ids_ref[...])
+    repeated = jnp.max(jnp.where((wide == tall) & row_first, REPEATED, 0), axis=0, keepdims=True)
+    marked_ref[...] = jnp.broadcast_to((wide[:1] + repeated)[None], marked_ref.shape)
+
+
+def one_hot(condition):
+    return jnp.where(condition, 1.0, 0.0).astype(jnp.bfloat16)
+
+
+def select_kernel(section_ref, ids_ref, cotangent_ref, own_ref, expand_ref, combine_ref, *, vocab_section):
+    token_slots, row_slots = expand_ref.shape
+    wide, tall, row_first, column_first = both_ways(ids_ref[...])
+    section = section_ref[0]
+    wide_in = wide // vocab_section == section
+    tall_in = tall // vocab_section == section
+    same = wide == tall
+    wide_repeat = jnp.max(jnp.where(same & row_first, 1, 0), axis=0, keepdims=True)
+    tall_repeat = jnp.max(jnp.where(same & column_first, 1.0, 0.0), axis=1, keepdims=True)
+    wide_new = wide_in & (jnp.broadcast_to(wide_repeat, (LANES, LANES)) == 0)
+    tall_new = tall_in & (jnp.broadcast_to(tall_repeat, (LANES, LANES)) == 0.0)
+    rank = jnp.sum(jnp.where(tall_in & row_first, 1, 0), axis=0, keepdims=True)
+    rank = jnp.where(wide_in[:1], rank, -1)
+    own = one_hot(lax.broadcasted_iota(jnp.int32, (token_slots, LANES), 0) == rank)
+    tall_place = jnp.sum(jnp.where(wide_new & column_first, 1.0, 0.0), axis=1, keepdims=True)
+    place = jnp.sum(
+        jnp.where(same & tall_new, jnp.broadcast_to(tall_place, (LANES, LANES)), 0.0), axis=0, keepdims=True
+    ).astype(jnp.int32)
+    place = jnp.where(wide_in[:1], place, -1)
+    rows = one_hot(lax.broadcasted_iota(jnp.int32, (row_slots, LANES), 0) == place)
+    over_tokens = (((1,), (1,)), ((), ()))
+    expand_ref[...] = lax.dot_general(
+        own, rows, over_tokens, preferred_element_type=jnp.float32
+    ).astype(jnp.bfloat16)
+    combine_ref[...] = lax.dot_general(
+        rows, own, over_tokens, preferred_element_type=jnp.float32
+    ).astype(jnp.bfloat16)
+    for s in range(cotangent_ref.shape[0]):
+        own_ref[s] = jnp.dot(
+            own, cotangent_ref[s], preferred_element_type=jnp.float32
+        ).astype(jnp.bfloat16)
+
+
+def grad_kernel(
+    section_ref, rows_ref, cotangent_ref, gain_ref, expand_ref, combine_ref,
+    by_column_ref, keep_ref, give_ref, embedded_ref,
+):
+    pieces, _, columns = rows_ref.shape
+    sections, slots, features = cotangent_ref.shape
+    per = features // columns
+    width = pieces * columns
+    expand = expand_ref[...]
+    combine = combine_ref[...]
+
+    def sums(k, carry):
+        squares, inners = carry
+        rows = jnp.concatenate([rows_ref[k * per + j] for j in range(per)], axis=1)
+        embedded = jnp.dot(expand, rows, preferred_element_type=jnp.float32)
+        embedded_ref[k] = embedded
+        scaled = cotangent_ref[k].astype(jnp.float32) * gain_ref[pl.ds(k, 1), :]
+        square = embedded * embedded
+        inner = scaled * embedded
+        for j in range(per):
+            squares = squares + square[:, j * columns : (j + 1) * columns]
+            inners = inners + inner[:, j * columns : (j + 1) * columns]
+        return squares, inners
+
+    zeros = jnp.zeros((slots, columns), jnp.float32)
+    squares, inners = lax.fori_loop(0, sections, sums, (zeros, zeros))
+    square_mean = jnp.sum(squares, axis=1, keepdims=True) * (1.0 / width)
+    inner = jnp.sum(inners, axis=1, keepdims=True) * (1.0 / width)
+    inverse = lax.rsqrt(square_mean + epsilon)
+    pull = inverse * inverse * inverse * inner
+    core = section_ref[0] % 2
+
+    def grads(k, out_ref, place):
+        scaled = cotangent_ref[k].astype(jnp.float32) * gain_ref[pl.ds(k, 1), :]
+        grad = (inverse * scaled - embedded_ref[k] * pull).astype(jnp.bfloat16)
+        out_ref[place] = grad
+        added = jnp.dot(combine, grad, preferred_element_type=jnp.float32).astype(jnp.bfloat16)
+        for j in range(per):
+            by_column_ref[k * per + j] = added[:, j * columns : (j + 1) * columns]
+
+    def chip(h, carry):
+        grads(2 * h + core, keep_ref, h)
+        grads(2 * h + 1 - core, give_ref, h)
+        return carry
+
+    lax.fori_loop(0, sections // 2, chip, 0)
+
+
+def spread_kernel(section_ref, ids_ref, kept_ref, given_ref, spread_ref, *, vocab_section):
+    slots = kept_ref.shape[1]
+    wide, tall, _, column_first = both_ways(ids_ref[...])
+    wide = wide // vocab_section
+    tall = tall // vocab_section
+    along = lax.broadcasted_iota(jnp.int32, (LANES, slots), 1)
+
+    def of(section):
+        rank = jnp.sum(jnp.where((wide == section) & column_first, 1.0, 0.0), axis=1, keepdims=True)
+        rank = jnp.where(tall[:, :1] == section, rank.astype(jnp.int32), -1)
+        return one_hot(along == rank)
+
+    section = section_ref[0]
+    mine = of(section)
+    theirs = of(section + 1 - 2 * (section % 2))
+    for h in range(kept_ref.shape[0]):
+        spread_ref[h] = (
+            jnp.dot(mine, kept_ref[h], preferred_element_type=jnp.float32)
+            + jnp.dot(theirs, given_ref[h], preferred_element_type=jnp.float32)
+        ).astype(jnp.bfloat16)
+
+
+def settle_kernel(fits_ref, fast_ref, slow_ref, out_ref, semaphore):
+    @pl.when(fits_ref[0] == 0)
+    def _():
+        copy = pltpu.make_async_copy(slow_ref, out_ref, semaphore)
+        copy.start()
+        copy.wait()
+
+
 def on_device(token_ids, embed_table, norm_gain, cotangent):
-    vocab_section = embed_table.shape[0]
+    vocab_section, columns = embed_table.shape
     groups = lax.axis_size("dp")
-    tokens = token_ids.shape[0]
-    section = lax.axis_index("section").reshape(1)
+    sections = lax.axis_size(SECTION)
+    tokens, features = cotangent.shape
+    V, S = pltpu.VMEM, pltpu.SMEM
+    bf16 = functools.partial(jax.ShapeDtypeStruct, dtype=jnp.bfloat16)
+    f32 = pltpu.VMEM
+    i32 = functools.partial(jax.ShapeDtypeStruct, dtype=jnp.int32)
+    section = lax.axis_index(SECTION).reshape(1)
     own_ids = token_ids.reshape(1, tokens)
-    all_ids = lax.all_to_all(
-        jnp.broadcast_to(own_ids[None], (groups, 1, tokens)), "dp", 0, 0, tiled=True
-    ).reshape(groups, tokens)
-    sections = jnp.arange(lax.axis_size("section"))
-    counts = jnp.sum(all_ids[:, :, None] // vocab_section == sections, axis=1)
-    fits = jnp.max(counts) <= SLOTS
-    return lax.cond(
-        fits,
-        functools.partial(passage, SLOTS),
-        functools.partial(passage, tokens),
+    all_cotangent = lax.all_gather(cotangent, SECTION, axis=0)
+    (marked,) = call(mark_kernel, (own_ids,), (V,), [i32((groups, 1, tokens))])
+    marked = lax.all_to_all(marked, "dp", 0, 0, tiled=True).reshape(groups, tokens)
+    all_ids = marked % REPEATED
+    in_section = all_ids[:, :, None] // vocab_section == jnp.arange(sections)
+    new_in_section = in_section & (marked < REPEATED)[:, :, None]
+    fits = (jnp.max(jnp.sum(in_section, axis=1)) <= TOKEN_SLOTS) & (
+        jnp.max(jnp.sum(new_in_section, axis=1)) <= ROW_SLOTS
+    )
+
+    wide_table = f32((vocab_section + CHUNK, columns), jnp.float32)
+    wide_slots = f32((ROW_SLOTS, columns), jnp.float32)
+    index, count = call(
+        functools.partial(row_plan_kernel, vocab_section=vocab_section),
+        (section, marked), (S, V), [i32((ROW_SLOTS, LANES)), i32((8, LANES))],
+    )
+    (rows,) = call(
+        row_pick_kernel, (index, count, embed_table), (S, S, V),
+        [bf16((groups, ROW_SLOTS, columns))], [wide_table, wide_slots],
+    )
+    full_rows = lax.all_to_all(rows, "dp", 0, 0, tiled=True)
+    slot_cotangent, expand, combine = call(
+        functools.partial(select_kernel, vocab_section=vocab_section),
+        (section, own_ids, all_cotangent), (S, V, V),
+        [
+            bf16((sections, TOKEN_SLOTS, features)),
+            bf16((TOKEN_SLOTS, ROW_SLOTS)),
+            bf16((ROW_SLOTS, TOKEN_SLOTS)),
+        ],
+    )
+    half = bf16((sections // 2, TOKEN_SLOTS, features))
+    by_column, keep, give = call(
+        grad_kernel,
+        (section, full_rows, slot_cotangent, norm_gain.reshape(sections, features), expand, combine),
+        (S, V, V, V, V, V),
+        [bf16(full_rows.shape), half, half],
+        [f32((sections, TOKEN_SLOTS, features), jnp.float32)],
+    )
+    given = lax.ppermute(give, CORES, [(0, 1), (1, 0)])
+    (spread,) = call(
+        functools.partial(spread_kernel, vocab_section=vocab_section),
+        (section, own_ids, keep, given), (S, V, V, V), [bf16((sections // 2, tokens, features))],
+    )
+    by_column, spread = lax.optimization_barrier((by_column, spread))
+    fast_grad = lax.psum_scatter(spread, CHIPS, scatter_dimension=0, tiled=True)[0]
+    back = lax.all_to_all(by_column, "dp", 0, 0, tiled=True)
+
+    def fast(index, count, back, *_):
+        (grad_table,) = call(
+            row_add_kernel, (index, count, back), (S, S, V),
+            [bf16((vocab_section, columns))], [wide_table, wide_slots],
+        )
+        return grad_table, jnp.zeros((tokens, features), jnp.bfloat16)
+
+    def slow(index, count, back, *operands):
+        return passage(tokens, *operands)
+
+    grad_table, slow_grad = lax.cond(
+        fits, fast, slow, index, count, back,
         section, all_ids, own_ids, embed_table, norm_gain, cotangent,
     )
+    anywhere = pl.BlockSpec(memory_space=pl.ANY)
+    own_grad = pl.pallas_call(
+        settle_kernel,
+        in_specs=[whole((1,), S), anywhere, anywhere],
+        out_specs=anywhere,
+        out_shape=bf16((tokens, features)),
+        scratch_shapes=[pltpu.SemaphoreType.DMA],
+        input_output_aliases={1: 0},
+    )(fits.astype(jnp.int32).reshape(1), fast_grad, slow_grad)
+    return grad_table, own_grad
 
 
 def solution(mesh):
+    split = Mesh(mesh.devices.reshape(-1, 2, mesh.shape["dp"]), (CHIPS, CORES, "dp"))
     return jax.shard_map(
         on_device,
-        mesh=mesh,
-        in_specs=(P("dp"), P("section", "dp"), P(), P("dp", "section")),
-        out_specs=(P("section", "dp"), P("dp", "section")),
+        mesh=split,
+        in_specs=(P("dp"), P(SECTION, "dp"), P(), P("dp", SECTION)),
+        out_specs=(P(SECTION, "dp"), P("dp", SECTION)),
         check_vma=False,
     )

time: 160 us -> 114 us (0.71)
  blocking collectives: 49.8 us -> 0 us
  between operations: 1.3 us -> 15.4 us
  Pallas kernels: 27.1 us -> 19.6 us
  starting transfers between devices: 32.8 us -> 29.3 us
  other arithmetic: 1.82 us -> 3.64 us
    all_to_all x2 -> x0, blocking collectives: 49.8 us -> none  [the longest x1 26.3 us: passage(): full_rows = lax.all_to_all(rows, 'dp', 0, 0, tiled=True)]
    all_to_all x3, waiting for transfers between devices: 43 us -> 31 us  [the longest x1 16.9 us: on_device(): back = lax.all_to_all(by_column, 'dp', 0, 0, tiled=True)]
    all_gather x0 -> x1, waiting for transfers between devices: none -> 10.1 us  [on_device(): all_cotangent = lax.all_gather(cotangent, SECTION, axis=0)]
    pallas_call x6 -> x7, Pallas kernels: 27.1 us -> 19.6 us  [call(): pl.pallas_call(kernel, in_specs=[whole(o.shape, s) for o, s in zip(operan...]
    all_to_all x3, starting transfers between devices: 32.8 us -> 27.3 us  [the longest x1 14.8 us: on_device(): lax.all_to_all(marked, 'dp', 0, 0, tiled=True).reshape(groups, tokens)]
    ppermute x0 -> x1, starting transfers between devices: none -> 1.91 us  [on_device(): given = lax.ppermute(give, CORES, [(0, 1), (1, 0)])]
    ppermute x0 -> x1, waiting for transfers between devices: none -> 1.69 us  [on_device(): given = lax.ppermute(give, CORES, [(0, 1), (1, 0)])]
    unnamed x0 -> x8, local copies, waits for them, and re-layouts: none -> 1.6 us
  transfers between devices with their start and end apart: 3 -> 6, of which waited for: 3 -> 5; matrix products, arithmetic and copies ran while one was open for 0% -> 3% of each run, Pallas kernels for 6% -> 13%
where the time goes in v3:
time: 114 us; the launch traced here: 113 us
  waiting for transfers between devices  43.5 us (38%)
  starting transfers between devices  29.3 us (26%)
  Pallas kernels  19.6 us (17%)
  between operations  15.4 us (14%)
  other arithmetic  3.64 us (3%)
  local copies, waits for them, and re-layouts  1.64 us (1%)
    pallas_call x7, Pallas kernels, call(): pl.pallas_call(kernel, in_specs=[whole(o.shape, s) for o, s in zip(operan...  19.6 us
    all_to_all x1, waiting for transfers between devices, on_device(): back = lax.all_to_all(by_column, 'dp', 0, 0, tiled=True)  16.9 us
    all_to_all x1, starting transfers between devices, on_device(): lax.all_to_all(marked, 'dp', 0, 0, tiled=True).reshape(groups, tokens)  14.8 us
    all_gather x1, waiting for transfers between devices, on_device(): all_cotangent = lax.all_gather(cotangent, SECTION, axis=0)  10.1 us
    all_to_all x1, waiting for transfers between devices, on_device(): lax.all_to_all(marked, 'dp', 0, 0, tiled=True).reshape(groups, tokens)  8.96 us
    all_to_all x1, starting transfers between devices, on_device(): back = lax.all_to_all(by_column, 'dp', 0, 0, tiled=True)  6.51 us
    all_to_all x1, starting transfers between devices, on_device(): full_rows = lax.all_to_all(rows, 'dp', 0, 0, tiled=True)  6 us
    all_to_all x1, waiting for transfers between devices, on_device(): full_rows = lax.all_to_all(rows, 'dp', 0, 0, tiled=True)  5.16 us
  transfers between devices with their start and end apart: 6, of which 5 were waited for; matrix products, arithmetic and copies ran while one was open for 3% of the time, Pallas kernels for 13%

profile of v3, /device:TPU:6, one launch (start us, length us, event | category | flops | bytes accessed | tf_op | source)
XLA Modules:
  0.0 113.1 jit_solution(357239505515518121)
XLA Ops:
  7.2 0.0 copy-start.6
  7.2 0.0 copy-start.5
  7.2 0.0 all-gather.3.cloned.1.call-start
  7.2 0.7 all-gather.3.cloned.1.call-update
  7.9 1.4 %shard_map.59 = s32[64,1,128]{2,1,0:T(1,128)} custom-call(s32[1,128]{1,0:T(1,128)} %bitcast.13), custom_call_target="tpu_custom_call" | custom-call | tf_op jit(solution)/shard_map/pallas_call | solution.py:176
  9.3 14.8 %all-to-all-start.4 = ((s32[64,1,128]{2,1,0:T(1,128)}), s32[64,1,128]{2,1,0:T(1,128)S(1)}, u32[]{:S(2)}, u32[]{:S(2)}) async-start(s32[64,1,128]{2,1,0:T(1,128)} %shard_map.59), calls=%async_computation.4 | async-start | bytes 65536 | tf_op jit(solution)/shard_map/all_to_all | solution.py:461
  24.2 9.0 %all-to-all-done.4 = s32[64,1,128]{2,1,0:T(1,128)S(1)} async-done(((s32[64,1,128]{2,1,0:T(1,128)}), s32[64,1,128]{2,1,0:T(1,128)S(1)}, u32[]{:S(2)}, u32[]{:S(2)}) %all-to-all-start.4) | async-done | bytes 32800 | tf_op jit(solution)/shard_map/all_to_all | solution.py:461
  33.1 0.5 shard_map.60
  33.6 5.9 %shard_map.61 = bf16[64,32,128]{2,1,0:T(8,128)(2,1)} custom-call(s32[32,128]{1,0:T(8,128)S(1)} %get-tuple-element.59.index_ref, s32[8,128]{1,0:T(8,128)S(1)} %get-tuple-element.60.count_ref, bf16[8192,128]{1,0:T(8,128)(2,1)} %table_ref.1), custom_call_target="tpu_custom_call" | custom-call | tf_op jit(solution)/shard_map/pallas_call | solution.py:176
  39.5 6.0 %all-to-all-start.5 = ((bf16[64,32,128]{2,1,0:T(8,128)(2,1)}), bf16[64,32,128]{2,1,0:T(8,128)(2,1)S(1)}, u32[]{:S(2)}, u32[]{:S(2)}) async-start(bf16[64,32,128]{2,1,0:T(8,128)(2,1)} %shard_map.61), calls=%async_computation.5 | async-start | bytes 1048576 | tf_op jit(solution)/shard_map/all_to_all | solution.py:479
  45.5 0.0 reduce-scatter.2.cloned.1.call-start
  45.5 0.0 copy-done.5
  45.6 10.1 %all-gather.3.cloned.1.call-done = bf16[1024,1024]{1,0:T(8,128)(2,1)} async-done(((bf16[128,1024]{1,0:T(8,128)(2,1)}), bf16[1024,1024]{1,0:T(8,128)(2,1)}) %all-gather.3.cloned.1.call-update) | async-done | bytes 2097168 | tf_op jit(solution)/shard_map/all_gather | solution.py:459
  55.7 0.0 copy-done.6
  55.7 0.0 copy-start.2
  55.7 1.6 %copy-done.2 = bf16[1024,1024]{1,0:T(8,128)(2,1)S(1)} copy-done((bf16[1024,1024]{1,0:T(8,128)(2,1)S(1)}, bf16[1024,1024]{1,0:T(8,128)(2,1)}, u32[]{:S(2)}) %copy-start.2) | copy-done | bytes 2097176
  57.3 0.7 shard_map.62
  57.9 5.2 %all-to-all-done.5.rows_ref = bf16[64,32,128]{2,1,0:T(8,128)(2,1)S(1)} async-done(((bf16[64,32,128]{2,1,0:T(8,128)(2,1)}), bf16[64,32,128]{2,1,0:T(8,128)(2,1)S(1)}, u32[]{:S(2)}, u32[]{:S(2)}) %all-to-all-start.5) | async-done | bytes 524320 | tf_op jit(solution)/shard_map/all_to_all | solution.py:479
  63.1 3.1 %shard_map.63 = (bf16[64,32,128]{2,1,0:T(8,128)(2,1)}, bf16[4,48,1024]{2,1,0:T(8,128)(2,1)S(1)}, bf16[4,48,1024]{2,1,0:T(8,128)(2,1)S(1)}) custom-call(s32[1]{0:T(128)} %bitcast.3.section_ref, bf16[64,32,128]{2,1,0:T(8,128)(2,1)S(1)} %all-to-all-done.5.rows_ref, bf16[8,48,1024]{2,1,0:T(8,128)(2,1)S(1)} %get-tuple-element.61.cotangent_ref, ...), custom_call_target="tpu_custom_call" | custom-call | tf_op jit(solution)/shard_map/pallas_call | solution.py:176
  66.2 1.9 %collective-permute-start = (bf16[4,48,1024]{2,1,0:T(8,128)(2,1)S(1)}, bf16[4,48,1024]{2,1,0:T(8,128)(2,1)S(1)}, u32[]{:S(2)}, u32[]{:S(2)}) collective-permute-start(bf16[4,48,1024]{2,1,0:T(8,128)(2,1)S(1)} %get-tuple-element.66), channel_id=1, source_target_pairs={{0,64},{64,0},{1,65},{65,1},{2,66},{66,2},{3,67},{67,3},{4,68},{68... | collective-permute-start | bytes 1179656 | tf_op jit(solution)/shard_map/ppermute | solution.py:497
  68.1 1.7 %collective-permute-done.given_ref = bf16[4,48,1024]{2,1,0:T(8,128)(2,1)S(1)} collective-permute-done((bf16[4,48,1024]{2,1,0:T(8,128)(2,1)S(1)}, bf16[4,48,1024]{2,1,0:T(8,128)(2,1)S(1)}, u32[]{:S(2)}, u32[]{:S(2)}) %collective-permute-start) | collective-permute-done | bytes 393248 | tf_op jit(solution)/shard_map/ppermute | solution.py:497
  69.8 0.0 copy-start.4
  69.8 1.9 %shard_map.64 = bf16[4,128,1024]{2,1,0:T(8,128)(2,1)} custom-call(s32[1]{0:T(128)} %bitcast.3.section_ref, s32[1,128]{1,0:T(1,128)S(1)} %bitcast.15, bf16[4,48,1024]{2,1,0:T(8,128)(2,1)S(1)} %get-tuple-element.65.kept_ref, bf16[4,48,1024]{2,1,0:T(8,128)(2,1)S(1)} %collective-permute-done.given_ref), custom_call_target="tpu_custom_call" | custom-call | tf_op jit(solution)/shard_map/pallas_call | solution.py:176
  71.7 0.0 reduce-scatter.2.cloned.1.call-update
  71.7 6.5 %all-to-all-start.6 = ((bf16[64,32,128]{2,1,0:T(8,128)(2,1)}), bf16[64,32,128]{2,1,0:T(8,128)(2,1)S(1)}, u32[]{:S(2)}, u32[]{:S(2)}) async-start(bf16[64,32,128]{2,1,0:T(8,128)(2,1)} %get-tuple-element.67), calls=%async_computation.6 | async-start | bytes 1048576 | tf_op jit(solution)/shard_map/all_to_all | solution.py:504
  78.3 2.2 %convert_reduce_fusion = (s32[64,8]{1,0:T(8,128)S(1)}, s32[64,8]{1,0:T(8,128)S(1)}) fusion(s32[64,128]{1,0:T(8,128)S(1)} %get-tuple-element.74, pred[64,128]{1,0:T(8,128)(4,1)S(1)} %broadcast_compare_fusion), kind=kLoop, calls=%fused_computation.1 | loop fusion | flops 392192 | bytes 45056 | tf_op jit(solution)/shard_map/reduce_sum | solution.py:466
  80.5 0.7 reduce_max.18
  81.3 0.6 reduce_max.19
  83.2 16.9 %all-to-all-done.6 = bf16[64,32,128]{2,1,0:T(8,128)(2,1)S(1)} async-done(((bf16[64,32,128]{2,1,0:T(8,128)(2,1)}), bf16[64,32,128]{2,1,0:T(8,128)(2,1)S(1)}, u32[]{:S(2)}, u32[]{:S(2)}) %all-to-all-start.6) | async-done | bytes 524320 | tf_op jit(solution)/shard_map/all_to_all | solution.py:504
  100.0 0.0 copy-done.4
  100.1 6.2 %conditional.1 = (bf16[8192,128]{1,0:T(8,128)(2,1)}, bf16[128,1024]{1,0:T(8,128)(2,1)S(1)}) conditional(s32[]{:T(128)} %convert_element_type.12, (s32[64,128]{1,0:T(8,128)S(1)}, s32[64,128]{1,0:T(8,128)S(1)}, s32[1]{0:T(128)}, bf16[8192,128]{1,0:T(8,128)(2,1)}, s32[1,128]{1,0:T(1,128)S(1)}, /*index=5*/bf16[128,1024]{1,0:T(8,128)(2,1)S(1)}, ...), branch_computations={%region_4.5_spmd, %region_5.6_spmd} | conditional | flops 40960 | bytes 46235812 | solution.py:516
  100.1 6.1 %branch_1_fun.1 = bf16[8192,128]{1,0:T(8,128)(2,1)} custom-call(s32[32,128]{1,0:T(8,128)S(1)} %get-tuple-element.42.index_ref, s32[8,128]{1,0:T(8,128)S(1)} %get-tuple-element.43.count_ref, bf16[64,32,128]{2,1,0:T(8,128)(2,1)S(1)} %get-tuple-element.44.grads_ref), custom_call_target="tpu_custom_call" | custom-call | tf_op jit(solution)/shard_map/cond/branch_1_fun/pallas_call | solution.py:176
  106.2 0.0 reduce-scatter.2.cloned.1.call-done
  (6 shorter events, 0.1 us)
Async XLA Ops:
  7.2 48.5 %copy-start.6 = (s32[128]{0:T(128)S(1)}, s32[128]{0:T(128)}, u32[]{:S(2)}) copy-start(s32[128]{0:T(128)} %param.6) | copy-start | bytes 1540
  7.2 38.4 %copy-start.5 = (f32[8192]{0:T(1024)S(1)}, f32[8192]{0:T(1024)}, u32[]{:S(2)}) copy-start(f32[8192]{0:T(1024)} %param.8) | copy-start | bytes 98308
  7.2 48.5 %all-gather.3.cloned.1.call-start = ((), (), s32[]{:S(2)}) async-start(), calls=%async_computation.9 | async-start | bytes 2359296 | tf_op jit(solution)/shard_map/all_gather | solution.py:459
  9.3 23.8 %all-to-all-start.4 = ((s32[64,1,128]{2,1,0:T(1,128)}), s32[64,1,128]{2,1,0:T(1,128)S(1)}, u32[]{:S(2)}, u32[]{:S(2)}) async-start(s32[64,1,128]{2,1,0:T(1,128)} %shard_map.59), calls=%async_computation.4 | async-start | bytes 65536 | tf_op jit(solution)/shard_map/all_to_all | solution.py:461
  39.5 23.6 %all-to-all-start.5 = ((bf16[64,32,128]{2,1,0:T(8,128)(2,1)}), bf16[64,32,128]{2,1,0:T(8,128)(2,1)S(1)}, u32[]{:S(2)}, u32[]{:S(2)}) async-start(bf16[64,32,128]{2,1,0:T(8,128)(2,1)} %shard_map.61), calls=%async_computation.5 | async-start | bytes 1048576 | tf_op jit(solution)/shard_map/all_to_all | solution.py:479
  45.5 60.8 %reduce-scatter.2.cloned.1.call-start = ((), (), s32[]{:S(2)}) async-start(), calls=%async_computation.8 | async-start | bytes 1310720 | tf_op jit(solution)/shard_map/reduce_scatter | solution.py:503
  55.7 1.6 %copy-start.2 = (bf16[1024,1024]{1,0:T(8,128)(2,1)S(1)}, bf16[1024,1024]{1,0:T(8,128)(2,1)}, u32[]{:S(2)}) copy-start(bf16[1024,1024]{1,0:T(8,128)(2,1)} %all-gather.3.cloned.1.call-done) | copy-start | bytes 6291460
  66.2 3.6 %collective-permute-start = (bf16[4,48,1024]{2,1,0:T(8,128)(2,1)S(1)}, bf16[4,48,1024]{2,1,0:T(8,128)(2,1)S(1)}, u32[]{:S(2)}, u32[]{:S(2)}) collective-permute-start(bf16[4,48,1024]{2,1,0:T(8,128)(2,1)S(1)} %get-tuple-element.66), channel_id=1, source_target_pairs={{0,64},{64,0},{1,65},{65,1},{2,66},{66,2},{3,67},{67,3},{4,68},{68... | collective-permute-start | bytes 1179656 | tf_op jit(solution)/shard_map/ppermute | solution.py:497
  69.8 30.3 %copy-start.4 = (bf16[128,1024]{1,0:T(8,128)(2,1)S(1)}, bf16[128,1024]{1,0:T(8,128)(2,1)}, u32[]{:S(2)}) copy-start(bf16[128,1024]{1,0:T(8,128)(2,1)} %param.9) | copy-start | bytes 786436
  71.7 28.3 %all-to-all-start.6 = ((bf16[64,32,128]{2,1,0:T(8,128)(2,1)}), bf16[64,32,128]{2,1,0:T(8,128)(2,1)S(1)}, u32[]{:S(2)}, u32[]{:S(2)}) async-start(bf16[64,32,128]{2,1,0:T(8,128)(2,1)} %get-tuple-element.67), calls=%async_computation.6 | async-start | bytes 1048576 | tf_op jit(solution)/shard_map/all_to_all | solution.py:504
Sparse Core Ops, SparseCore 0:
  10.2 45.4 all-gather.2
  71.8 30.9 reduce-scatter.1

commit v4 on v3

--- a/solution.py
+++ b/solution.py
@@ -21,6 +21,8 @@
 
 
 def whole(shape, space=pltpu.VMEM):
+    if space == pltpu.HBM:
+        return pl.BlockSpec(memory_space=space)
     return pl.BlockSpec(shape, lambda *_: (0,) * len(shape), memory_space=space)
 
 
@@ -171,15 +173,15 @@
     lax.fori_loop(0, total_ref.shape[0] // step, narrow, 0)
 
 
-def call(kernel, operands, spaces, outs, scratch=()):
+def call(kernel, operands, spaces, outs, scratch=(), semaphores=(), room=6):
     held = sum(math.prod(a.shape) * a.dtype.itemsize for a in (*operands, *outs, *scratch))
     return pl.pallas_call(
         kernel,
         in_specs=[whole(o.shape, s) for o, s in zip(operands, spaces)],
         out_specs=[whole(o.shape) for o in outs],
         out_shape=outs,
-        scratch_shapes=list(scratch),
-        compiler_params=pltpu.CompilerParams(vmem_limit_bytes=2 * held + (6 << 20)),
+        scratch_shapes=[*scratch, *semaphores],
+        compiler_params=pltpu.CompilerParams(vmem_limit_bytes=2 * held + (room << 20)),
     )(*operands)
 
 
@@ -225,12 +227,12 @@
     return grad_table, own_grad
 
 
-def row_plan_kernel(section_ref, ids_ref, index_ref, count_ref, *, vocab_section):
-    slots = index_ref.shape[0]
-    ids = ids_ref[...].astype(jnp.float32)
+def row_plan(section, ids, plan_ref, vocab_section):
+    slots = plan_ref.shape[0] - CHUNK
+    ids = ids.astype(jnp.float32)
     ids = jnp.concatenate([ids, ids], axis=0)
     ids = ids.T.astype(jnp.int32)
-    local = ids - section_ref[0] * vocab_section
+    local = ids - section * vocab_section
     inside = (local >= 0) & (local < vocab_section) & (ids < REPEATED)
     before = (
         lax.broadcasted_iota(jnp.int32, (LANES, LANES), 1)
@@ -245,41 +247,62 @@
     rank = jnp.where(inside, rank, -1)
     short = local - vocab_section
     for c in range(slots):
-        index_ref[pl.ds(c, 1), :] = vocab_section + jnp.sum(
+        plan_ref[pl.ds(c, 1), :] = vocab_section + jnp.sum(
             jnp.where(rank == c, short, 0), axis=0, keepdims=True
         )
     count = jnp.minimum(jnp.sum(ones, axis=0, keepdims=True).astype(jnp.int32), slots)
-    count_ref[...] = jnp.broadcast_to((count + (CHUNK - 1)) // CHUNK, count_ref.shape)
-
-
-def row_pick_kernel(index_ref, count_ref, table_ref, rows_ref, wide_ref, picked_ref):
+    plan_ref[pl.ds(slots, CHUNK), :] = jnp.broadcast_to((count + (CHUNK - 1)) // CHUNK, (CHUNK, LANES))
+
+
+def row_pick_kernel(
+    section_ref, ids_ref, table_ref, rows_ref, plan_ref,
+    held_ref, wide_ref, picked_ref, steps_ref, arrived, planned, *, vocab_section
+):
     groups, slots, columns = rows_ref.shape
     entries = table_ref.shape[0]
-    step = 512
+    pieces = arrived.shape[0]
+    piece = entries // pieces
+    copies = [
+        pltpu.make_async_copy(
+            table_ref.at[pl.ds(i * piece, piece)], held_ref.at[pl.ds(i * piece, piece)], arrived.at[i]
+        )
+        for i in range(pieces)
+    ]
+    for copy in copies:
+        copy.start()
+    row_plan(section_ref[0], ids_ref[...], plan_ref, vocab_section)
+    plan_copy = pltpu.make_async_copy(plan_ref, steps_ref, planned)
+    plan_copy.start()
     picked_ref[...] = jnp.zeros(picked_ref.shape, jnp.float32)
     wide_ref[pl.ds(entries, CHUNK), :] = jnp.zeros((CHUNK, columns), jnp.float32)
-
-    def widen(i, carry):
-        wide_ref[pl.ds(i * step, step), :] = table_ref[pl.ds(i * step, step), :].astype(jnp.float32)
-        return carry
-
-    lax.fori_loop(0, entries // step, widen, 0)
+    step = 512
+
+    for i, copy in enumerate(copies):
+        copy.wait()
+
+        def widen(j, carry):
+            at = pl.ds(pl.multiple_of(i * piece + j * step, step), step)
+            wide_ref[at, :] = held_ref[at, :].astype(jnp.float32)
+            return carry
+
+        lax.fori_loop(0, piece // step, widen, 0)
+    plan_copy.wait()
 
     def group(g, carry):
         def chunk(i, carry):
             for j in range(CHUNK):
                 c = i * CHUNK + j
-                picked_ref[pl.ds(c, 1), :] = wide_ref[pl.ds(index_ref[c, g], 1), :]
+                picked_ref[pl.ds(c, 1), :] = wide_ref[pl.ds(steps_ref[c, g], 1), :]
             return carry
 
-        lax.fori_loop(0, count_ref[0, g], chunk, 0)
+        lax.fori_loop(0, steps_ref[slots, g], chunk, 0)
         rows_ref[g] = picked_ref[...].astype(jnp.bfloat16)
         return carry
 
     lax.fori_loop(0, groups, group, 0)
 
 
-def row_add_kernel(index_ref, count_ref, grads_ref, table_ref, total_ref, wide_ref):
+def row_add_kernel(plan_ref, grads_ref, table_ref, total_ref, wide_ref):
     groups, slots, columns = grads_ref.shape
     entries = table_ref.shape[0]
     step = 512
@@ -295,7 +318,7 @@
         wide_ref[...] = grads_ref[g].astype(jnp.float32)
 
         def chunk(i, carry):
-            rows = [pl.ds(index_ref[i * CHUNK + j, g], 1) for j in range(CHUNK)]
+            rows = [pl.ds(plan_ref[i * CHUNK + j, g], 1) for j in range(CHUNK)]
             sums = [
                 total_ref[row, :] + wide_ref[pl.ds(i * CHUNK + j, 1), :]
                 for j, row in enumerate(rows)
@@ -304,7 +327,7 @@
                 total_ref[row, :] = value
             return carry
 
-        lax.fori_loop(0, count_ref[0, g], chunk, 0)
+        lax.fori_loop(0, plan_ref[slots, g], chunk, 0)
         return carry
 
     lax.fori_loop(0, groups, group, 0)
@@ -334,7 +357,15 @@
     return jnp.where(condition, 1.0, 0.0).astype(jnp.bfloat16)
 
 
-def select_kernel(section_ref, ids_ref, cotangent_ref, own_ref, expand_ref, combine_ref, *, vocab_section):
+def select_kernel(
+    section_ref, ids_ref, cotangent_ref, own_ref, expand_ref, combine_ref, held_ref, arrived, *, vocab_section
+):
+    copies = [
+        pltpu.make_async_copy(cotangent_ref.at[s], held_ref.at[s], arrived.at[s])
+        for s in range(cotangent_ref.shape[0])
+    ]
+    for copy in copies:
+        copy.start()
     token_slots, row_slots = expand_ref.shape
     wide, tall, row_first, column_first = both_ways(ids_ref[...])
     section = section_ref[0]
@@ -361,28 +392,33 @@
     combine_ref[...] = lax.dot_general(
         rows, own, over_tokens, preferred_element_type=jnp.float32
     ).astype(jnp.bfloat16)
-    for s in range(cotangent_ref.shape[0]):
+    for s, copy in enumerate(copies):
+        copy.wait()
         own_ref[s] = jnp.dot(
-            own, cotangent_ref[s], preferred_element_type=jnp.float32
+            own, held_ref[s], preferred_element_type=jnp.float32
         ).astype(jnp.bfloat16)
 
 
-def grad_kernel(
-    section_ref, rows_ref, cotangent_ref, gain_ref, expand_ref, combine_ref,
-    by_column_ref, keep_ref, give_ref, embedded_ref,
+def slot_grad(k, cotangent_ref, gain_ref, embedded_ref, inverse, pull):
+    scaled = cotangent_ref[k].astype(jnp.float32) * gain_ref[pl.ds(k, 1), :]
+    return (inverse * scaled - embedded_ref[k].astype(jnp.float32) * pull).astype(jnp.bfloat16)
+
+
+def give_kernel(
+    section_ref, rows_ref, cotangent_ref, gain_ref, expand_ref,
+    give_ref, inverse_ref, pull_ref, embedded_ref,
 ):
     pieces, _, columns = rows_ref.shape
     sections, slots, features = cotangent_ref.shape
     per = features // columns
     width = pieces * columns
     expand = expand_ref[...]
-    combine = combine_ref[...]
 
     def sums(k, carry):
         squares, inners = carry
         rows = jnp.concatenate([rows_ref[k * per + j] for j in range(per)], axis=1)
         embedded = jnp.dot(expand, rows, preferred_element_type=jnp.float32)
-        embedded_ref[k] = embedded
+        embedded_ref[k] = embedded.astype(jnp.bfloat16)
         scaled = cotangent_ref[k].astype(jnp.float32) * gain_ref[pl.ds(k, 1), :]
         square = embedded * embedded
         inner = scaled * embedded
@@ -397,19 +433,42 @@
     inner = jnp.sum(inners, axis=1, keepdims=True) * (1.0 / width)
     inverse = lax.rsqrt(square_mean + epsilon)
     pull = inverse * inverse * inverse * inner
+    inverse_ref[...] = jnp.broadcast_to(inverse, inverse_ref.shape)
+    pull_ref[...] = jnp.broadcast_to(pull, pull_ref.shape)
     core = section_ref[0] % 2
 
-    def grads(k, out_ref, place):
-        scaled = cotangent_ref[k].astype(jnp.float32) * gain_ref[pl.ds(k, 1), :]
-        grad = (inverse * scaled - embedded_ref[k] * pull).astype(jnp.bfloat16)
-        out_ref[place] = grad
+    def chip(h, carry):
+        give_ref[h] = slot_grad(
+            2 * h + 1 - core, cotangent_ref, gain_ref, embedded_ref, inverse, pull
+        )
+        return carry
+
+    lax.fori_loop(0, sections // 2, chip, 0)
+
+
+def keep_kernel(
+    section_ref, cotangent_ref, gain_ref, embedded_ref, inverse_ref, pull_ref, give_ref, combine_ref,
+    by_column_ref, keep_ref,
+):
+    columns = by_column_ref.shape[2]
+    sections, _, features = cotangent_ref.shape
+    per = features // columns
+    combine = combine_ref[...]
+    inverse = inverse_ref[:, :1]
+    pull = pull_ref[:, :1]
+    core = section_ref[0] % 2
+
+    def add(k, grad):
         added = jnp.dot(combine, grad, preferred_element_type=jnp.float32).astype(jnp.bfloat16)
         for j in range(per):
             by_column_ref[k * per + j] = added[:, j * columns : (j + 1) * columns]
 
     def chip(h, carry):
-        grads(2 * h + core, keep_ref, h)
-        grads(2 * h + 1 - core, give_ref, h)
+        k = 2 * h + core
+        grad = slot_grad(k, cotangent_ref, gain_ref, embedded_ref, inverse, pull)
+        keep_ref[h] = grad
+        add(k, grad)
+        add(2 * h + 1 - core, give_ref[h])
         return carry
 
     lax.fori_loop(0, sections // 2, chip, 0)
@@ -466,35 +525,37 @@
         jnp.max(jnp.sum(new_in_section, axis=1)) <= ROW_SLOTS
     )
 
-    wide_table = f32((vocab_section + CHUNK, columns), jnp.float32)
+    wide_shape = (vocab_section + CHUNK, columns)
     wide_slots = f32((ROW_SLOTS, columns), jnp.float32)
-    index, count = call(
-        functools.partial(row_plan_kernel, vocab_section=vocab_section),
-        (section, marked), (S, V), [i32((ROW_SLOTS, LANES)), i32((8, LANES))],
-    )
-    (rows,) = call(
-        row_pick_kernel, (index, count, embed_table), (S, S, V),
-        [bf16((groups, ROW_SLOTS, columns))], [wide_table, wide_slots],
+    plan_shape = (ROW_SLOTS + CHUNK, LANES)
+    rows, plan = call(
+        functools.partial(row_pick_kernel, vocab_section=vocab_section),
+        (section, marked, embed_table), (S, V, pltpu.HBM),
+        [bf16((groups, ROW_SLOTS, columns)), i32(plan_shape)],
+        [f32(embed_table.shape, jnp.bfloat16), f32(wide_shape, jnp.float32), wide_slots],
+        [pltpu.SMEM(plan_shape, jnp.int32), pltpu.SemaphoreType.DMA((4,)), pltpu.SemaphoreType.DMA],
     )
     full_rows = lax.all_to_all(rows, "dp", 0, 0, tiled=True)
+    own_slots = bf16((sections, TOKEN_SLOTS, features))
     slot_cotangent, expand, combine = call(
         functools.partial(select_kernel, vocab_section=vocab_section),
-        (section, own_ids, all_cotangent), (S, V, V),
-        [
-            bf16((sections, TOKEN_SLOTS, features)),
-            bf16((TOKEN_SLOTS, ROW_SLOTS)),
-            bf16((ROW_SLOTS, TOKEN_SLOTS)),
-        ],
+        (section, own_ids, all_cotangent), (S, V, pltpu.HBM),
+        [own_slots, bf16((TOKEN_SLOTS, ROW_SLOTS)), bf16((ROW_SLOTS, TOKEN_SLOTS))],
+        [f32((sections, tokens, features), jnp.bfloat16)],
+        [pltpu.SemaphoreType.DMA((sections,))], room=42,
     )
     half = bf16((sections // 2, TOKEN_SLOTS, features))
-    by_column, keep, give = call(
-        grad_kernel,
-        (section, full_rows, slot_cotangent, norm_gain.reshape(sections, features), expand, combine),
-        (S, V, V, V, V, V),
-        [bf16(full_rows.shape), half, half],
-        [f32((sections, TOKEN_SLOTS, features), jnp.float32)],
+    statistic = jax.ShapeDtypeStruct((TOKEN_SLOTS, LANES), jnp.float32)
+    gain = norm_gain.reshape(sections, features)
+    give, inverse, pull, embedded = call(
+        give_kernel, (section, full_rows, slot_cotangent, gain, expand), (S, V, V, V, V),
+        [half, statistic, statistic, own_slots],
     )
     given = lax.ppermute(give, CORES, [(0, 1), (1, 0)])
+    by_column, keep = call(
+        keep_kernel, (section, slot_cotangent, gain, embedded, inverse, pull, give, combine),
+        (S, V, V, V, V, V, V, V), [bf16(full_rows.shape), half],
+    )
     (spread,) = call(
         functools.partial(spread_kernel, vocab_section=vocab_section),
         (section, own_ids, keep, given), (S, V, V, V), [bf16((sections // 2, tokens, features))],
@@ -503,18 +564,18 @@
     fast_grad = lax.psum_scatter(spread, CHIPS, scatter_dimension=0, tiled=True)[0]
     back = lax.all_to_all(by_column, "dp", 0, 0, tiled=True)
 
-    def fast(index, count, back, *_):
+    def fast(plan, back, *_):
         (grad_table,) = call(
-            row_add_kernel, (index, count, back), (S, S, V),
-            [bf16((vocab_section, columns))], [wide_table, wide_slots],
+            row_add_kernel, (plan, back), (S, V),
+            [bf16((vocab_section, columns))], [f32(wide_shape, jnp.float32), wide_slots],
         )
         return grad_table, jnp.zeros((tokens, features), jnp.bfloat16)
 
-    def slow(index, count, back, *operands):
+    def slow(plan, back, *operands):
         return passage(tokens, *operands)
 
     grad_table, slow_grad = lax.cond(
-        fits, fast, slow, index, count, back,
+        fits, fast, slow, plan, back,
         section, all_ids, own_ids, embed_table, norm_gain, cotangent,
     )
     anywhere = pl.BlockSpec(memory_space=pl.ANY)

time: 114 us -> 115 us (level)
  Pallas kernels: 19.6 us -> 21.4 us
  local copies, waits for them, and re-layouts: 1.64 us -> 0.05 us
    all_to_all x1, waiting for transfers between devices: 16.9 us -> 19 us  [on_device(): back = lax.all_to_all(by_column, 'dp', 0, 0, tiled=True)]
    pallas_call x7, Pallas kernels: 19.6 us -> 21.3 us  [call(): pl.pallas_call(kernel, in_specs=[whole(o.shape, s) for o, s in zip(operan...]
    ppermute x1, waiting for transfers between devices: 1.69 us -> 0.01 us  [on_device(): given = lax.ppermute(give, CORES, [(0, 1), (1, 0)])]
    unnamed x8 -> x6, local copies, waits for them, and re-layouts: 1.6 us -> 0.01 us
  transfers between devices with their start and end apart: 6 -> 6, of which waited for: 5 -> 4; matrix products, arithmetic and copies ran while one was open for 3% -> 3% of each run, Pallas kernels for 13% -> 16%
where the time goes in v4:
time: 115 us
  waiting for transfers between devices  43.9 us (38%)
  starting transfers between devices  30.3 us (26%)
  Pallas kernels  21.4 us (19%)
  between operations  15.5 us (13%)
  other arithmetic  3.64 us (3%)
    pallas_call x7, Pallas kernels, call(): pl.pallas_call(kernel, in_specs=[whole(o.shape, s) for o, s in zip(operan...  21.3 us
    all_to_all x1, waiting for transfers between devices, on_device(): back = lax.all_to_all(by_column, 'dp', 0, 0, tiled=True)  19 us
    all_to_all x1, starting transfers between devices, on_device(): lax.all_to_all(marked, 'dp', 0, 0, tiled=True).reshape(groups, tokens)  14.8 us
    all_gather x1, waiting for transfers between devices, on_device(): all_cotangent = lax.all_gather(cotangent, SECTION, axis=0)  10.8 us
    all_to_all x1, waiting for transfers between devices, on_device(): lax.all_to_all(marked, 'dp', 0, 0, tiled=True).reshape(groups, tokens)  8.96 us
    all_to_all x1, starting transfers between devices, on_device(): back = lax.all_to_all(by_column, 'dp', 0, 0, tiled=True)  7.52 us
    all_to_all x1, starting transfers between devices, on_device(): full_rows = lax.all_to_all(rows, 'dp', 0, 0, tiled=True)  6.01 us
    all_to_all x1, waiting for transfers between devices, on_device(): full_rows = lax.all_to_all(rows, 'dp', 0, 0, tiled=True)  4.36 us
  transfers between devices with their start and end apart: 6, of which 4 were waited for; matrix products, arithmetic and copies ran while one was open for 3% of the time, Pallas kernels for 16%

profile of v4, /device:TPU:6, one launch (start us, length us, event | category | flops | bytes accessed | tf_op | source)
XLA Modules:
  0.0 114.7 jit_solution(5404001759049685119)
XLA Ops:
  7.2 0.0 copy-start.5
  7.2 0.0 copy-start.4
  7.2 0.0 all-gather.3.cloned.1.call-start
  7.2 0.7 all-gather.3.cloned.1.call-update
  7.9 1.4 %shard_map.59 = s32[64,1,128]{2,1,0:T(1,128)} custom-call(s32[1,128]{1,0:T(1,128)} %bitcast.13), custom_call_target="tpu_custom_call" | custom-call | tf_op jit(solution)/shard_map/pallas_call | solution.py:178
  9.3 14.8 %all-to-all-start.4 = ((s32[64,1,128]{2,1,0:T(1,128)}), s32[64,1,128]{2,1,0:T(1,128)S(1)}, u32[]{:S(2)}, u32[]{:S(2)}) async-start(s32[64,1,128]{2,1,0:T(1,128)} %shard_map.59), calls=%async_computation.4 | async-start | bytes 65536 | tf_op jit(solution)/shard_map/all_to_all | solution.py:520
  24.2 9.0 %all-to-all-done.4 = s32[64,1,128]{2,1,0:T(1,128)S(1)} async-done(((s32[64,1,128]{2,1,0:T(1,128)}), s32[64,1,128]{2,1,0:T(1,128)S(1)}, u32[]{:S(2)}, u32[]{:S(2)}) %all-to-all-start.4) | async-done | bytes 32800 | tf_op jit(solution)/shard_map/all_to_all | solution.py:520
  33.1 5.7 %shard_map.60 = (bf16[64,32,128]{2,1,0:T(8,128)(2,1)}, s32[40,128]{1,0:T(8,128)S(1)}) custom-call(s32[1]{0:T(128)} %bitcast.3.section_ref, s32[64,128]{1,0:T(8,128)S(1)} %bitcast.7, bf16[8192,128]{1,0:T(8,128)(2,1)} %table_ref.1), custom_call_target="tpu_custom_call" | custom-call | tf_op jit(solution)/shard_map/pallas_call | solution.py:178
  38.8 6.0 %all-to-all-start.5 = ((bf16[64,32,128]{2,1,0:T(8,128)(2,1)}), bf16[64,32,128]{2,1,0:T(8,128)(2,1)S(1)}, u32[]{:S(2)}, u32[]{:S(2)}) async-start(bf16[64,32,128]{2,1,0:T(8,128)(2,1)} %get-tuple-element.61), calls=%async_computation.5 | async-start | bytes 1048576 | tf_op jit(solution)/shard_map/all_to_all | solution.py:538
  44.9 0.0 reduce-scatter.2.cloned.1.call-start
  44.9 0.0 copy-done.4
  44.9 10.8 %all-gather.3.cloned.1.call-done = bf16[1024,1024]{1,0:T(8,128)(2,1)} async-done(((bf16[128,1024]{1,0:T(8,128)(2,1)}), bf16[1024,1024]{1,0:T(8,128)(2,1)}) %all-gather.3.cloned.1.call-update) | async-done | bytes 2097168 | tf_op jit(solution)/shard_map/all_gather | solution.py:518
  55.8 0.0 copy-done.5
  55.8 2.5 %shard_map.61 = (bf16[8,48,1024]{2,1,0:T(8,128)(2,1)S(1)}, bf16[48,32]{1,0:T(8,128)(2,1)S(1)}, bf16[32,48]{1,0:T(8,128)(2,1)S(1)}) custom-call(s32[1]{0:T(128)} %bitcast.3.section_ref, s32[1,128]{1,0:T(1,128)S(1)} %bitcast.14, bf16[8,128,1024]{2,1,0:T(8,128)(2,1)} %bitcast.10), custom_call_target="tpu_custom_call" | custom-call | tf_op jit(solution)/shard_map/pallas_call | solution.py:178
  58.3 4.4 %all-to-all-done.5.rows_ref = bf16[64,32,128]{2,1,0:T(8,128)(2,1)S(1)} async-done(((bf16[64,32,128]{2,1,0:T(8,128)(2,1)}), bf16[64,32,128]{2,1,0:T(8,128)(2,1)S(1)}, u32[]{:S(2)}, u32[]{:S(2)}) %all-to-all-start.5) | async-done | bytes 524320 | tf_op jit(solution)/shard_map/all_to_all | solution.py:538
  62.7 1.6 %shard_map.62 = (bf16[4,48,1024]{2,1,0:T(8,128)(2,1)S(1)}, f32[48,128]{1,0:T(8,128)S(1)}, f32[48,128]{1,0:T(8,128)S(1)}, bf16[8,48,1024]{2,1,0:T(8,128)(2,1)S(1)}) custom-call(s32[1]{0:T(128)} %bitcast.3.section_ref, bf16[64,32,128]{2,1,0:T(8,128)(2,1)S(1)} %all-to-all-done.5.rows_ref, bf16[8,48,1024]{2,1,0:T(8,128)(2,1)S(1)} %get-tuple-element.60.cotangent_ref, ...), custom_call_target="tpu_custom_call" | custom-call | tf_op jit(solution)/shard_map/pallas_call | solution.py:178
  64.3 1.9 %collective-permute-start = (bf16[4,48,1024]{2,1,0:T(8,128)(2,1)S(1)}, bf16[4,48,1024]{2,1,0:T(8,128)(2,1)S(1)}, u32[]{:S(2)}, u32[]{:S(2)}) collective-permute-start(bf16[4,48,1024]{2,1,0:T(8,128)(2,1)S(1)} %get-tuple-element.66.give_ref), channel_id=1, source_target_pairs={{0,64},{64,0},{1,65},{65,1},{2,66},{66,2},{3,67},{67,3},{4,68},{68... | collective-permute-start | bytes 1179656 | tf_op jit(solution)/shard_map/ppermute | solution.py:554
  66.2 1.8 %shard_map.63 = (bf16[64,32,128]{2,1,0:T(8,128)(2,1)}, bf16[4,48,1024]{2,1,0:T(8,128)(2,1)S(1)}) custom-call(s32[1]{0:T(128)} %bitcast.3.section_ref, bf16[8,48,1024]{2,1,0:T(8,128)(2,1)S(1)} %get-tuple-element.60.cotangent_ref, f32[8,1024]{1,0:T(8,128)S(1)} %reshape.84.gain_ref, bf16[8,48,1024]{2,1,0:T(8,128)(2,1)S(1)} %get-tuple-element.63.embedded_ref, ...), custom_call_target="tpu_custom_call" | custom-call | tf_op jit(solution)/shard_map/pallas_call | solution.py:178
  68.1 0.0 collective-permute-done.given_ref
  68.1 0.0 copy-start.3
  68.1 1.9 %shard_map.64 = bf16[4,128,1024]{2,1,0:T(8,128)(2,1)} custom-call(s32[1]{0:T(128)} %bitcast.3.section_ref, s32[1,128]{1,0:T(1,128)S(1)} %bitcast.15, bf16[4,48,1024]{2,1,0:T(8,128)(2,1)S(1)} %get-tuple-element.69.kept_ref, bf16[4,48,1024]{2,1,0:T(8,128)(2,1)S(1)} %collective-permute-done.given_ref), custom_call_target="tpu_custom_call" | custom-call | tf_op jit(solution)/shard_map/pallas_call | solution.py:178
  70.0 0.0 reduce-scatter.2.cloned.1.call-update
  70.0 7.5 %all-to-all-start.6 = ((bf16[64,32,128]{2,1,0:T(8,128)(2,1)}), bf16[64,32,128]{2,1,0:T(8,128)(2,1)S(1)}, u32[]{:S(2)}, u32[]{:S(2)}) async-start(bf16[64,32,128]{2,1,0:T(8,128)(2,1)} %get-tuple-element.70), calls=%async_computation.6 | async-start | bytes 1048576 | tf_op jit(solution)/shard_map/all_to_all | solution.py:565
  77.6 2.2 %convert_reduce_fusion = (s32[64,8]{1,0:T(8,128)S(1)}, s32[64,8]{1,0:T(8,128)S(1)}) fusion(s32[64,128]{1,0:T(8,128)S(1)} %get-tuple-element.77, pred[64,128]{1,0:T(8,128)(4,1)S(1)} %broadcast_compare_fusion), kind=kLoop, calls=%fused_computation.1 | loop fusion | flops 392192 | bytes 45056 | tf_op jit(solution)/shard_map/reduce_sum | solution.py:525
  79.8 0.7 reduce_max.18
  80.6 0.6 reduce_max.19
  82.5 19.0 %all-to-all-done.6 = bf16[64,32,128]{2,1,0:T(8,128)(2,1)S(1)} async-done(((bf16[64,32,128]{2,1,0:T(8,128)(2,1)}), bf16[64,32,128]{2,1,0:T(8,128)(2,1)S(1)}, u32[]{:S(2)}, u32[]{:S(2)}) %all-to-all-start.6) | async-done | bytes 524320 | tf_op jit(solution)/shard_map/all_to_all | solution.py:565
  101.5 0.0 copy-done.3
  101.5 6.4 %conditional.1 = (bf16[8192,128]{1,0:T(8,128)(2,1)}, bf16[128,1024]{1,0:T(8,128)(2,1)S(1)}) conditional(s32[]{:T(128)} %convert_element_type.12, (s32[64,128]{1,0:T(8,128)S(1)}, s32[64,128]{1,0:T(8,128)S(1)}, s32[1]{0:T(128)}, bf16[8192,128]{1,0:T(8,128)(2,1)}, s32[1,128]{1,0:T(1,128)S(1)}, /*index=5*/bf16[128,1024]{1,0:T(8,128)(2,1)S(1)}, ...), branch_computations={%region_4.5_spmd, %region_5.6_spmd} | conditional | flops 40960 | bytes 46235812 | solution.py:577
  101.5 6.3 %branch_1_fun.1 = bf16[8192,128]{1,0:T(8,128)(2,1)} custom-call(s32[40,128]{1,0:T(8,128)S(1)} %get-tuple-element.40.plan_ref, bf16[64,32,128]{2,1,0:T(8,128)(2,1)S(1)} %get-tuple-element.41.grads_ref), custom_call_target="tpu_custom_call" | custom-call | tf_op jit(solution)/shard_map/cond/branch_1_fun/pallas_call | solution.py:178
  107.8 0.0 reduce-scatter.2.cloned.1.call-done
  (6 shorter events, 0.1 us)
Async XLA Ops:
  7.2 48.6 %copy-start.5 = (s32[128]{0:T(128)S(1)}, s32[128]{0:T(128)}, u32[]{:S(2)}) copy-start(s32[128]{0:T(128)} %param.6) | copy-start | bytes 1540
  7.2 37.7 %copy-start.4 = (f32[8192]{0:T(1024)S(1)}, f32[8192]{0:T(1024)}, u32[]{:S(2)}) copy-start(f32[8192]{0:T(1024)} %param.8) | copy-start | bytes 98308
  7.2 48.6 %all-gather.3.cloned.1.call-start = ((), (), s32[]{:S(2)}) async-start(), calls=%async_computation.9 | async-start | bytes 2359296 | tf_op jit(solution)/shard_map/all_gather | solution.py:518
  9.3 23.8 %all-to-all-start.4 = ((s32[64,1,128]{2,1,0:T(1,128)}), s32[64,1,128]{2,1,0:T(1,128)S(1)}, u32[]{:S(2)}, u32[]{:S(2)}) async-start(s32[64,1,128]{2,1,0:T(1,128)} %shard_map.59), calls=%async_computation.4 | async-start | bytes 65536 | tf_op jit(solution)/shard_map/all_to_all | solution.py:520
  38.8 23.8 %all-to-all-start.5 = ((bf16[64,32,128]{2,1,0:T(8,128)(2,1)}), bf16[64,32,128]{2,1,0:T(8,128)(2,1)S(1)}, u32[]{:S(2)}, u32[]{:S(2)}) async-start(bf16[64,32,128]{2,1,0:T(8,128)(2,1)} %get-tuple-element.61), calls=%async_computation.5 | async-start | bytes 1048576 | tf_op jit(solution)/shard_map/all_to_all | solution.py:538
  44.9 63.0 %reduce-scatter.2.cloned.1.call-start = ((), (), s32[]{:S(2)}) async-start(), calls=%async_computation.8 | async-start | bytes 1310720 | tf_op jit(solution)/shard_map/reduce_scatter | solution.py:564
  64.3 3.8 %collective-permute-start = (bf16[4,48,1024]{2,1,0:T(8,128)(2,1)S(1)}, bf16[4,48,1024]{2,1,0:T(8,128)(2,1)S(1)}, u32[]{:S(2)}, u32[]{:S(2)}) collective-permute-start(bf16[4,48,1024]{2,1,0:T(8,128)(2,1)S(1)} %get-tuple-element.66.give_ref), channel_id=1, source_target_pairs={{0,64},{64,0},{1,65},{65,1},{2,66},{66,2},{3,67},{67,3},{4,68},{68... | collective-permute-start | bytes 1179656 | tf_op jit(solution)/shard_map/ppermute | solution.py:554
  68.1 33.4 %copy-start.3 = (bf16[128,1024]{1,0:T(8,128)(2,1)S(1)}, bf16[128,1024]{1,0:T(8,128)(2,1)}, u32[]{:S(2)}) copy-start(bf16[128,1024]{1,0:T(8,128)(2,1)} %param.9) | copy-start | bytes 786436
  70.0 31.4 %all-to-all-start.6 = ((bf16[64,32,128]{2,1,0:T(8,128)(2,1)}), bf16[64,32,128]{2,1,0:T(8,128)(2,1)S(1)}, u32[]{:S(2)}, u32[]{:S(2)}) async-start(bf16[64,32,128]{2,1,0:T(8,128)(2,1)} %get-tuple-element.70), calls=%async_computation.6 | async-start | bytes 1048576 | tf_op jit(solution)/shard_map/all_to_all | solution.py:565
Sparse Core Ops, SparseCore 0:
  10.2 45.5 all-gather.2
  70.1 32.3 reduce-scatter.1

commit v5 on v4

--- a/solution.py
+++ b/solution.py
@@ -357,18 +357,32 @@
     return jnp.where(condition, 1.0, 0.0).astype(jnp.bfloat16)
 
 
-def select_kernel(
-    section_ref, ids_ref, cotangent_ref, own_ref, expand_ref, combine_ref, held_ref, arrived, *, vocab_section
-):
-    copies = [
-        pltpu.make_async_copy(cotangent_ref.at[s], held_ref.at[s], arrived.at[s])
-        for s in range(cotangent_ref.shape[0])
-    ]
-    for copy in copies:
-        copy.start()
+def ranks(ids_row, vocab_section):
+    wide, tall, row_first, column_first = both_ways(ids_row)
+    wide = wide // vocab_section
+    tall = tall // vocab_section
+    same = wide == tall
+    as_row = jnp.sum(jnp.where(same & row_first, 1, 0), axis=0, keepdims=True)
+    as_column = jnp.sum(jnp.where(same & column_first, 1.0, 0.0), axis=1, keepdims=True)
+    return wide[:1], as_row, tall[:, :1], as_column.astype(jnp.int32)
+
+
+def hand_kernel(section_ref, ids_ref, cotangent_ref, *refs, vocab_section):
+    *hand_refs, expand_ref, combine_ref = refs
     token_slots, row_slots = expand_ref.shape
+    section = section_ref[0]
+    wide_section, wide_rank, _, _ = ranks(ids_ref[...], vocab_section)
+    slot = lax.broadcasted_iota(jnp.int32, (token_slots, LANES), 0)
+    cotangent = cotangent_ref[...]
+    for k, hand_ref in enumerate(hand_refs):
+        for c in range(2):
+            to = 2 * ((section // 2) ^ k) + c
+            wanted = one_hot((slot == wide_rank) & (wide_section == to))
+            hand_ref[c] = jnp.dot(
+                wanted, cotangent, preferred_element_type=jnp.float32
+            ).astype(jnp.bfloat16)
+
     wide, tall, row_first, column_first = both_ways(ids_ref[...])
-    section = section_ref[0]
     wide_in = wide // vocab_section == section
     tall_in = tall // vocab_section == section
     same = wide == tall
@@ -376,9 +390,7 @@
     tall_repeat = jnp.max(jnp.where(same & column_first, 1.0, 0.0), axis=1, keepdims=True)
     wide_new = wide_in & (jnp.broadcast_to(wide_repeat, (LANES, LANES)) == 0)
     tall_new = tall_in & (jnp.broadcast_to(tall_repeat, (LANES, LANES)) == 0.0)
-    rank = jnp.sum(jnp.where(tall_in & row_first, 1, 0), axis=0, keepdims=True)
-    rank = jnp.where(wide_in[:1], rank, -1)
-    own = one_hot(lax.broadcasted_iota(jnp.int32, (token_slots, LANES), 0) == rank)
+    own = one_hot((slot == wide_rank) & (wide_section == section))
     tall_place = jnp.sum(jnp.where(wide_new & column_first, 1.0, 0.0), axis=1, keepdims=True)
     place = jnp.sum(
         jnp.where(same & tall_new, jnp.broadcast_to(tall_place, (LANES, LANES)), 0.0), axis=0, keepdims=True
@@ -392,108 +404,72 @@
     combine_ref[...] = lax.dot_general(
         rows, own, over_tokens, preferred_element_type=jnp.float32
     ).astype(jnp.bfloat16)
-    for s, copy in enumerate(copies):
-        copy.wait()
-        own_ref[s] = jnp.dot(
-            own, held_ref[s], preferred_element_type=jnp.float32
-        ).astype(jnp.bfloat16)
-
-
-def slot_grad(k, cotangent_ref, gain_ref, embedded_ref, inverse, pull):
-    scaled = cotangent_ref[k].astype(jnp.float32) * gain_ref[pl.ds(k, 1), :]
-    return (inverse * scaled - embedded_ref[k].astype(jnp.float32) * pull).astype(jnp.bfloat16)
-
-
-def give_kernel(
-    section_ref, rows_ref, cotangent_ref, gain_ref, expand_ref,
-    give_ref, inverse_ref, pull_ref, embedded_ref,
-):
+
+
+def part_kernel(section_ref, *refs):
+    *hand_refs, give_ref = refs
+    for k, hand_ref in enumerate(hand_refs):
+        give_ref[k] = hand_ref[1 - section_ref[0] % 2]
+
+
+def grad_kernel(section_ref, rows_ref, gain_ref, expand_ref, combine_ref, got_ref, *refs, chips):
+    own_refs, by_column_ref, out_refs = refs[:chips], refs[chips], refs[chips + 1 : -1]
+    embedded_ref = refs[-1]
     pieces, _, columns = rows_ref.shape
-    sections, slots, features = cotangent_ref.shape
+    _, slots, features = got_ref.shape
     per = features // columns
     width = pieces * columns
     expand = expand_ref[...]
-
-    def sums(k, carry):
-        squares, inners = carry
-        rows = jnp.concatenate([rows_ref[k * per + j] for j in range(per)], axis=1)
+    combine = combine_ref[...]
+    section = section_ref[0]
+    core = section % 2
+    parts = []
+    for k in range(chips):
+        chip = (section // 2) ^ k
+        parts.append((k, 2 * chip + core, core, own_refs[k].at[core]))
+        parts.append((k, 2 * chip + 1 - core, 1 - core, got_ref.at[k]))
+
+    squares = jnp.zeros((slots, columns), jnp.float32)
+    inners = jnp.zeros((slots, columns), jnp.float32)
+    for i, (_, s, _, cotangent_ref) in enumerate(parts):
+        rows = jnp.concatenate([rows_ref[s * per + j] for j in range(per)], axis=1)
         embedded = jnp.dot(expand, rows, preferred_element_type=jnp.float32)
-        embedded_ref[k] = embedded.astype(jnp.bfloat16)
-        scaled = cotangent_ref[k].astype(jnp.float32) * gain_ref[pl.ds(k, 1), :]
+        embedded_ref[i] = embedded.astype(jnp.bfloat16)
+        scaled = cotangent_ref[...].astype(jnp.float32) * gain_ref[pl.ds(s, 1), :]
         square = embedded * embedded
         inner = scaled * embedded
         for j in range(per):
             squares = squares + square[:, j * columns : (j + 1) * columns]
             inners = inners + inner[:, j * columns : (j + 1) * columns]
-        return squares, inners
-
-    zeros = jnp.zeros((slots, columns), jnp.float32)
-    squares, inners = lax.fori_loop(0, sections, sums, (zeros, zeros))
     square_mean = jnp.sum(squares, axis=1, keepdims=True) * (1.0 / width)
     inner = jnp.sum(inners, axis=1, keepdims=True) * (1.0 / width)
     inverse = lax.rsqrt(square_mean + epsilon)
     pull = inverse * inverse * inverse * inner
-    inverse_ref[...] = jnp.broadcast_to(inverse, inverse_ref.shape)
-    pull_ref[...] = jnp.broadcast_to(pull, pull_ref.shape)
-    core = section_ref[0] % 2
-
-    def chip(h, carry):
-        give_ref[h] = slot_grad(
-            2 * h + 1 - core, cotangent_ref, gain_ref, embedded_ref, inverse, pull
-        )
-        return carry
-
-    lax.fori_loop(0, sections // 2, chip, 0)
-
-
-def keep_kernel(
-    section_ref, cotangent_ref, gain_ref, embedded_ref, inverse_ref, pull_ref, give_ref, combine_ref,
-    by_column_ref, keep_ref,
-):
-    columns = by_column_ref.shape[2]
-    sections, _, features = cotangent_ref.shape
-    per = features // columns
-    combine = combine_ref[...]
-    inverse = inverse_ref[:, :1]
-    pull = pull_ref[:, :1]
-    core = section_ref[0] % 2
-
-    def add(k, grad):
+
+    for i, (k, s, place, cotangent_ref) in enumerate(parts):
+        scaled = cotangent_ref[...].astype(jnp.float32) * gain_ref[pl.ds(s, 1), :]
+        grad = (inverse * scaled - embedded_ref[i].astype(jnp.float32) * pull).astype(jnp.bfloat16)
+        out_refs[k][place] = grad
         added = jnp.dot(combine, grad, preferred_element_type=jnp.float32).astype(jnp.bfloat16)
         for j in range(per):
-            by_column_ref[k * per + j] = added[:, j * columns : (j + 1) * columns]
-
-    def chip(h, carry):
-        k = 2 * h + core
-        grad = slot_grad(k, cotangent_ref, gain_ref, embedded_ref, inverse, pull)
-        keep_ref[h] = grad
-        add(k, grad)
-        add(2 * h + 1 - core, give_ref[h])
-        return carry
-
-    lax.fori_loop(0, sections // 2, chip, 0)
-
-
-def spread_kernel(section_ref, ids_ref, kept_ref, given_ref, spread_ref, *, vocab_section):
-    slots = kept_ref.shape[1]
-    wide, tall, _, column_first = both_ways(ids_ref[...])
-    wide = wide // vocab_section
-    tall = tall // vocab_section
+            by_column_ref[s * per + j] = added[:, j * columns : (j + 1) * columns]
+
+
+def gather_kernel(section_ref, ids_ref, got_ref, *refs, vocab_section):
+    *home_refs, own_ref = refs
+    slots = got_ref.shape[1]
+    _, _, tall_section, tall_rank = ranks(ids_ref[...], vocab_section)
     along = lax.broadcasted_iota(jnp.int32, (LANES, slots), 1)
-
-    def of(section):
-        rank = jnp.sum(jnp.where((wide == section) & column_first, 1.0, 0.0), axis=1, keepdims=True)
-        rank = jnp.where(tall[:, :1] == section, rank.astype(jnp.int32), -1)
-        return one_hot(along == rank)
-
     section = section_ref[0]
-    mine = of(section)
-    theirs = of(section + 1 - 2 * (section % 2))
-    for h in range(kept_ref.shape[0]):
-        spread_ref[h] = (
-            jnp.dot(mine, kept_ref[h], preferred_element_type=jnp.float32)
-            + jnp.dot(theirs, given_ref[h], preferred_element_type=jnp.float32)
-        ).astype(jnp.bfloat16)
+    core = section % 2
+    total = jnp.zeros(own_ref.shape, jnp.float32)
+    for k, home_ref in enumerate(home_refs):
+        chip = (section // 2) ^ k
+        mine = one_hot((along == tall_rank) & (tall_section == 2 * chip + core))
+        theirs = one_hot((along == tall_rank) & (tall_section == 2 * chip + 1 - core))
+        total = total + jnp.dot(mine, home_ref[core], preferred_element_type=jnp.float32)
+        total = total + jnp.dot(theirs, got_ref[k], preferred_element_type=jnp.float32)
+    own_ref[...] = total.astype(jnp.bfloat16)
 
 
 def settle_kernel(fits_ref, fast_ref, slow_ref, out_ref, semaphore):
@@ -515,7 +491,6 @@
     i32 = functools.partial(jax.ShapeDtypeStruct, dtype=jnp.int32)
     section = lax.axis_index(SECTION).reshape(1)
     own_ids = token_ids.reshape(1, tokens)
-    all_cotangent = lax.all_gather(cotangent, SECTION, axis=0)
     (marked,) = call(mark_kernel, (own_ids,), (V,), [i32((groups, 1, tokens))])
     marked = lax.all_to_all(marked, "dp", 0, 0, tiled=True).reshape(groups, tokens)
     all_ids = marked % REPEATED
@@ -527,6 +502,13 @@
 
     wide_shape = (vocab_section + CHUNK, columns)
     wide_slots = f32((ROW_SLOTS, columns), jnp.float32)
+    *hands, expand, combine = call(
+        functools.partial(hand_kernel, vocab_section=vocab_section),
+        (section, own_ids, cotangent), (S, V, V),
+        [bf16((2, TOKEN_SLOTS, features))] * (sections // 2)
+        + [bf16((TOKEN_SLOTS, ROW_SLOTS)), bf16((ROW_SLOTS, TOKEN_SLOTS))],
+    )
+    hands, marked = lax.optimization_barrier((hands, marked))
     plan_shape = (ROW_SLOTS + CHUNK, LANES)
     rows, plan = call(
         functools.partial(row_pick_kernel, vocab_section=vocab_section),
@@ -536,33 +518,35 @@
         [pltpu.SMEM(plan_shape, jnp.int32), pltpu.SemaphoreType.DMA((4,)), pltpu.SemaphoreType.DMA],
     )
     full_rows = lax.all_to_all(rows, "dp", 0, 0, tiled=True)
-    own_slots = bf16((sections, TOKEN_SLOTS, features))
-    slot_cotangent, expand, combine = call(
-        functools.partial(select_kernel, vocab_section=vocab_section),
-        (section, own_ids, all_cotangent), (S, V, pltpu.HBM),
-        [own_slots, bf16((TOKEN_SLOTS, ROW_SLOTS)), bf16((ROW_SLOTS, TOKEN_SLOTS))],
-        [f32((sections, tokens, features), jnp.bfloat16)],
-        [pltpu.SemaphoreType.DMA((sections,))], room=42,
-    )
-    half = bf16((sections // 2, TOKEN_SLOTS, features))
-    statistic = jax.ShapeDtypeStruct((TOKEN_SLOTS, LANES), jnp.float32)
-    gain = norm_gain.reshape(sections, features)
-    give, inverse, pull, embedded = call(
-        give_kernel, (section, full_rows, slot_cotangent, gain, expand), (S, V, V, V, V),
-        [half, statistic, statistic, own_slots],
-    )
-    given = lax.ppermute(give, CORES, [(0, 1), (1, 0)])
-    by_column, keep = call(
-        keep_kernel, (section, slot_cotangent, gain, embedded, inverse, pull, give, combine),
-        (S, V, V, V, V, V, V, V), [bf16(full_rows.shape), half],
-    )
-    (spread,) = call(
-        functools.partial(spread_kernel, vocab_section=vocab_section),
-        (section, own_ids, keep, given), (S, V, V, V), [bf16((sections // 2, tokens, features))],
-    )
-    by_column, spread = lax.optimization_barrier((by_column, spread))
-    fast_grad = lax.psum_scatter(spread, CHIPS, scatter_dimension=0, tiled=True)[0]
+    chips = sections // 2
+    both = bf16((2, TOKEN_SLOTS, features))
+    one = bf16((chips, TOKEN_SLOTS, features))
+
+    def between_chips(arrays):
+        return arrays[:1] + [
+            lax.ppermute(a, CHIPS, [(i, i ^ k) for i in range(chips)])
+            for k, a in enumerate(arrays[1:], 1)
+        ]
+
+    def from_sibling(arrays):
+        (give,) = call(part_kernel, (section, *arrays), (S,) + (V,) * chips, [one])
+        return lax.ppermute(give, CORES, [(0, 1), (1, 0)])
+
+    handed = between_chips(hands)
+    got = from_sibling(handed)
+    by_column, *outs = call(
+        functools.partial(grad_kernel, chips=chips),
+        (section, full_rows, norm_gain.reshape(sections, features), expand, combine, got, *handed),
+        (S,) + (V,) * (5 + chips), [bf16(full_rows.shape)] + [both] * chips,
+        [f32((sections, TOKEN_SLOTS, features), jnp.bfloat16)],
+    )
+    home = between_chips(outs)
     back = lax.all_to_all(by_column, "dp", 0, 0, tiled=True)
+    home_got = from_sibling(home)
+    (fast_grad,) = call(
+        functools.partial(gather_kernel, vocab_section=vocab_section),
+        (section, own_ids, home_got, *home), (S,) + (V,) * (2 + chips), [bf16((tokens, features))],
+    )
 
     def fast(plan, back, *_):
         (grad_table,) = call(

time: 115 us -> 126 us (1.096); the launches traced: 115 us -> 124 us
  starting transfers between devices: 30.3 us -> 61.9 us
  between operations: 15.5 us -> 2.11 us
  waiting for transfers between devices: 43.9 us -> 37.9 us
  Pallas kernels: 21.4 us -> 18.3 us
    ppermute x1 -> x8, waiting for transfers between devices: 0.01 us -> 30.5 us  [the longest x6 28.8 us: between_chips(): lax.ppermute(a, CHIPS, [(i, i ^ k) for i in range(chips)])]
    ppermute x1 -> x8, starting transfers between devices: 1.92 us -> 28.3 us  [the longest x6 24.4 us: between_chips(): lax.ppermute(a, CHIPS, [(i, i ^ k) for i in range(chips)])]
    all_to_all x1, waiting for transfers between devices: 19 us -> 0.01 us  [on_device(): back = lax.all_to_all(by_column, 'dp', 0, 0, tiled=True)]
    all_gather x1 -> x0, waiting for transfers between devices: 10.8 us -> none  [on_device(): all_cotangent = lax.all_gather(cotangent, SECTION, axis=0)]
    all_to_all x1, starting transfers between devices: 7.52 us -> 12.8 us  [on_device(): back = lax.all_to_all(by_column, 'dp', 0, 0, tiled=True)]
    all_to_all x1, waiting for transfers between devices: 4.36 us -> 0.01 us  [on_device(): full_rows = lax.all_to_all(rows, 'dp', 0, 0, tiled=True)]
    pallas_call x7 -> x8, Pallas kernels: 21.3 us -> 18.3 us  [call(): pl.pallas_call(kernel, in_specs=[whole(o.shape, s) for o, s in zip(operan...]
    all_to_all x1, waiting for transfers between devices: 8.96 us -> 7.43 us  [on_device(): lax.all_to_all(marked, 'dp', 0, 0, tiled=True).reshape(groups, tokens)]
  transfers between devices with their start and end apart: 6 -> 11, of which waited for: 4 -> 6; matrix products, arithmetic and copies ran while one was open for 3% -> 3% of each run, Pallas kernels for 16% -> 3%
where the time goes in v5:
time: 126 us; the launch traced here: 124 us
  starting transfers between devices  61.9 us (49%)
  waiting for transfers between devices  37.9 us (30%)
  Pallas kernels  18.3 us (15%)
  other arithmetic  3.6 us (3%)
  between operations  2.11 us (2%)
    ppermute x6, waiting for transfers between devices, between_chips(): lax.ppermute(a, CHIPS, [(i, i ^ k) for i in range(chips)])  28.8 us
    ppermute x6, starting transfers between devices, between_chips(): lax.ppermute(a, CHIPS, [(i, i ^ k) for i in range(chips)])  24.4 us
    pallas_call x8, Pallas kernels, call(): pl.pallas_call(kernel, in_specs=[whole(o.shape, s) for o, s in zip(operan...  18.3 us
    all_to_all x1, starting transfers between devices, on_device(): lax.all_to_all(marked, 'dp', 0, 0, tiled=True).reshape(groups, tokens)  14.8 us
    all_to_all x1, starting transfers between devices, on_device(): back = lax.all_to_all(by_column, 'dp', 0, 0, tiled=True)  12.8 us
    all_to_all x1, waiting for transfers between devices, on_device(): lax.all_to_all(marked, 'dp', 0, 0, tiled=True).reshape(groups, tokens)  7.43 us
    all_to_all x1, starting transfers between devices, on_device(): full_rows = lax.all_to_all(rows, 'dp', 0, 0, tiled=True)  6.01 us
    ppermute x2, starting transfers between devices, from_sibling(): return lax.ppermute(give, CORES, [(0, 1), (1, 0)])  3.85 us
  transfers between devices with their start and end apart: 11, of which 6 were waited for; matrix products, arithmetic and copies ran while one was open for 3% of the time, Pallas kernels for 3%

profile of v5, /device:TPU:6, one launch (start us, length us, event | category | flops | bytes accessed | tf_op | source)
XLA Modules:
  0.0 123.9 jit_solution(9415598040106914061)
XLA Ops:
  0.6 1.4 %shard_map.59 = s32[64,1,128]{2,1,0:T(1,128)} custom-call(s32[1,128]{1,0:T(1,128)} %bitcast.9), custom_call_target="tpu_custom_call" | custom-call | tf_op jit(solution)/shard_map/pallas_call | solution.py:178
  2.0 14.8 %all-to-all-start.4 = ((s32[64,1,128]{2,1,0:T(1,128)}), s32[64,1,128]{2,1,0:T(1,128)S(1)}, u32[]{:S(2)}, u32[]{:S(2)}) async-start(s32[64,1,128]{2,1,0:T(1,128)} %shard_map.59), calls=%async_computation.4 | async-start | bytes 65536 | tf_op jit(solution)/shard_map/all_to_all | solution.py:495
  16.9 1.5 %shard_map.60 = (bf16[2,48,1024]{2,1,0:T(8,128)(2,1)S(1)}, bf16[2,48,1024]{2,1,0:T(8,128)(2,1)S(1)}, bf16[2,48,1024]{2,1,0:T(8,128)(2,1)S(1)}, bf16[2,48,1024]{2...) custom-call(s32[1]{0:T(128)} %bitcast.3.section_ref, s32[1,128]{1,0:T(1,128)} %bitcast.10, ...), custom_call_target="tpu_custom_call" | custom-call | tf_op jit(solution)/shard_map/pallas_call | solution.py:178
  18.4 7.4 %all-to-all-done.4 = s32[64,1,128]{2,1,0:T(1,128)S(1)} async-done(((s32[64,1,128]{2,1,0:T(1,128)}), s32[64,1,128]{2,1,0:T(1,128)S(1)}, u32[]{:S(2)}, u32[]{:S(2)}) %all-to-all-start.4) | async-done | bytes 32800 | tf_op jit(solution)/shard_map/all_to_all | solution.py:495
  25.8 0.0 copy-start.4
  25.8 5.6 %shard_map.61 = (bf16[64,32,128]{2,1,0:T(8,128)(2,1)}, s32[40,128]{1,0:T(8,128)S(1)}) custom-call(s32[1]{0:T(128)} %bitcast.3.section_ref, s32[64,128]{1,0:T(8,128)S(1)} %bitcast.5, bf16[8192,128]{1,0:T(8,128)(2,1)} %table_ref.1), custom_call_target="tpu_custom_call" | custom-call | tf_op jit(solution)/shard_map/pallas_call | solution.py:178
  31.5 6.0 %all-to-all-start.5 = ((bf16[64,32,128]{2,1,0:T(8,128)(2,1)}), bf16[64,32,128]{2,1,0:T(8,128)(2,1)S(1)}, u32[]{:S(2)}, u32[]{:S(2)}) async-start(bf16[64,32,128]{2,1,0:T(8,128)(2,1)} %get-tuple-element.70), calls=%async_computation.5 | async-start | bytes 1048576 | tf_op jit(solution)/shard_map/all_to_all | solution.py:520
  37.5 4.5 %collective-permute-start = (bf16[2,48,1024]{2,1,0:T(8,128)(2,1)S(1)}, bf16[2,48,1024]{2,1,0:T(8,128)(2,1)S(1)}, u32[]{:S(2)}, u32[]{:S(2)}) collective-permute-start(bf16[2,48,1024]{2,1,0:T(8,128)(2,1)S(1)} %get-tuple-element.74), channel_id=1, source_target_pairs={{0,128},{128,0},{256,384},{384,256},{1,129},{129,1},{257,385},{385... | collective-permute-start | bytes 589832 | tf_op jit(solution)/shard_map/ppermute | solution.py:527
  42.0 4.8 %collective-permute-start.1 = (bf16[2,48,1024]{2,1,0:T(8,128)(2,1)S(1)}, bf16[2,48,1024]{2,1,0:T(8,128)(2,1)S(1)}, u32[]{:S(2)}, u32[]{:S(2)}) collective-permute-start(bf16[2,48,1024]{2,1,0:T(8,128)(2,1)S(1)} %get-tuple-element.75), channel_id=1, source_target_pairs={{0,256},{128,384},{256,0},{384,128},{1,257},{129,385},{257,1},{385... | collective-permute-start | bytes 589832 | tf_op jit(solution)/shard_map/ppermute | solution.py:527
  46.8 2.9 %collective-permute-start.2 = (bf16[2,48,1024]{2,1,0:T(8,128)(2,1)S(1)}, bf16[2,48,1024]{2,1,0:T(8,128)(2,1)S(1)}, u32[]{:S(2)}, u32[]{:S(2)}) collective-permute-start(bf16[2,48,1024]{2,1,0:T(8,128)(2,1)S(1)} %get-tuple-element.76), channel_id=1, source_target_pairs={{0,384},{128,256},{256,128},{384,0},{1,385},{129,257},{257,129},{3... | collective-permute-start | bytes 589832 | tf_op jit(solution)/shard_map/ppermute | solution.py:527
  49.7 0.0 collective-permute-done.refs_1_
  49.7 9.1 %collective-permute-done.1.refs_2_ = bf16[2,48,1024]{2,1,0:T(8,128)(2,1)S(1)} collective-permute-done((bf16[2,48,1024]{2,1,0:T(8,128)(2,1)S(1)}, bf16[2,48,1024]{2,1,0:T(8,128)(2,1)S(1)}, u32[]{:S(2)}, u32[]{:S(2)}) %collective-permute-start.1) | collective-permute-done | bytes 196640 | tf_op jit(solution)/shard_map/ppermute | solution.py:527
  58.9 4.8 %collective-permute-done.2.refs_3_ = bf16[2,48,1024]{2,1,0:T(8,128)(2,1)S(1)} collective-permute-done((bf16[2,48,1024]{2,1,0:T(8,128)(2,1)S(1)}, bf16[2,48,1024]{2,1,0:T(8,128)(2,1)S(1)}, u32[]{:S(2)}, u32[]{:S(2)}) %collective-permute-start.2) | collective-permute-done | bytes 196640 | tf_op jit(solution)/shard_map/ppermute | solution.py:527
  63.6 1.9 %collective-permute-start.3 = (bf16[4,48,1024]{2,1,0:T(8,128)(2,1)S(1)}, bf16[4,48,1024]{2,1,0:T(8,128)(2,1)S(1)}, u32[]{:S(2)}, u32[]{:S(2)}) collective-permute-start(bf16[4,48,1024]{2,1,0:T(8,128)(2,1)S(1)} %shard_map.62), channel_id=1, source_target_pairs={{0,64},{64,0},{1,65},{65,1},{2,66},{66,2},{3,67},{67,3},{4,68},{68... | collective-permute-start | bytes 1179656 | tf_op jit(solution)/shard_map/ppermute | solution.py:533
  65.6 0.0 copy-done.4
  65.6 1.7 %collective-permute-done.3.got_ref = bf16[4,48,1024]{2,1,0:T(8,128)(2,1)S(1)} collective-permute-done((bf16[4,48,1024]{2,1,0:T(8,128)(2,1)S(1)}, bf16[4,48,1024]{2,1,0:T(8,128)(2,1)S(1)}, u32[]{:S(2)}, u32[]{:S(2)}) %collective-permute-start.3) | collective-permute-done | bytes 393248 | tf_op jit(solution)/shard_map/ppermute | solution.py:533
  67.3 0.0 all-to-all-done.5.rows_ref
  67.3 0.0 copy-start.5
  67.3 1.9 %shard_map.63 = (bf16[64,32,128]{2,1,0:T(8,128)(2,1)}, bf16[2,48,1024]{2,1,0:T(8,128)(2,1)S(1)}, bf16[2,48,1024]{2,1,0:T(8,128)(2,1)S(1)}, bf16[2,48,1024]{2,1,0:T(8,128)(2,1)S(1)}, bf16[2,48,1024]{2,1,0:T(8,128)(2,1)S(1)}) custom-call(s32[1]{0:T(128)} %bitcast.3.section_ref, bf16[64,32,128]{2,1,0:T(8,128)(2,1)S(1)} %all-to-all-done.5.rows_ref, ...), custom_call_target="tpu_custom_call" | custom-call | tf_op jit(solution)/shard_map/pallas_call | solution.py:178
  69.1 0.0 copy-start.3
  69.1 12.8 %all-to-all-start.6 = ((bf16[64,32,128]{2,1,0:T(8,128)(2,1)}), bf16[64,32,128]{2,1,0:T(8,128)(2,1)S(1)}, u32[]{:S(2)}, u32[]{:S(2)}) async-start(bf16[64,32,128]{2,1,0:T(8,128)(2,1)} %get-tuple-element.77), calls=%async_computation.6 | async-start | bytes 1048576 | tf_op jit(solution)/shard_map/all_to_all | solution.py:544
  81.9 4.0 %collective-permute-start.4 = (bf16[2,48,1024]{2,1,0:T(8,128)(2,1)S(1)}, bf16[2,48,1024]{2,1,0:T(8,128)(2,1)S(1)}, u32[]{:S(2)}, u32[]{:S(2)}) collective-permute-start(bf16[2,48,1024]{2,1,0:T(8,128)(2,1)S(1)} %get-tuple-element.80), channel_id=1, source_target_pairs={{0,128},{128,0},{256,384},{384,256},{1,129},{129,1},{257,385},{385... | collective-permute-start | bytes 589832 | tf_op jit(solution)/shard_map/ppermute | solution.py:527
  85.9 4.4 %collective-permute-start.5 = (bf16[2,48,1024]{2,1,0:T(8,128)(2,1)S(1)}, bf16[2,48,1024]{2,1,0:T(8,128)(2,1)S(1)}, u32[]{:S(2)}, u32[]{:S(2)}) collective-permute-start(bf16[2,48,1024]{2,1,0:T(8,128)(2,1)S(1)} %get-tuple-element.81), channel_id=1, source_target_pairs={{0,256},{128,384},{256,0},{384,128},{1,257},{129,385},{257,1},{385... | collective-permute-start | bytes 589832 | tf_op jit(solution)/shard_map/ppermute | solution.py:527
  90.3 3.8 %collective-permute-start.6 = (bf16[2,48,1024]{2,1,0:T(8,128)(2,1)S(1)}, bf16[2,48,1024]{2,1,0:T(8,128)(2,1)S(1)}, u32[]{:S(2)}, u32[]{:S(2)}) collective-permute-start(bf16[2,48,1024]{2,1,0:T(8,128)(2,1)S(1)} %get-tuple-element.82), channel_id=1, source_target_pairs={{0,384},{128,256},{256,128},{384,0},{1,385},{129,257},{257,129},{3... | collective-permute-start | bytes 589832 | tf_op jit(solution)/shard_map/ppermute | solution.py:527
  94.2 9.6 %collective-permute-done.4.refs_1_ = bf16[2,48,1024]{2,1,0:T(8,128)(2,1)S(1)} collective-permute-done((bf16[2,48,1024]{2,1,0:T(8,128)(2,1)S(1)}, bf16[2,48,1024]{2,1,0:T(8,128)(2,1)S(1)}, u32[]{:S(2)}, u32[]{:S(2)}) %collective-permute-start.4) | collective-permute-done | bytes 196640 | tf_op jit(solution)/shard_map/ppermute | solution.py:527
  103.8 0.0 collective-permute-done.5.refs_2_
  103.8 5.3 %collective-permute-done.6.refs_3_ = bf16[2,48,1024]{2,1,0:T(8,128)(2,1)S(1)} collective-permute-done((bf16[2,48,1024]{2,1,0:T(8,128)(2,1)S(1)}, bf16[2,48,1024]{2,1,0:T(8,128)(2,1)S(1)}, u32[]{:S(2)}, u32[]{:S(2)}) %collective-permute-start.6) | collective-permute-done | bytes 196640 | tf_op jit(solution)/shard_map/ppermute | solution.py:527
  109.1 1.9 %collective-permute-start.7 = (bf16[4,48,1024]{2,1,0:T(8,128)(2,1)S(1)}, bf16[4,48,1024]{2,1,0:T(8,128)(2,1)S(1)}, u32[]{:S(2)}, u32[]{:S(2)}) collective-permute-start(bf16[4,48,1024]{2,1,0:T(8,128)(2,1)S(1)} %shard_map.64), channel_id=1, source_target_pairs={{0,64},{64,0},{1,65},{65,1},{2,66},{66,2},{3,67},{67,3},{4,68},{68... | collective-permute-start | bytes 1179656 | tf_op jit(solution)/shard_map/ppermute | solution.py:533
  111.1 2.2 %convert_reduce_fusion = (s32[64,8]{1,0:T(8,128)S(1)}, s32[64,8]{1,0:T(8,128)S(1)}) fusion(s32[64,128]{1,0:T(8,128)S(1)} %get-tuple-element.87, pred[64,128]{1,0:T(8,128)(4,1)S(1)} %broadcast_compare_fusion), kind=kLoop, calls=%fused_computation.1 | loop fusion | flops 392192 | bytes 45056 | tf_op jit(solution)/shard_map/reduce_sum | solution.py:500
  113.4 0.6 reduce_max.18
  114.0 0.7 reduce_max.19
  116.0 0.0 collective-permute-done.7.got_ref
  116.0 0.0 copy-done.5
  116.0 1.6 %shard_map.65.fast_ref = bf16[128,1024]{1,0:T(8,128)(2,1)} custom-call(s32[1]{0:T(128)} %bitcast.3.section_ref, s32[1,128]{1,0:T(1,128)S(1)} %bitcast.11, bf16[4,48,1024]{2,1,0:T(8,128)(2,1)S(1)} %collective-permute-done.7.got_ref, bf16[2,48,1024]{2,1,0:T(8,128)(2,1)S(1)} %get-tuple-element.79.refs_0_, ...), custom_call_target="tpu_custom_call" | custom-call | tf_op jit(solution)/shard_map/pallas_call | solution.py:178
  117.6 0.0 all-to-all-done.6
  117.6 0.0 copy-done.3
  117.6 6.3 %conditional.1 = (bf16[8192,128]{1,0:T(8,128)(2,1)}, bf16[128,1024]{1,0:T(8,128)(2,1)S(1)}) conditional(s32[]{:T(128)} %convert_element_type.12, (s32[64,128]{1,0:T(8,128)S(1)}, s32[64,128]{1,0:T(8,128)S(1)}, s32[1]{0:T(128)}, bf16[8192,128]{1,0:T(8,128)(2,1)}, s32[1,128]{1,0:T(1,128)S(1)}, /*index=5*/bf16[128,1024]{1,0:T(8,128)(2,1)S(1)}, ...), branch_computations={%region_4.5_spmd, %region_5.6_spmd} | conditional | flops 40960 | bytes 46235812 | solution.py:561
  117.6 6.2 %branch_1_fun.1 = bf16[8192,128]{1,0:T(8,128)(2,1)} custom-call(s32[40,128]{1,0:T(8,128)S(1)} %get-tuple-element.40.plan_ref, bf16[64,32,128]{2,1,0:T(8,128)(2,1)S(1)} %get-tuple-element.41.grads_ref), custom_call_target="tpu_custom_call" | custom-call | tf_op jit(solution)/shard_map/cond/branch_1_fun/pallas_call | solution.py:178
  (8 shorter events, 0.2 us)
Async XLA Ops:
  2.0 23.8 %all-to-all-start.4 = ((s32[64,1,128]{2,1,0:T(1,128)}), s32[64,1,128]{2,1,0:T(1,128)S(1)}, u32[]{:S(2)}, u32[]{:S(2)}) async-start(s32[64,1,128]{2,1,0:T(1,128)} %shard_map.59), calls=%async_computation.4 | async-start | bytes 65536 | tf_op jit(solution)/shard_map/all_to_all | solution.py:495
  25.8 39.8 %copy-start.4 = (f32[8192]{0:T(1024)S(1)}, f32[8192]{0:T(1024)}, u32[]{:S(2)}) copy-start(f32[8192]{0:T(1024)} %param.8) | copy-start | bytes 98308
  31.5 35.8 %all-to-all-start.5 = ((bf16[64,32,128]{2,1,0:T(8,128)(2,1)}), bf16[64,32,128]{2,1,0:T(8,128)(2,1)S(1)}, u32[]{:S(2)}, u32[]{:S(2)}) async-start(bf16[64,32,128]{2,1,0:T(8,128)(2,1)} %get-tuple-element.70), calls=%async_computation.5 | async-start | bytes 1048576 | tf_op jit(solution)/shard_map/all_to_all | solution.py:520
  37.5 12.2 %collective-permute-start = (bf16[2,48,1024]{2,1,0:T(8,128)(2,1)S(1)}, bf16[2,48,1024]{2,1,0:T(8,128)(2,1)S(1)}, u32[]{:S(2)}, u32[]{:S(2)}) collective-permute-start(bf16[2,48,1024]{2,1,0:T(8,128)(2,1)S(1)} %get-tuple-element.74), channel_id=1, source_target_pairs={{0,128},{128,0},{256,384},{384,256},{1,129},{129,1},{257,385},{385... | collective-permute-start | bytes 589832 | tf_op jit(solution)/shard_map/ppermute | solution.py:527
  42.0 16.9 %collective-permute-start.1 = (bf16[2,48,1024]{2,1,0:T(8,128)(2,1)S(1)}, bf16[2,48,1024]{2,1,0:T(8,128)(2,1)S(1)}, u32[]{:S(2)}, u32[]{:S(2)}) collective-permute-start(bf16[2,48,1024]{2,1,0:T(8,128)(2,1)S(1)} %get-tuple-element.75), channel_id=1, source_target_pairs={{0,256},{128,384},{256,0},{384,128},{1,257},{129,385},{257,1},{385... | collective-permute-start | bytes 589832 | tf_op jit(solution)/shard_map/ppermute | solution.py:527
  46.8 16.8 %collective-permute-start.2 = (bf16[2,48,1024]{2,1,0:T(8,128)(2,1)S(1)}, bf16[2,48,1024]{2,1,0:T(8,128)(2,1)S(1)}, u32[]{:S(2)}, u32[]{:S(2)}) collective-permute-start(bf16[2,48,1024]{2,1,0:T(8,128)(2,1)S(1)} %get-tuple-element.76), channel_id=1, source_target_pairs={{0,384},{128,256},{256,128},{384,0},{1,385},{129,257},{257,129},{3... | collective-permute-start | bytes 589832 | tf_op jit(solution)/shard_map/ppermute | solution.py:527
  63.6 3.6 %collective-permute-start.3 = (bf16[4,48,1024]{2,1,0:T(8,128)(2,1)S(1)}, bf16[4,48,1024]{2,1,0:T(8,128)(2,1)S(1)}, u32[]{:S(2)}, u32[]{:S(2)}) collective-permute-start(bf16[4,48,1024]{2,1,0:T(8,128)(2,1)S(1)} %shard_map.62), channel_id=1, source_target_pairs={{0,64},{64,0},{1,65},{65,1},{2,66},{66,2},{3,67},{67,3},{4,68},{68... | collective-permute-start | bytes 1179656 | tf_op jit(solution)/shard_map/ppermute | solution.py:533
  67.3 48.7 %copy-start.5 = (s32[128]{0:T(128)S(1)}, s32[128]{0:T(128)}, u32[]{:S(2)}) copy-start(s32[128]{0:T(128)} %param.6) | copy-start | bytes 1540
  69.1 48.5 %copy-start.3 = (bf16[128,1024]{1,0:T(8,128)(2,1)S(1)}, bf16[128,1024]{1,0:T(8,128)(2,1)}, u32[]{:S(2)}) copy-start(bf16[128,1024]{1,0:T(8,128)(2,1)} %cotangent_ref.1) | copy-start | bytes 786436
  69.1 48.5 %all-to-all-start.6 = ((bf16[64,32,128]{2,1,0:T(8,128)(2,1)}), bf16[64,32,128]{2,1,0:T(8,128)(2,1)S(1)}, u32[]{:S(2)}, u32[]{:S(2)}) async-start(bf16[64,32,128]{2,1,0:T(8,128)(2,1)} %get-tuple-element.77), calls=%async_computation.6 | async-start | bytes 1048576 | tf_op jit(solution)/shard_map/all_to_all | solution.py:544
  81.9 21.9 %collective-permute-start.4 = (bf16[2,48,1024]{2,1,0:T(8,128)(2,1)S(1)}, bf16[2,48,1024]{2,1,0:T(8,128)(2,1)S(1)}, u32[]{:S(2)}, u32[]{:S(2)}) collective-permute-start(bf16[2,48,1024]{2,1,0:T(8,128)(2,1)S(1)} %get-tuple-element.80), channel_id=1, source_target_pairs={{0,128},{128,0},{256,384},{384,256},{1,129},{129,1},{257,385},{385... | collective-permute-start | bytes 589832 | tf_op jit(solution)/shard_map/ppermute | solution.py:527
  85.9 17.9 %collective-permute-start.5 = (bf16[2,48,1024]{2,1,0:T(8,128)(2,1)S(1)}, bf16[2,48,1024]{2,1,0:T(8,128)(2,1)S(1)}, u32[]{:S(2)}, u32[]{:S(2)}) collective-permute-start(bf16[2,48,1024]{2,1,0:T(8,128)(2,1)S(1)} %get-tuple-element.81), channel_id=1, source_target_pairs={{0,256},{128,384},{256,0},{384,128},{1,257},{129,385},{257,1},{385... | collective-permute-start | bytes 589832 | tf_op jit(solution)/shard_map/ppermute | solution.py:527
  90.3 18.8 %collective-permute-start.6 = (bf16[2,48,1024]{2,1,0:T(8,128)(2,1)S(1)}, bf16[2,48,1024]{2,1,0:T(8,128)(2,1)S(1)}, u32[]{:S(2)}, u32[]{:S(2)}) collective-permute-start(bf16[2,48,1024]{2,1,0:T(8,128)(2,1)S(1)} %get-tuple-element.82), channel_id=1, source_target_pairs={{0,384},{128,256},{256,128},{384,0},{1,385},{129,257},{257,129},{3... | collective-permute-start | bytes 589832 | tf_op jit(solution)/shard_map/ppermute | solution.py:527
  109.1 6.8 %collective-permute-start.7 = (bf16[4,48,1024]{2,1,0:T(8,128)(2,1)S(1)}, bf16[4,48,1024]{2,1,0:T(8,128)(2,1)S(1)}, u32[]{:S(2)}, u32[]{:S(2)}) collective-permute-start(bf16[4,48,1024]{2,1,0:T(8,128)(2,1)S(1)} %shard_map.64), channel_id=1, source_target_pairs={{0,64},{64,0},{1,65},{65,1},{2,66},{66,2},{3,67},{67,3},{4,68},{68... | collective-permute-start | bytes 1179656 | tf_op jit(solution)/shard_map/ppermute | solution.py:533

commit v6 on v5

--- a/solution.py
+++ b/solution.py
@@ -10,9 +10,11 @@
 from jax.sharding import PartitionSpec as P
 
 epsilon = 1e-05
-TOKEN_SLOTS = 48
+TOKEN_SLOTS = 72
 ROW_SLOTS = 32
 CHUNK = 8
+FRONT_EARLY = 2
+BACK_EARLY = 2
 REPEATED = 1 << 16
 CHIPS = "section_0"
 CORES = "section_1"
@@ -357,10 +359,10 @@
     return jnp.where(condition, 1.0, 0.0).astype(jnp.bfloat16)
 
 
-def ranks(ids_row, vocab_section):
+def chip_ranks(ids_row, vocab_section):
     wide, tall, row_first, column_first = both_ways(ids_row)
-    wide = wide // vocab_section
-    tall = tall // vocab_section
+    wide = wide // (2 * vocab_section)
+    tall = tall // (2 * vocab_section)
     same = wide == tall
     as_row = jnp.sum(jnp.where(same & row_first, 1, 0), axis=0, keepdims=True)
     as_column = jnp.sum(jnp.where(same & column_first, 1.0, 0.0), axis=1, keepdims=True)
@@ -371,16 +373,14 @@
     *hand_refs, expand_ref, combine_ref = refs
     token_slots, row_slots = expand_ref.shape
     section = section_ref[0]
-    wide_section, wide_rank, _, _ = ranks(ids_ref[...], vocab_section)
+    wide_chip, wide_rank, _, _ = chip_ranks(ids_ref[...], vocab_section)
     slot = lax.broadcasted_iota(jnp.int32, (token_slots, LANES), 0)
     cotangent = cotangent_ref[...]
     for k, hand_ref in enumerate(hand_refs):
-        for c in range(2):
-            to = 2 * ((section // 2) ^ k) + c
-            wanted = one_hot((slot == wide_rank) & (wide_section == to))
-            hand_ref[c] = jnp.dot(
-                wanted, cotangent, preferred_element_type=jnp.float32
-            ).astype(jnp.bfloat16)
+        wanted = one_hot((slot == wide_rank) & (wide_chip == (section // 2) ^ k))
+        hand_ref[...] = jnp.dot(
+            wanted, cotangent, preferred_element_type=jnp.float32
+        ).astype(jnp.bfloat16)
 
     wide, tall, row_first, column_first = both_ways(ids_ref[...])
     wide_in = wide // vocab_section == section
@@ -390,7 +390,7 @@
     tall_repeat = jnp.max(jnp.where(same & column_first, 1.0, 0.0), axis=1, keepdims=True)
     wide_new = wide_in & (jnp.broadcast_to(wide_repeat, (LANES, LANES)) == 0)
     tall_new = tall_in & (jnp.broadcast_to(tall_repeat, (LANES, LANES)) == 0.0)
-    own = one_hot((slot == wide_rank) & (wide_section == section))
+    own = one_hot((slot == wide_rank) & wide_in[:1])
     tall_place = jnp.sum(jnp.where(wide_new & column_first, 1.0, 0.0), axis=1, keepdims=True)
     place = jnp.sum(
         jnp.where(same & tall_new, jnp.broadcast_to(tall_place, (LANES, LANES)), 0.0), axis=0, keepdims=True
@@ -406,32 +406,30 @@
     ).astype(jnp.bfloat16)
 
 
-def part_kernel(section_ref, *refs):
-    *hand_refs, give_ref = refs
-    for k, hand_ref in enumerate(hand_refs):
-        give_ref[k] = hand_ref[1 - section_ref[0] % 2]
-
-
-def grad_kernel(section_ref, rows_ref, gain_ref, expand_ref, combine_ref, got_ref, *refs, chips):
-    own_refs, by_column_ref, out_refs = refs[:chips], refs[chips], refs[chips + 1 : -1]
-    embedded_ref = refs[-1]
+def stack_kernel(*refs):
+    *part_refs, stack_ref = refs
+    for k, part_ref in enumerate(part_refs):
+        stack_ref[k] = part_ref[...]
+
+
+def grad_kernel(section_ref, rows_ref, gain_ref, expand_ref, got_ref, *refs):
+    *hand_refs, keep_ref, give_ref, embedded_ref = refs
     pieces, _, columns = rows_ref.shape
-    _, slots, features = got_ref.shape
+    chips, slots, features = got_ref.shape
     per = features // columns
     width = pieces * columns
     expand = expand_ref[...]
-    combine = combine_ref[...]
     section = section_ref[0]
     core = section % 2
     parts = []
     for k in range(chips):
         chip = (section // 2) ^ k
-        parts.append((k, 2 * chip + core, core, own_refs[k].at[core]))
-        parts.append((k, 2 * chip + 1 - core, 1 - core, got_ref.at[k]))
+        parts.append((2 * chip + core, hand_refs[k], keep_ref.at[k]))
+        parts.append((2 * chip + 1 - core, got_ref.at[k], give_ref.at[k]))
 
     squares = jnp.zeros((slots, columns), jnp.float32)
     inners = jnp.zeros((slots, columns), jnp.float32)
-    for i, (_, s, _, cotangent_ref) in enumerate(parts):
+    for i, (s, cotangent_ref, _) in enumerate(parts):
         rows = jnp.concatenate([rows_ref[s * per + j] for j in range(per)], axis=1)
         embedded = jnp.dot(expand, rows, preferred_element_type=jnp.float32)
         embedded_ref[i] = embedded.astype(jnp.bfloat16)
@@ -443,32 +441,44 @@
             inners = inners + inner[:, j * columns : (j + 1) * columns]
     square_mean = jnp.sum(squares, axis=1, keepdims=True) * (1.0 / width)
     inner = jnp.sum(inners, axis=1, keepdims=True) * (1.0 / width)
-    inverse = lax.rsqrt(square_mean + epsilon)
+    own = jnp.sum(expand.astype(jnp.float32), axis=1, keepdims=True)
+    inverse = jnp.where(own > 0.0, lax.rsqrt(square_mean + epsilon), 0.0)
     pull = inverse * inverse * inverse * inner
 
-    for i, (k, s, place, cotangent_ref) in enumerate(parts):
+    for i, (s, cotangent_ref, out_ref) in enumerate(parts):
         scaled = cotangent_ref[...].astype(jnp.float32) * gain_ref[pl.ds(s, 1), :]
-        grad = (inverse * scaled - embedded_ref[i].astype(jnp.float32) * pull).astype(jnp.bfloat16)
-        out_refs[k][place] = grad
-        added = jnp.dot(combine, grad, preferred_element_type=jnp.float32).astype(jnp.bfloat16)
-        for j in range(per):
-            by_column_ref[s * per + j] = added[:, j * columns : (j + 1) * columns]
-
-
-def gather_kernel(section_ref, ids_ref, got_ref, *refs, vocab_section):
-    *home_refs, own_ref = refs
-    slots = got_ref.shape[1]
-    _, _, tall_section, tall_rank = ranks(ids_ref[...], vocab_section)
-    along = lax.broadcasted_iota(jnp.int32, (LANES, slots), 1)
+        out_ref[...] = (inverse * scaled - embedded_ref[i].astype(jnp.float32) * pull).astype(jnp.bfloat16)
+
+
+def combine_kernel(section_ref, combine_ref, keep_ref, give_ref, by_column_ref):
+    columns = by_column_ref.shape[2]
+    chips, _, features = keep_ref.shape
+    per = features // columns
+    combine = combine_ref[...]
     section = section_ref[0]
     core = section % 2
+    for k in range(chips):
+        chip = (section // 2) ^ k
+        for s, grad_ref in ((2 * chip + core, keep_ref), (2 * chip + 1 - core, give_ref)):
+            added = jnp.dot(combine, grad_ref[k], preferred_element_type=jnp.float32).astype(jnp.bfloat16)
+            for j in range(per):
+                by_column_ref[s * per + j] = added[:, j * columns : (j + 1) * columns]
+
+
+def merge_kernel(keep_ref, got_ref, *out_refs):
+    for k, out_ref in enumerate(out_refs):
+        out_ref[...] = (keep_ref[k].astype(jnp.float32) + got_ref[k].astype(jnp.float32)).astype(jnp.bfloat16)
+
+
+def gather_kernel(section_ref, ids_ref, *refs, vocab_section):
+    *home_refs, own_ref = refs
+    slots = home_refs[0].shape[0]
+    _, _, tall_chip, tall_rank = chip_ranks(ids_ref[...], vocab_section)
+    along = lax.broadcasted_iota(jnp.int32, (LANES, slots), 1)
     total = jnp.zeros(own_ref.shape, jnp.float32)
     for k, home_ref in enumerate(home_refs):
-        chip = (section // 2) ^ k
-        mine = one_hot((along == tall_rank) & (tall_section == 2 * chip + core))
-        theirs = one_hot((along == tall_rank) & (tall_section == 2 * chip + 1 - core))
-        total = total + jnp.dot(mine, home_ref[core], preferred_element_type=jnp.float32)
-        total = total + jnp.dot(theirs, got_ref[k], preferred_element_type=jnp.float32)
+        wanted = one_hot((along == tall_rank) & (tall_chip == (section_ref[0] // 2) ^ k))
+        total = total + jnp.dot(wanted, home_ref[...], preferred_element_type=jnp.float32)
     own_ref[...] = total.astype(jnp.bfloat16)
 
 
@@ -492,23 +502,35 @@
     section = lax.axis_index(SECTION).reshape(1)
     own_ids = token_ids.reshape(1, tokens)
     (marked,) = call(mark_kernel, (own_ids,), (V,), [i32((groups, 1, tokens))])
-    marked = lax.all_to_all(marked, "dp", 0, 0, tiled=True).reshape(groups, tokens)
-    all_ids = marked % REPEATED
-    in_section = all_ids[:, :, None] // vocab_section == jnp.arange(sections)
-    new_in_section = in_section & (marked < REPEATED)[:, :, None]
-    fits = (jnp.max(jnp.sum(in_section, axis=1)) <= TOKEN_SLOTS) & (
-        jnp.max(jnp.sum(new_in_section, axis=1)) <= ROW_SLOTS
-    )
-
-    wide_shape = (vocab_section + CHUNK, columns)
-    wide_slots = f32((ROW_SLOTS, columns), jnp.float32)
+    marked = lax.all_to_all(marked, "dp", 0, 0, tiled=True)
+    chips = sections // 2
+    part = bf16((TOKEN_SLOTS, features))
+    parts = bf16((chips, TOKEN_SLOTS, features))
+
+    def to_chip(k, array):
+        return lax.ppermute(array, CHIPS, [(i, i ^ k) for i in range(chips)])
+
+    def to_sibling(array):
+        return lax.ppermute(array, CORES, [(0, 1), (1, 0)])
+
     *hands, expand, combine = call(
         functools.partial(hand_kernel, vocab_section=vocab_section),
         (section, own_ids, cotangent), (S, V, V),
-        [bf16((2, TOKEN_SLOTS, features))] * (sections // 2)
-        + [bf16((TOKEN_SLOTS, ROW_SLOTS)), bf16((ROW_SLOTS, TOKEN_SLOTS))],
-    )
-    hands, marked = lax.optimization_barrier((hands, marked))
+        [part] * chips + [bf16((TOKEN_SLOTS, ROW_SLOTS)), bf16((ROW_SLOTS, TOKEN_SLOTS))],
+    )
+    handed = hands[:1] + [to_chip(k, hands[k]) for k in range(1, chips)]
+    marked, handed[:FRONT_EARLY] = lax.optimization_barrier((marked, handed[:FRONT_EARLY]))
+    marked = marked.reshape(groups, tokens)
+    all_ids = marked % REPEATED
+    in_chip = all_ids[:, :, None] // (2 * vocab_section) == jnp.arange(chips)
+    in_section = all_ids[:, :, None] // vocab_section == jnp.arange(sections)
+    new_in_section = in_section & (marked < REPEATED)[:, :, None]
+    fits = (jnp.max(jnp.sum(in_chip, axis=1)) <= TOKEN_SLOTS) & (
+        jnp.max(jnp.sum(new_in_section, axis=1)) <= ROW_SLOTS
+    )
+
+    wide_shape = (vocab_section + CHUNK, columns)
+    wide_slots = f32((ROW_SLOTS, columns), jnp.float32)
     plan_shape = (ROW_SLOTS + CHUNK, LANES)
     rows, plan = call(
         functools.partial(row_pick_kernel, vocab_section=vocab_section),
@@ -518,34 +540,24 @@
         [pltpu.SMEM(plan_shape, jnp.int32), pltpu.SemaphoreType.DMA((4,)), pltpu.SemaphoreType.DMA],
     )
     full_rows = lax.all_to_all(rows, "dp", 0, 0, tiled=True)
-    chips = sections // 2
-    both = bf16((2, TOKEN_SLOTS, features))
-    one = bf16((chips, TOKEN_SLOTS, features))
-
-    def between_chips(arrays):
-        return arrays[:1] + [
-            lax.ppermute(a, CHIPS, [(i, i ^ k) for i in range(chips)])
-            for k, a in enumerate(arrays[1:], 1)
-        ]
-
-    def from_sibling(arrays):
-        (give,) = call(part_kernel, (section, *arrays), (S,) + (V,) * chips, [one])
-        return lax.ppermute(give, CORES, [(0, 1), (1, 0)])
-
-    handed = between_chips(hands)
-    got = from_sibling(handed)
-    by_column, *outs = call(
-        functools.partial(grad_kernel, chips=chips),
-        (section, full_rows, norm_gain.reshape(sections, features), expand, combine, got, *handed),
-        (S,) + (V,) * (5 + chips), [bf16(full_rows.shape)] + [both] * chips,
+    (stack,) = call(stack_kernel, tuple(handed), (V,) * chips, [parts])
+    got = to_sibling(stack)
+    keep, give = call(
+        grad_kernel,
+        (section, full_rows, norm_gain.reshape(sections, features), expand, got, *handed),
+        (S,) + (V,) * (4 + chips), [parts, parts],
         [f32((sections, TOKEN_SLOTS, features), jnp.bfloat16)],
     )
-    home = between_chips(outs)
+    (by_column,) = call(
+        combine_kernel, (section, combine, keep, give), (S, V, V, V), [bf16(full_rows.shape)]
+    )
+    outs = call(merge_kernel, (keep, to_sibling(give)), (V, V), [part] * chips)
+    home = [outs[0]] + [to_chip(k, outs[k]) for k in range(1, chips)]
+    by_column, home[:BACK_EARLY] = lax.optimization_barrier((by_column, home[:BACK_EARLY]))
     back = lax.all_to_all(by_column, "dp", 0, 0, tiled=True)
-    home_got = from_sibling(home)
     (fast_grad,) = call(
         functools.partial(gather_kernel, vocab_section=vocab_section),
-        (section, own_ids, home_got, *home), (S,) + (V,) * (2 + chips), [bf16((tokens, features))],
+        (section, own_ids, *home), (S,) + (V,) * (1 + chips), [bf16((tokens, features))],
     )
 
     def fast(plan, back, *_):

time: 126 us -> 122 us (0.968)
  the two profiles are of different devices: /device:TPU:6 before, /device:TPU:9 now
where the time goes in v6:
time: 122 us; the launch traced here: 121 us
  starting transfers between devices  45.5 us (37%)
  waiting for transfers between devices  29.7 us (24%)
  blocking collectives  22.6 us (19%)
  Pallas kernels  18.7 us (15%)
  other arithmetic  2.65 us (2%)
  between operations  2.03 us (2%)
    ppermute x6, waiting for transfers between devices, to_chip(): return lax.ppermute(array, CHIPS, [(i, i ^ k) for i in range(chips)])  26.5 us
    all_to_all x1, blocking collectives, on_device(): marked = lax.all_to_all(marked, 'dp', 0, 0, tiled=True)  22.6 us
    ppermute x6, starting transfers between devices, to_chip(): return lax.ppermute(array, CHIPS, [(i, i ^ k) for i in range(chips)])  21.5 us
    pallas_call x9, Pallas kernels, call(): pl.pallas_call(kernel, in_specs=[whole(o.shape, s) for o, s in zip(operan...  18.7 us
    all_to_all x1, starting transfers between devices, on_device(): back = lax.all_to_all(by_column, 'dp', 0, 0, tiled=True)  13 us
    all_to_all x1, starting transfers between devices, on_device(): full_rows = lax.all_to_all(rows, 'dp', 0, 0, tiled=True)  5.51 us
    ppermute x2, starting transfers between devices, to_sibling(): return lax.ppermute(array, CORES, [(0, 1), (1, 0)])  5.45 us
    ppermute x2, waiting for transfers between devices, to_sibling(): return lax.ppermute(array, CORES, [(0, 1), (1, 0)])  3.19 us
  transfers between devices with their start and end apart: 10, of which 7 were waited for; matrix products, arithmetic and copies ran while one was open for 2% of the time, Pallas kernels for 3%

profile of v6, /device:TPU:9, one launch (start us, length us, event | category | flops | bytes accessed | tf_op | source)
XLA Modules:
  0.0 121.2 jit_solution(9136321972152900629)
XLA Ops:
  0.6 1.5 %shard_map.60 = (bf16[72,1024]{1,0:T(8,128)(2,1)S(1)}, bf16[72,1024]{1,0:T(8,128)(2,1)S(1)}, bf16[72,1024]{1,0:T(8,128)(2,1)S(1)}, bf16[72,1024]{1,0:T(8,128)(2,...) custom-call(s32[1]{0:T(128)} %bitcast.2.section_ref, s32[1,128]{1,0:T(1,128)} %bitcast.9, ...), custom_call_target="tpu_custom_call" | custom-call | tf_op jit(solution)/shard_map/pallas_call | solution.py:180
  2.1 4.2 %collective-permute-start = (bf16[72,1024]{1,0:T(8,128)(2,1)S(1)}, bf16[72,1024]{1,0:T(8,128)(2,1)S(1)}, u32[]{:S(2)}, u32[]{:S(2)}) collective-permute-start(bf16[72,1024]{1,0:T(8,128)(2,1)S(1)} %get-tuple-element.67), channel_id=1, source_target_pairs={{0,128},{128,0},{256,384},{384,256},{1,129},{129,1},{257,385},{385... | collective-permute-start | bytes 442376 | tf_op jit(solution)/shard_map/ppermute | solution.py:511
  6.3 0.8 shard_map.59
  7.1 22.6 %all_to_all.33 = s32[64,1,128]{2,1,0:T(1,128)S(1)} all-to-all(s32[64,1,128]{2,1,0:T(1,128)S(1)} %shard_map.59), channel_id=1, replica_groups=mesh['section_0'=4,'section_1'=2,'dp'=64] {'dp'}, dimensions={0} | all-to-all | bytes 65536 | tf_op jit(solution)/shard_map/all_to_all | solution.py:505
  29.7 0.0 collective-permute-done.refs_1_
  29.7 0.0 copy-start.4
  29.7 6.0 %shard_map.61 = (bf16[64,32,128]{2,1,0:T(8,128)(2,1)}, s32[40,128]{1,0:T(8,128)S(1)}) custom-call(s32[1]{0:T(128)} %bitcast.2.section_ref, s32[64,128]{1,0:T(8,128)S(1)} %bitcast.5, bf16[8192,128]{1,0:T(8,128)(2,1)} %table_ref.1), custom_call_target="tpu_custom_call" | custom-call | tf_op jit(solution)/shard_map/pallas_call | solution.py:180
  35.7 5.5 %all-to-all-start.5 = ((bf16[64,32,128]{2,1,0:T(8,128)(2,1)}), bf16[64,32,128]{2,1,0:T(8,128)(2,1)S(1)}, u32[]{:S(2)}, u32[]{:S(2)}) async-start(bf16[64,32,128]{2,1,0:T(8,128)(2,1)} %get-tuple-element.71), calls=%async_computation.5 | async-start | bytes 1048576 | tf_op jit(solution)/shard_map/all_to_all | solution.py:542
  41.3 4.3 %collective-permute-start.1 = (bf16[72,1024]{1,0:T(8,128)(2,1)S(1)}, bf16[72,1024]{1,0:T(8,128)(2,1)S(1)}, u32[]{:S(2)}, u32[]{:S(2)}) collective-permute-start(bf16[72,1024]{1,0:T(8,128)(2,1)S(1)} %get-tuple-element.75), channel_id=1, source_target_pairs={{0,256},{128,384},{256,0},{384,128},{1,257},{129,385},{257,1},{385... | collective-permute-start | bytes 442376 | tf_op jit(solution)/shard_map/ppermute | solution.py:511
  45.6 2.4 %collective-permute-start.2 = (bf16[72,1024]{1,0:T(8,128)(2,1)S(1)}, bf16[72,1024]{1,0:T(8,128)(2,1)S(1)}, u32[]{:S(2)}, u32[]{:S(2)}) collective-permute-start(bf16[72,1024]{1,0:T(8,128)(2,1)S(1)} %get-tuple-element.76), channel_id=1, source_target_pairs={{0,384},{128,256},{256,128},{384,0},{1,385},{129,257},{257,129},{3... | collective-permute-start | bytes 442376 | tf_op jit(solution)/shard_map/ppermute | solution.py:511
  48.0 6.1 %collective-permute-done.1.refs_2_ = bf16[72,1024]{1,0:T(8,128)(2,1)S(1)} collective-permute-done((bf16[72,1024]{1,0:T(8,128)(2,1)S(1)}, bf16[72,1024]{1,0:T(8,128)(2,1)S(1)}, u32[]{:S(2)}, u32[]{:S(2)}) %collective-permute-start.1) | collective-permute-done | bytes 147488 | tf_op jit(solution)/shard_map/ppermute | solution.py:511
  54.1 6.9 %collective-permute-done.2.refs_3_ = bf16[72,1024]{1,0:T(8,128)(2,1)S(1)} collective-permute-done((bf16[72,1024]{1,0:T(8,128)(2,1)S(1)}, bf16[72,1024]{1,0:T(8,128)(2,1)S(1)}, u32[]{:S(2)}, u32[]{:S(2)}) %collective-permute-start.2) | collective-permute-done | bytes 147488 | tf_op jit(solution)/shard_map/ppermute | solution.py:511
  61.1 3.2 %collective-permute-start.3 = (bf16[4,72,1024]{2,1,0:T(8,128)(2,1)S(1)}, bf16[4,72,1024]{2,1,0:T(8,128)(2,1)S(1)}, u32[]{:S(2)}, u32[]{:S(2)}) collective-permute-start(bf16[4,72,1024]{2,1,0:T(8,128)(2,1)S(1)} %shard_map.62), channel_id=1, source_target_pairs={{0,64},{64,0},{1,65},{65,1},{2,66},{66,2},{3,67},{67,3},{4,68},{68... | collective-permute-start | bytes 1769480 | tf_op jit(solution)/shard_map/ppermute | solution.py:514
  64.3 0.0 copy-done.4
  64.3 1.6 %collective-permute-done.3.got_ref = bf16[4,72,1024]{2,1,0:T(8,128)(2,1)S(1)} collective-permute-done((bf16[4,72,1024]{2,1,0:T(8,128)(2,1)S(1)}, bf16[4,72,1024]{2,1,0:T(8,128)(2,1)S(1)}, u32[]{:S(2)}, u32[]{:S(2)}) %collective-permute-start.3) | collective-permute-done | bytes 589856 | tf_op jit(solution)/shard_map/ppermute | solution.py:514
  65.9 0.0 all-to-all-done.5.rows_ref
  65.9 1.2 shard_map.63
  67.1 2.3 %collective-permute-start.4 = (bf16[4,72,1024]{2,1,0:T(8,128)(2,1)S(1)}, bf16[4,72,1024]{2,1,0:T(8,128)(2,1)S(1)}, u32[]{:S(2)}, u32[]{:S(2)}) collective-permute-start(bf16[4,72,1024]{2,1,0:T(8,128)(2,1)S(1)} %get-tuple-element.78.give_ref), channel_id=1, source_target_pairs={{0,64},{64,0},{1,65},{65,1},{2,66},{66,2},{3,67},{67,3},{4,68},{68... | collective-permute-start | bytes 1769480 | tf_op jit(solution)/shard_map/ppermute | solution.py:514
  69.4 1.6 %collective-permute-done.4.got_ref = bf16[4,72,1024]{2,1,0:T(8,128)(2,1)S(1)} collective-permute-done((bf16[4,72,1024]{2,1,0:T(8,128)(2,1)S(1)}, bf16[4,72,1024]{2,1,0:T(8,128)(2,1)S(1)}, u32[]{:S(2)}, u32[]{:S(2)}) %collective-permute-start.4) | collective-permute-done | bytes 589856 | tf_op jit(solution)/shard_map/ppermute | solution.py:514
  71.0 0.0 copy-start.5
  71.0 0.2 shard_map.65
  71.2 0.0 copy-start.3
  71.2 2.1 %collective-permute-start.5 = (bf16[72,1024]{1,0:T(8,128)(2,1)S(1)}, bf16[72,1024]{1,0:T(8,128)(2,1)S(1)}, u32[]{:S(2)}, u32[]{:S(2)}) collective-permute-start(bf16[72,1024]{1,0:T(8,128)(2,1)S(1)} %get-tuple-element.80), channel_id=1, source_target_pairs={{0,128},{128,0},{256,384},{384,256},{1,129},{129,1},{257,385},{385... | collective-permute-start | bytes 442376 | tf_op jit(solution)/shard_map/ppermute | solution.py:511
  73.2 1.1 shard_map.64
  74.4 4.9 %collective-permute-done.5.refs_1_ = bf16[72,1024]{1,0:T(8,128)(2,1)S(1)} collective-permute-done((bf16[72,1024]{1,0:T(8,128)(2,1)S(1)}, bf16[72,1024]{1,0:T(8,128)(2,1)S(1)}, u32[]{:S(2)}, u32[]{:S(2)}) %collective-permute-start.5) | collective-permute-done | bytes 147488 | tf_op jit(solution)/shard_map/ppermute | solution.py:511
  79.2 13.0 %all-to-all-start.6 = ((bf16[64,32,128]{2,1,0:T(8,128)(2,1)}), bf16[64,32,128]{2,1,0:T(8,128)(2,1)S(1)}, u32[]{:S(2)}, u32[]{:S(2)}) async-start(bf16[64,32,128]{2,1,0:T(8,128)(2,1)} %shard_map.64), calls=%async_computation.6 | async-start | bytes 1048576 | tf_op jit(solution)/shard_map/all_to_all | solution.py:557
  92.3 0.1 negate_select_fusion.5
  92.3 4.6 %collective-permute-start.6 = (bf16[72,1024]{1,0:T(8,128)(2,1)S(1)}, bf16[72,1024]{1,0:T(8,128)(2,1)S(1)}, u32[]{:S(2)}, u32[]{:S(2)}) collective-permute-start(bf16[72,1024]{1,0:T(8,128)(2,1)S(1)} %get-tuple-element.85), channel_id=1, source_target_pairs={{0,256},{128,384},{256,0},{384,128},{1,257},{129,385},{257,1},{385... | collective-permute-start | bytes 442376 | tf_op jit(solution)/shard_map/ppermute | solution.py:511
  96.9 3.9 %collective-permute-start.7 = (bf16[72,1024]{1,0:T(8,128)(2,1)S(1)}, bf16[72,1024]{1,0:T(8,128)(2,1)S(1)}, u32[]{:S(2)}, u32[]{:S(2)}) collective-permute-start(bf16[72,1024]{1,0:T(8,128)(2,1)S(1)} %get-tuple-element.86), channel_id=1, source_target_pairs={{0,384},{128,256},{256,128},{384,0},{1,385},{129,257},{257,129},{3... | collective-permute-start | bytes 442376 | tf_op jit(solution)/shard_map/ppermute | solution.py:511
  100.8 0.1 convert_reduce_fusion.1
  101.0 0.6 reduce_max.18
  101.6 1.2 convert_reduce_fusion
  102.8 0.6 reduce_max.19
  104.6 0.4 collective-permute-done.6.refs_2_
  105.0 8.2 %collective-permute-done.7.refs_3_ = bf16[72,1024]{1,0:T(8,128)(2,1)S(1)} collective-permute-done((bf16[72,1024]{1,0:T(8,128)(2,1)S(1)}, bf16[72,1024]{1,0:T(8,128)(2,1)S(1)}, u32[]{:S(2)}, u32[]{:S(2)}) %collective-permute-start.7) | collective-permute-done | bytes 147488 | tf_op jit(solution)/shard_map/ppermute | solution.py:511
  113.2 0.0 copy-done.5
  113.2 1.3 %shard_map.66.fast_ref = bf16[128,1024]{1,0:T(8,128)(2,1)} custom-call(s32[1]{0:T(128)} %bitcast.2.section_ref, s32[1,128]{1,0:T(1,128)S(1)} %bitcast.11, bf16[72,1024]{1,0:T(8,128)(2,1)S(1)} %get-tuple-element.83.refs_0_, bf16[72,1024]{1,0:T(8,128)(2,1)S(1)} %collective-permute-done.5.refs_1_, bf16[72,1024]{1,0:T(8,128)(2,1)S(1)} %collective-permute-done.6.refs_2_, ...), custom_call_target="tpu_custom_call" | custom-call | tf_op jit(solution)/shard_map/pallas_call | solution.py:180
  114.5 0.0 all-to-all-done.6
  114.5 0.0 copy-done.3
  114.5 6.7 %conditional.1 = (bf16[8192,128]{1,0:T(8,128)(2,1)}, bf16[128,1024]{1,0:T(8,128)(2,1)S(1)}) conditional(s32[]{:T(128)} %convert_element_type.12, (s32[64,128]{1,0:T(8,128)S(1)}, s32[64,128]{1,0:T(8,128)S(1)}, s32[1]{0:T(128)}, bf16[8192,128]{1,0:T(8,128)(2,1)}, s32[1,128]{1,0:T(1,128)S(1)}, /*index=5*/bf16[128,1024]{1,0:T(8,128)(2,1)S(1)}, ...), branch_computations={%region_4.5_spmd, %region_5.6_spmd} | conditional | flops 40960 | bytes 46235812 | solution.py:573
  114.5 6.6 %branch_1_fun.1 = bf16[8192,128]{1,0:T(8,128)(2,1)} custom-call(s32[40,128]{1,0:T(8,128)S(1)} %get-tuple-element.40.plan_ref, bf16[64,32,128]{2,1,0:T(8,128)(2,1)S(1)} %get-tuple-element.41.grads_ref), custom_call_target="tpu_custom_call" | custom-call | tf_op jit(solution)/shard_map/cond/branch_1_fun/pallas_call | solution.py:180
  (6 shorter events, 0.1 us)
Async XLA Ops:
  2.1 27.6 %collective-permute-start = (bf16[72,1024]{1,0:T(8,128)(2,1)S(1)}, bf16[72,1024]{1,0:T(8,128)(2,1)S(1)}, u32[]{:S(2)}, u32[]{:S(2)}) collective-permute-start(bf16[72,1024]{1,0:T(8,128)(2,1)S(1)} %get-tuple-element.67), channel_id=1, source_target_pairs={{0,128},{128,0},{256,384},{384,256},{1,129},{129,1},{257,385},{385... | collective-permute-start | bytes 442376 | tf_op jit(solution)/shard_map/ppermute | solution.py:511
  29.7 34.5 %copy-start.4 = (f32[8192]{0:T(1024)S(1)}, f32[8192]{0:T(1024)}, u32[]{:S(2)}) copy-start(f32[8192]{0:T(1024)} %param.8) | copy-start | bytes 98308
  35.7 30.1 %all-to-all-start.5 = ((bf16[64,32,128]{2,1,0:T(8,128)(2,1)}), bf16[64,32,128]{2,1,0:T(8,128)(2,1)S(1)}, u32[]{:S(2)}, u32[]{:S(2)}) async-start(bf16[64,32,128]{2,1,0:T(8,128)(2,1)} %get-tuple-element.71), calls=%async_computation.5 | async-start | bytes 1048576 | tf_op jit(solution)/shard_map/all_to_all | solution.py:542
  41.3 12.9 %collective-permute-start.1 = (bf16[72,1024]{1,0:T(8,128)(2,1)S(1)}, bf16[72,1024]{1,0:T(8,128)(2,1)S(1)}, u32[]{:S(2)}, u32[]{:S(2)}) collective-permute-start(bf16[72,1024]{1,0:T(8,128)(2,1)S(1)} %get-tuple-element.75), channel_id=1, source_target_pairs={{0,256},{128,384},{256,0},{384,128},{1,257},{129,385},{257,1},{385... | collective-permute-start | bytes 442376 | tf_op jit(solution)/shard_map/ppermute | solution.py:511
  45.6 15.5 %collective-permute-start.2 = (bf16[72,1024]{1,0:T(8,128)(2,1)S(1)}, bf16[72,1024]{1,0:T(8,128)(2,1)S(1)}, u32[]{:S(2)}, u32[]{:S(2)}) collective-permute-start(bf16[72,1024]{1,0:T(8,128)(2,1)S(1)} %get-tuple-element.76), channel_id=1, source_target_pairs={{0,384},{128,256},{256,128},{384,0},{1,385},{129,257},{257,129},{3... | collective-permute-start | bytes 442376 | tf_op jit(solution)/shard_map/ppermute | solution.py:511
  61.1 4.8 %collective-permute-start.3 = (bf16[4,72,1024]{2,1,0:T(8,128)(2,1)S(1)}, bf16[4,72,1024]{2,1,0:T(8,128)(2,1)S(1)}, u32[]{:S(2)}, u32[]{:S(2)}) collective-permute-start(bf16[4,72,1024]{2,1,0:T(8,128)(2,1)S(1)} %shard_map.62), channel_id=1, source_target_pairs={{0,64},{64,0},{1,65},{65,1},{2,66},{66,2},{3,67},{67,3},{4,68},{68... | collective-permute-start | bytes 1769480 | tf_op jit(solution)/shard_map/ppermute | solution.py:514
  67.1 3.9 %collective-permute-start.4 = (bf16[4,72,1024]{2,1,0:T(8,128)(2,1)S(1)}, bf16[4,72,1024]{2,1,0:T(8,128)(2,1)S(1)}, u32[]{:S(2)}, u32[]{:S(2)}) collective-permute-start(bf16[4,72,1024]{2,1,0:T(8,128)(2,1)S(1)} %get-tuple-element.78.give_ref), channel_id=1, source_target_pairs={{0,64},{64,0},{1,65},{65,1},{2,66},{66,2},{3,67},{67,3},{4,68},{68... | collective-permute-start | bytes 1769480 | tf_op jit(solution)/shard_map/ppermute | solution.py:514
  71.0 42.2 %copy-start.5 = (s32[128]{0:T(128)S(1)}, s32[128]{0:T(128)}, u32[]{:S(2)}) copy-start(s32[128]{0:T(128)} %param.6) | copy-start | bytes 1540
  71.2 43.4 %copy-start.3 = (bf16[128,1024]{1,0:T(8,128)(2,1)S(1)}, bf16[128,1024]{1,0:T(8,128)(2,1)}, u32[]{:S(2)}) copy-start(bf16[128,1024]{1,0:T(8,128)(2,1)} %cotangent_ref.1) | copy-start | bytes 786436
  71.2 8.0 %collective-permute-start.5 = (bf16[72,1024]{1,0:T(8,128)(2,1)S(1)}, bf16[72,1024]{1,0:T(8,128)(2,1)S(1)}, u32[]{:S(2)}, u32[]{:S(2)}) collective-permute-start(bf16[72,1024]{1,0:T(8,128)(2,1)S(1)} %get-tuple-element.80), channel_id=1, source_target_pairs={{0,128},{128,0},{256,384},{384,256},{1,129},{129,1},{257,385},{385... | collective-permute-start | bytes 442376 | tf_op jit(solution)/shard_map/ppermute | solution.py:511
  79.2 35.3 %all-to-all-start.6 = ((bf16[64,32,128]{2,1,0:T(8,128)(2,1)}), bf16[64,32,128]{2,1,0:T(8,128)(2,1)S(1)}, u32[]{:S(2)}, u32[]{:S(2)}) async-start(bf16[64,32,128]{2,1,0:T(8,128)(2,1)} %shard_map.64), calls=%async_computation.6 | async-start | bytes 1048576 | tf_op jit(solution)/shard_map/all_to_all | solution.py:557
  92.3 12.7 %collective-permute-start.6 = (bf16[72,1024]{1,0:T(8,128)(2,1)S(1)}, bf16[72,1024]{1,0:T(8,128)(2,1)S(1)}, u32[]{:S(2)}, u32[]{:S(2)}) collective-permute-start(bf16[72,1024]{1,0:T(8,128)(2,1)S(1)} %get-tuple-element.85), channel_id=1, source_target_pairs={{0,256},{128,384},{256,0},{384,128},{1,257},{129,385},{257,1},{385... | collective-permute-start | bytes 442376 | tf_op jit(solution)/shard_map/ppermute | solution.py:511
  96.9 16.3 %collective-permute-start.7 = (bf16[72,1024]{1,0:T(8,128)(2,1)S(1)}, bf16[72,1024]{1,0:T(8,128)(2,1)S(1)}, u32[]{:S(2)}, u32[]{:S(2)}) collective-permute-start(bf16[72,1024]{1,0:T(8,128)(2,1)S(1)} %get-tuple-element.86), channel_id=1, source_target_pairs={{0,384},{128,256},{256,128},{384,0},{1,385},{129,257},{257,129},{3... | collective-permute-start | bytes 442376 | tf_op jit(solution)/shard_map/ppermute | solution.py:511

commit v7 on v6

--- a/solution.py
+++ b/solution.py
@@ -13,8 +13,8 @@
 TOKEN_SLOTS = 72
 ROW_SLOTS = 32
 CHUNK = 8
-FRONT_EARLY = 2
-BACK_EARLY = 2
+FAR_FIRST = (2, 1, 3)
+EARLY = 2
 REPEATED = 1 << 16
 CHIPS = "section_0"
 CORES = "section_1"
@@ -490,6 +490,10 @@
         copy.wait()
 
 
+def in_order(own, travelled):
+    return [own[0]] + [travelled[FAR_FIRST.index(k)] for k in range(1, len(own))]
+
+
 def on_device(token_ids, embed_table, norm_gain, cotangent):
     vocab_section, columns = embed_table.shape
     groups = lax.axis_size("dp")
@@ -518,8 +522,9 @@
         (section, own_ids, cotangent), (S, V, V),
         [part] * chips + [bf16((TOKEN_SLOTS, ROW_SLOTS)), bf16((ROW_SLOTS, TOKEN_SLOTS))],
     )
-    handed = hands[:1] + [to_chip(k, hands[k]) for k in range(1, chips)]
-    marked, handed[:FRONT_EARLY] = lax.optimization_barrier((marked, handed[:FRONT_EARLY]))
+    handed = [to_chip(k, hands[k]) for k in FAR_FIRST]
+    marked, handed[:EARLY] = lax.optimization_barrier((marked, handed[:EARLY]))
+    handed = in_order(hands, handed)
     marked = marked.reshape(groups, tokens)
     all_ids = marked % REPEATED
     in_chip = all_ids[:, :, None] // (2 * vocab_section) == jnp.arange(chips)
@@ -540,6 +545,7 @@
         [pltpu.SMEM(plan_shape, jnp.int32), pltpu.SemaphoreType.DMA((4,)), pltpu.SemaphoreType.DMA],
     )
     full_rows = lax.all_to_all(rows, "dp", 0, 0, tiled=True)
+    fits, full_rows = lax.optimization_barrier((fits, full_rows))
     (stack,) = call(stack_kernel, tuple(handed), (V,) * chips, [parts])
     got = to_sibling(stack)
     keep, give = call(
@@ -552,13 +558,9 @@
         combine_kernel, (section, combine, keep, give), (S, V, V, V), [bf16(full_rows.shape)]
     )
     outs = call(merge_kernel, (keep, to_sibling(give)), (V, V), [part] * chips)
-    home = [outs[0]] + [to_chip(k, outs[k]) for k in range(1, chips)]
-    by_column, home[:BACK_EARLY] = lax.optimization_barrier((by_column, home[:BACK_EARLY]))
+    by_column, outs = lax.optimization_barrier((by_column, list(outs)))
+    home = [to_chip(k, outs[k]) for k in FAR_FIRST]
     back = lax.all_to_all(by_column, "dp", 0, 0, tiled=True)
-    (fast_grad,) = call(
-        functools.partial(gather_kernel, vocab_section=vocab_section),
-        (section, own_ids, *home), (S,) + (V,) * (1 + chips), [bf16((tokens, features))],
-    )
 
     def fast(plan, back, *_):
         (grad_table,) = call(
@@ -573,6 +575,11 @@
     grad_table, slow_grad = lax.cond(
         fits, fast, slow, plan, back,
         section, all_ids, own_ids, embed_table, norm_gain, cotangent,
+    )
+    grad_table, slow_grad, home = lax.optimization_barrier((grad_table, slow_grad, home))
+    (fast_grad,) = call(
+        functools.partial(gather_kernel, vocab_section=vocab_section),
+        (section, own_ids, *in_order(outs, home)), (S,) + (V,) * (1 + chips), [bf16((tokens, features))],
     )
     anywhere = pl.BlockSpec(memory_space=pl.ANY)
     own_grad = pl.pallas_call(

time: 122 us -> 107 us (0.88)
  the two profiles are of different devices: /device:TPU:9 before, /device:TPU:6 now
where the time goes in v7:
time: 107 us; the launch traced here: 105 us
  starting transfers between devices  49.1 us (46%)
  blocking collectives  22.8 us (21%)
  Pallas kernels  16.5 us (15%)
  waiting for transfers between devices  11.3 us (11%)
  other arithmetic  3.34 us (3%)
  between operations  2.11 us (2%)
    ppermute x6, starting transfers between devices, to_chip(): return lax.ppermute(array, CHIPS, [(i, i ^ k) for i in range(chips)])  25.1 us
    all_to_all x1, blocking collectives, on_device(): marked = lax.all_to_all(marked, 'dp', 0, 0, tiled=True)  22.8 us
    pallas_call x9, Pallas kernels, call(): pl.pallas_call(kernel, in_specs=[whole(o.shape, s) for o, s in zip(operan...  16.5 us
    all_to_all x1, starting transfers between devices, on_device(): back = lax.all_to_all(by_column, 'dp', 0, 0, tiled=True)  13.5 us
    ppermute x6, waiting for transfers between devices, to_chip(): return lax.ppermute(array, CHIPS, [(i, i ^ k) for i in range(chips)])  6.9 us
    all_to_all x1, starting transfers between devices, on_device(): full_rows = lax.all_to_all(rows, 'dp', 0, 0, tiled=True)  6.01 us
    ppermute x2, starting transfers between devices, to_sibling(): return lax.ppermute(array, CORES, [(0, 1), (1, 0)])  4.45 us
    all_to_all x1, waiting for transfers between devices, on_device(): back = lax.all_to_all(by_column, 'dp', 0, 0, tiled=True)  3.93 us
  transfers between devices with their start and end apart: 10, of which 4 were waited for; matrix products, arithmetic and copies ran while one was open for 3% of the time, Pallas kernels for 6%

profile of v7, /device:TPU:6, one launch (start us, length us, event | category | flops | bytes accessed | tf_op | source)
XLA Modules:
  0.0 105.2 jit_solution(776482072210737816)
XLA Ops:
  0.6 0.0 copy-start.5
  0.6 1.5 %shard_map.60 = (bf16[72,1024]{1,0:T(8,128)(2,1)S(1)}, bf16[72,1024]{1,0:T(8,128)(2,1)S(1)}, bf16[72,1024]{1,0:T(8,128)(2,1)S(1)}, bf16[72,1024]{1,0:T(8,128)(2,...) custom-call(s32[1]{0:T(128)} %bitcast.2.section_ref, s32[1,128]{1,0:T(1,128)} %bitcast.9, ...), custom_call_target="tpu_custom_call" | custom-call | tf_op jit(solution)/shard_map/pallas_call | solution.py:180
  2.1 7.7 %collective-permute-start = (bf16[72,1024]{1,0:T(8,128)(2,1)S(1)}, bf16[72,1024]{1,0:T(8,128)(2,1)S(1)}, u32[]{:S(2)}, u32[]{:S(2)}) collective-permute-start(bf16[72,1024]{1,0:T(8,128)(2,1)S(1)} %get-tuple-element.75), channel_id=1, source_target_pairs={{0,256},{128,384},{256,0},{384,128},{1,257},{129,385},{257,1},{385... | collective-permute-start | bytes 442376 | tf_op jit(solution)/shard_map/ppermute | solution.py:515
  9.8 2.7 %collective-permute-start.1 = (bf16[72,1024]{1,0:T(8,128)(2,1)S(1)}, bf16[72,1024]{1,0:T(8,128)(2,1)S(1)}, u32[]{:S(2)}, u32[]{:S(2)}) collective-permute-start(bf16[72,1024]{1,0:T(8,128)(2,1)S(1)} %get-tuple-element.76), channel_id=1, source_target_pairs={{0,128},{128,0},{256,384},{384,256},{1,129},{129,1},{257,385},{385... | collective-permute-start | bytes 442376 | tf_op jit(solution)/shard_map/ppermute | solution.py:515
  12.6 0.8 shard_map.59
  13.3 22.8 %all_to_all.33 = s32[64,1,128]{2,1,0:T(1,128)S(1)} all-to-all(s32[64,1,128]{2,1,0:T(1,128)S(1)} %shard_map.59), channel_id=1, replica_groups=mesh['section_0'=4,'section_1'=2,'dp'=64] {'dp'}, dimensions={0} | all-to-all | bytes 65536 | tf_op jit(solution)/shard_map/all_to_all | solution.py:509
  36.1 0.0 collective-permute-done.refs_2_
  36.1 0.0 collective-permute-done.1.refs_1_
  36.1 5.6 %shard_map.61 = (bf16[64,32,128]{2,1,0:T(8,128)(2,1)}, s32[40,128]{1,0:T(8,128)S(1)}) custom-call(s32[1]{0:T(128)} %bitcast.2.section_ref, s32[64,128]{1,0:T(8,128)S(1)} %bitcast.5, bf16[8192,128]{1,0:T(8,128)(2,1)} %table_ref.1), custom_call_target="tpu_custom_call" | custom-call | tf_op jit(solution)/shard_map/pallas_call | solution.py:180
  41.7 6.0 %all-to-all-start.5 = ((bf16[64,32,128]{2,1,0:T(8,128)(2,1)}), bf16[64,32,128]{2,1,0:T(8,128)(2,1)S(1)}, u32[]{:S(2)}, u32[]{:S(2)}) async-start(bf16[64,32,128]{2,1,0:T(8,128)(2,1)} %get-tuple-element.78), calls=%async_computation.5 | async-start | bytes 1048576 | tf_op jit(solution)/shard_map/all_to_all | solution.py:547
  47.7 2.4 %collective-permute-start.2 = (bf16[72,1024]{1,0:T(8,128)(2,1)S(1)}, bf16[72,1024]{1,0:T(8,128)(2,1)S(1)}, u32[]{:S(2)}, u32[]{:S(2)}) collective-permute-start(bf16[72,1024]{1,0:T(8,128)(2,1)S(1)} %get-tuple-element.87), channel_id=1, source_target_pairs={{0,384},{128,256},{256,128},{384,0},{1,385},{129,257},{257,129},{3... | collective-permute-start | bytes 442376 | tf_op jit(solution)/shard_map/ppermute | solution.py:515
  50.2 0.0 copy-done.5
  50.2 6.7 %collective-permute-done.2.refs_3_ = bf16[72,1024]{1,0:T(8,128)(2,1)S(1)} collective-permute-done((bf16[72,1024]{1,0:T(8,128)(2,1)S(1)}, bf16[72,1024]{1,0:T(8,128)(2,1)S(1)}, u32[]{:S(2)}, u32[]{:S(2)}) %collective-permute-start.2) | collective-permute-done | bytes 147488 | tf_op jit(solution)/shard_map/ppermute | solution.py:515
  56.9 1.9 %collective-permute-start.3 = (bf16[4,72,1024]{2,1,0:T(8,128)(2,1)S(1)}, bf16[4,72,1024]{2,1,0:T(8,128)(2,1)S(1)}, u32[]{:S(2)}, u32[]{:S(2)}) collective-permute-start(bf16[4,72,1024]{2,1,0:T(8,128)(2,1)S(1)} %shard_map.62), channel_id=1, source_target_pairs={{0,64},{64,0},{1,65},{65,1},{2,66},{66,2},{3,67},{67,3},{4,68},{68... | collective-permute-start | bytes 1769480 | tf_op jit(solution)/shard_map/ppermute | solution.py:518
  58.8 0.7 negate_select_fusion.5
  59.5 0.1 convert_reduce_fusion.1
  59.6 0.7 reduce_max.18
  60.3 1.2 %convert_reduce_fusion = s32[64,8]{1,0:T(8,128)S(1)} fusion(s32[64,128]{1,0:T(8,128)S(1)} %get-tuple-element.107, pred[64,128]{1,0:T(8,128)(4,1)S(1)} %broadcast_compare_fusion), kind=kLoop, calls=%fused_computation.1 | loop fusion | flops 261632 | bytes 43008 | tf_op jit(solution)/shard_map/reduce_sum | solution.py:534
  61.5 0.7 reduce_max.19
  63.5 0.0 all-to-all-done.5.rows_ref
  63.5 0.0 collective-permute-done.3.got_ref
  63.5 1.2 %shard_map.63 = (bf16[4,72,1024]{2,1,0:T(8,128)(2,1)S(1)}, bf16[4,72,1024]{2,1,0:T(8,128)(2,1)S(1)}) custom-call(s32[1]{0:T(128)} %bitcast.2.section_ref, bf16[64,32,128]{2,1,0:T(8,128)(2,1)S(1)} %all-to-all-done.5.rows_ref, f32[8,1024]{1,0:T(8,128)S(1)} %reshape.118.gain_ref, bf16[72,32]{1,0:T(8,128)(2,1)S(1)} %get-tuple-element.83.expand_ref, ...), custom_call_target="tpu_custom_call" | custom-call | tf_op jit(solution)/shard_map/pallas_call | solution.py:180
  64.7 0.0 copy-start.4
  64.7 0.0 copy-start.7
  64.7 2.5 %collective-permute-start.4 = (bf16[4,72,1024]{2,1,0:T(8,128)(2,1)S(1)}, bf16[4,72,1024]{2,1,0:T(8,128)(2,1)S(1)}, u32[]{:S(2)}, u32[]{:S(2)}) collective-permute-start(bf16[4,72,1024]{2,1,0:T(8,128)(2,1)S(1)} %get-tuple-element.89.give_ref), channel_id=1, source_target_pairs={{0,64},{64,0},{1,65},{65,1},{2,66},{66,2},{3,67},{67,3},{4,68},{68... | collective-permute-start | bytes 1769480 | tf_op jit(solution)/shard_map/ppermute | solution.py:518
  67.3 1.1 %shard_map.64 = bf16[64,32,128]{2,1,0:T(8,128)(2,1)} custom-call(s32[1]{0:T(128)} %bitcast.2.section_ref, bf16[32,72]{1,0:T(8,128)(2,1)S(1)} %get-tuple-element.81.combine_ref, bf16[4,72,1024]{2,1,0:T(8,128)(2,1)S(1)} %get-tuple-element.88.keep_ref, bf16[4,72,1024]{2,1,0:T(8,128)(2,1)S(1)} %get-tuple-element.89.give_ref), custom_call_target="tpu_custom_call" | custom-call | tf_op jit(solution)/shard_map/pallas_call | solution.py:180
  68.4 0.5 collective-permute-done.4.got_ref
  68.9 0.2 shard_map.65
  69.0 13.5 %all-to-all-start.6 = ((bf16[64,32,128]{2,1,0:T(8,128)(2,1)}), bf16[64,32,128]{2,1,0:T(8,128)(2,1)S(1)}, u32[]{:S(2)}, u32[]{:S(2)}) async-start(bf16[64,32,128]{2,1,0:T(8,128)(2,1)} %shard_map.64), calls=%async_computation.6 | async-start | bytes 1048576 | tf_op jit(solution)/shard_map/all_to_all | solution.py:563
  82.6 4.9 %collective-permute-start.5 = (bf16[72,1024]{1,0:T(8,128)(2,1)S(1)}, bf16[72,1024]{1,0:T(8,128)(2,1)S(1)}, u32[]{:S(2)}, u32[]{:S(2)}) collective-permute-start(bf16[72,1024]{1,0:T(8,128)(2,1)S(1)} %get-tuple-element.97), channel_id=1, source_target_pairs={{0,256},{128,384},{256,0},{384,128},{1,257},{129,385},{257,1},{385... | collective-permute-start | bytes 442376 | tf_op jit(solution)/shard_map/ppermute | solution.py:515
  87.5 2.0 %collective-permute-start.6 = (bf16[72,1024]{1,0:T(8,128)(2,1)S(1)}, bf16[72,1024]{1,0:T(8,128)(2,1)S(1)}, u32[]{:S(2)}, u32[]{:S(2)}) collective-permute-start(bf16[72,1024]{1,0:T(8,128)(2,1)S(1)} %get-tuple-element.98), channel_id=1, source_target_pairs={{0,128},{128,0},{256,384},{384,256},{1,129},{129,1},{257,385},{385... | collective-permute-start | bytes 442376 | tf_op jit(solution)/shard_map/ppermute | solution.py:515
  89.5 5.3 %collective-permute-start.7 = (bf16[72,1024]{1,0:T(8,128)(2,1)S(1)}, bf16[72,1024]{1,0:T(8,128)(2,1)S(1)}, u32[]{:S(2)}, u32[]{:S(2)}) collective-permute-start(bf16[72,1024]{1,0:T(8,128)(2,1)S(1)} %get-tuple-element.99), channel_id=1, source_target_pairs={{0,384},{128,256},{256,128},{384,0},{1,385},{129,257},{257,129},{3... | collective-permute-start | bytes 442376 | tf_op jit(solution)/shard_map/ppermute | solution.py:515
  94.8 3.9 %all-to-all-done.6 = bf16[64,32,128]{2,1,0:T(8,128)(2,1)S(1)} async-done(((bf16[64,32,128]{2,1,0:T(8,128)(2,1)}), bf16[64,32,128]{2,1,0:T(8,128)(2,1)S(1)}, u32[]{:S(2)}, u32[]{:S(2)}) %all-to-all-start.6) | async-done | bytes 524320 | tf_op jit(solution)/shard_map/all_to_all | solution.py:563
  98.8 0.0 copy-done.4
  98.8 0.0 copy-done.7
  98.8 4.9 %conditional.1 = (bf16[8192,128]{1,0:T(8,128)(2,1)S(1)}, bf16[128,1024]{1,0:T(8,128)(2,1)S(1)}) conditional(s32[]{:T(128)} %convert_element_type.12, (s32[64,128]{1,0:T(8,128)}, s32[64,128]{1,0:T(8,128)S(1)}, s32[1]{0:T(128)}, bf16[8192,128]{1,0:T(8,128)(2,1)}, s32[1,128]{1,0:T(1,128)S(1)}, /*index=5*/bf16[128,1024]{1,0:T(8,128)(2,1)S(1)}, ...), branch_computations={%region_4.5_spmd, %region_5.6_spmd} | conditional | flops 40960 | bytes 46366912 | solution.py:575
  98.8 4.8 %branch_1_fun.1 = bf16[8192,128]{1,0:T(8,128)(2,1)S(1)} custom-call(s32[40,128]{1,0:T(8,128)S(1)} %get-tuple-element.40.plan_ref, bf16[64,32,128]{2,1,0:T(8,128)(2,1)S(1)} %get-tuple-element.41.grads_ref), custom_call_target="tpu_custom_call" | custom-call | tf_op jit(solution)/shard_map/cond/branch_1_fun/pallas_call | solution.py:180
  103.7 0.0 copy-start.3
  103.7 0.0 collective-permute-done.5.refs_2_
  103.7 0.2 collective-permute-done.6.refs_1_
  103.9 0.0 collective-permute-done.7.refs_3_
  103.9 1.3 %shard_map.66.fast_ref = bf16[128,1024]{1,0:T(8,128)(2,1)} custom-call(s32[1]{0:T(128)} %bitcast.2.section_ref, s32[1,128]{1,0:T(1,128)S(1)} %bitcast.12, bf16[72,1024]{1,0:T(8,128)(2,1)S(1)} %get-tuple-element.101.refs_0_, bf16[72,1024]{1,0:T(8,128)(2,1)S(1)} %collective-permute-done.6.refs_1_, bf16[72,1024]{1,0:T(8,128)(2,1)S(1)} %collective-permute-done.5.refs_2_, ...), custom_call_target="tpu_custom_call" | custom-call | tf_op jit(solution)/shard_map/pallas_call | solution.py:180
  105.2 0.0 copy-done.3
  (6 shorter events, 0.1 us)
Async XLA Ops:
  0.6 49.6 %copy-start.5 = (f32[8192]{0:T(1024)S(1)}, f32[8192]{0:T(1024)}, u32[]{:S(2)}) copy-start(f32[8192]{0:T(1024)} %param.8) | copy-start | bytes 98308
  2.1 34.0 %collective-permute-start = (bf16[72,1024]{1,0:T(8,128)(2,1)S(1)}, bf16[72,1024]{1,0:T(8,128)(2,1)S(1)}, u32[]{:S(2)}, u32[]{:S(2)}) collective-permute-start(bf16[72,1024]{1,0:T(8,128)(2,1)S(1)} %get-tuple-element.75), channel_id=1, source_target_pairs={{0,256},{128,384},{256,0},{384,128},{1,257},{129,385},{257,1},{385... | collective-permute-start | bytes 442376 | tf_op jit(solution)/shard_map/ppermute | solution.py:515
  9.8 26.3 %collective-permute-start.1 = (bf16[72,1024]{1,0:T(8,128)(2,1)S(1)}, bf16[72,1024]{1,0:T(8,128)(2,1)S(1)}, u32[]{:S(2)}, u32[]{:S(2)}) collective-permute-start(bf16[72,1024]{1,0:T(8,128)(2,1)S(1)} %get-tuple-element.76), channel_id=1, source_target_pairs={{0,128},{128,0},{256,384},{384,256},{1,129},{129,1},{257,385},{385... | collective-permute-start | bytes 442376 | tf_op jit(solution)/shard_map/ppermute | solution.py:515
  41.7 21.7 %all-to-all-start.5 = ((bf16[64,32,128]{2,1,0:T(8,128)(2,1)}), bf16[64,32,128]{2,1,0:T(8,128)(2,1)S(1)}, u32[]{:S(2)}, u32[]{:S(2)}) async-start(bf16[64,32,128]{2,1,0:T(8,128)(2,1)} %get-tuple-element.78), calls=%async_computation.5 | async-start | bytes 1048576 | tf_op jit(solution)/shard_map/all_to_all | solution.py:547
  47.7 9.2 %collective-permute-start.2 = (bf16[72,1024]{1,0:T(8,128)(2,1)S(1)}, bf16[72,1024]{1,0:T(8,128)(2,1)S(1)}, u32[]{:S(2)}, u32[]{:S(2)}) collective-permute-start(bf16[72,1024]{1,0:T(8,128)(2,1)S(1)} %get-tuple-element.87), channel_id=1, source_target_pairs={{0,384},{128,256},{256,128},{384,0},{1,385},{129,257},{257,129},{3... | collective-permute-start | bytes 442376 | tf_op jit(solution)/shard_map/ppermute | solution.py:515
  56.9 6.5 %collective-permute-start.3 = (bf16[4,72,1024]{2,1,0:T(8,128)(2,1)S(1)}, bf16[4,72,1024]{2,1,0:T(8,128)(2,1)S(1)}, u32[]{:S(2)}, u32[]{:S(2)}) collective-permute-start(bf16[4,72,1024]{2,1,0:T(8,128)(2,1)S(1)} %shard_map.62), channel_id=1, source_target_pairs={{0,64},{64,0},{1,65},{65,1},{2,66},{66,2},{3,67},{67,3},{4,68},{68... | collective-permute-start | bytes 1769480 | tf_op jit(solution)/shard_map/ppermute | solution.py:518
  64.7 34.1 %copy-start.4 = (bf16[128,1024]{1,0:T(8,128)(2,1)S(1)}, bf16[128,1024]{1,0:T(8,128)(2,1)}, u32[]{:S(2)}) copy-start(bf16[128,1024]{1,0:T(8,128)(2,1)} %cotangent_ref.1) | copy-start | bytes 786436
  64.7 34.1 %copy-start.7 = (s32[128]{0:T(128)S(1)}, s32[128]{0:T(128)}, u32[]{:S(2)}) copy-start(s32[128]{0:T(128)} %param.6) | copy-start | bytes 1540
  64.7 4.2 %collective-permute-start.4 = (bf16[4,72,1024]{2,1,0:T(8,128)(2,1)S(1)}, bf16[4,72,1024]{2,1,0:T(8,128)(2,1)S(1)}, u32[]{:S(2)}, u32[]{:S(2)}) collective-permute-start(bf16[4,72,1024]{2,1,0:T(8,128)(2,1)S(1)} %get-tuple-element.89.give_ref), channel_id=1, source_target_pairs={{0,64},{64,0},{1,65},{65,1},{2,66},{66,2},{3,67},{67,3},{4,68},{68... | collective-permute-start | bytes 1769480 | tf_op jit(solution)/shard_map/ppermute | solution.py:518
  69.0 29.7 %all-to-all-start.6 = ((bf16[64,32,128]{2,1,0:T(8,128)(2,1)}), bf16[64,32,128]{2,1,0:T(8,128)(2,1)S(1)}, u32[]{:S(2)}, u32[]{:S(2)}) async-start(bf16[64,32,128]{2,1,0:T(8,128)(2,1)} %shard_map.64), calls=%async_computation.6 | async-start | bytes 1048576 | tf_op jit(solution)/shard_map/all_to_all | solution.py:563
  82.6 21.1 %collective-permute-start.5 = (bf16[72,1024]{1,0:T(8,128)(2,1)S(1)}, bf16[72,1024]{1,0:T(8,128)(2,1)S(1)}, u32[]{:S(2)}, u32[]{:S(2)}) collective-permute-start(bf16[72,1024]{1,0:T(8,128)(2,1)S(1)} %get-tuple-element.97), channel_id=1, source_target_pairs={{0,256},{128,384},{256,0},{384,128},{1,257},{129,385},{257,1},{385... | collective-permute-start | bytes 442376 | tf_op jit(solution)/shard_map/ppermute | solution.py:515
  87.5 16.4 %collective-permute-start.6 = (bf16[72,1024]{1,0:T(8,128)(2,1)S(1)}, bf16[72,1024]{1,0:T(8,128)(2,1)S(1)}, u32[]{:S(2)}, u32[]{:S(2)}) collective-permute-start(bf16[72,1024]{1,0:T(8,128)(2,1)S(1)} %get-tuple-element.98), channel_id=1, source_target_pairs={{0,128},{128,0},{256,384},{384,256},{1,129},{129,1},{257,385},{385... | collective-permute-start | bytes 442376 | tf_op jit(solution)/shard_map/ppermute | solution.py:515
  89.5 14.4 %collective-permute-start.7 = (bf16[72,1024]{1,0:T(8,128)(2,1)S(1)}, bf16[72,1024]{1,0:T(8,128)(2,1)S(1)}, u32[]{:S(2)}, u32[]{:S(2)}) collective-permute-start(bf16[72,1024]{1,0:T(8,128)(2,1)S(1)} %get-tuple-element.99), channel_id=1, source_target_pairs={{0,384},{128,256},{256,128},{384,0},{1,385},{129,257},{257,129},{3... | collective-permute-start | bytes 442376 | tf_op jit(solution)/shard_map/ppermute | solution.py:515
  103.7 1.6 %copy-start.3 = (bf16[8192,128]{1,0:T(8,128)(2,1)}, bf16[8192,128]{1,0:T(8,128)(2,1)S(1)}, u32[]{:S(2)}) copy-start(bf16[8192,128]{1,0:T(8,128)(2,1)S(1)} %get-tuple-element.73) | copy-start | bytes 6291460

commit v8 on v7

--- a/solution.py
+++ b/solution.py
@@ -14,7 +14,7 @@
 ROW_SLOTS = 32
 CHUNK = 8
 FAR_FIRST = (2, 1, 3)
-EARLY = 2
+EARLY = 1
 REPEATED = 1 << 16
 CHIPS = "section_0"
 CORES = "section_1"
@@ -229,11 +229,21 @@
     return grad_table, own_grad
 
 
-def row_plan(section, ids, plan_ref, vocab_section):
+def row_plan(section, ids, plan_ref, over_ref, vocab_section):
     slots = plan_ref.shape[0] - CHUNK
+    sections = 1 + (REPEATED - 1) // vocab_section
     ids = ids.astype(jnp.float32)
     ids = jnp.concatenate([ids, ids], axis=0)
     ids = ids.T.astype(jnp.int32)
+    home = (ids % REPEATED) // vocab_section
+    over = jnp.full((1, LANES), -1, jnp.int32)
+    for s in range(sections):
+        new = jnp.where((home == s) & (ids < REPEATED), 1, 0)
+        over = jnp.maximum(over, jnp.sum(new, axis=0, keepdims=True) - slots)
+    for s in range(0, sections, 2):
+        here = jnp.where(home // 2 == s // 2, 1, 0)
+        over = jnp.maximum(over, jnp.sum(here, axis=0, keepdims=True) - TOKEN_SLOTS)
+    over_ref[...] = jnp.broadcast_to(over, over_ref.shape)
     local = ids - section * vocab_section
     inside = (local >= 0) & (local < vocab_section) & (ids < REPEATED)
     before = (
@@ -257,7 +267,7 @@
 
 
 def row_pick_kernel(
-    section_ref, ids_ref, table_ref, rows_ref, plan_ref,
+    section_ref, ids_ref, table_ref, rows_ref, plan_ref, over_ref,
     held_ref, wide_ref, picked_ref, steps_ref, arrived, planned, *, vocab_section
 ):
     groups, slots, columns = rows_ref.shape
@@ -272,7 +282,7 @@
     ]
     for copy in copies:
         copy.start()
-    row_plan(section_ref[0], ids_ref[...], plan_ref, vocab_section)
+    row_plan(section_ref[0], ids_ref[...], plan_ref, over_ref, vocab_section)
     plan_copy = pltpu.make_async_copy(plan_ref, steps_ref, planned)
     plan_copy.start()
     picked_ref[...] = jnp.zeros(picked_ref.shape, jnp.float32)
@@ -526,26 +536,17 @@
     marked, handed[:EARLY] = lax.optimization_barrier((marked, handed[:EARLY]))
     handed = in_order(hands, handed)
     marked = marked.reshape(groups, tokens)
-    all_ids = marked % REPEATED
-    in_chip = all_ids[:, :, None] // (2 * vocab_section) == jnp.arange(chips)
-    in_section = all_ids[:, :, None] // vocab_section == jnp.arange(sections)
-    new_in_section = in_section & (marked < REPEATED)[:, :, None]
-    fits = (jnp.max(jnp.sum(in_chip, axis=1)) <= TOKEN_SLOTS) & (
-        jnp.max(jnp.sum(new_in_section, axis=1)) <= ROW_SLOTS
-    )
-
     wide_shape = (vocab_section + CHUNK, columns)
     wide_slots = f32((ROW_SLOTS, columns), jnp.float32)
     plan_shape = (ROW_SLOTS + CHUNK, LANES)
-    rows, plan = call(
+    rows, plan, over = call(
         functools.partial(row_pick_kernel, vocab_section=vocab_section),
         (section, marked, embed_table), (S, V, pltpu.HBM),
-        [bf16((groups, ROW_SLOTS, columns)), i32(plan_shape)],
+        [bf16((groups, ROW_SLOTS, columns)), i32(plan_shape), i32((8, LANES))],
         [f32(embed_table.shape, jnp.bfloat16), f32(wide_shape, jnp.float32), wide_slots],
         [pltpu.SMEM(plan_shape, jnp.int32), pltpu.SemaphoreType.DMA((4,)), pltpu.SemaphoreType.DMA],
     )
     full_rows = lax.all_to_all(rows, "dp", 0, 0, tiled=True)
-    fits, full_rows = lax.optimization_barrier((fits, full_rows))
     (stack,) = call(stack_kernel, tuple(handed), (V,) * chips, [parts])
     got = to_sibling(stack)
     keep, give = call(
@@ -569,12 +570,14 @@
         )
         return grad_table, jnp.zeros((tokens, features), jnp.bfloat16)
 
-    def slow(plan, back, *operands):
-        return passage(tokens, *operands)
+    def slow(plan, back, section, marked, *operands):
+        return passage(tokens, section, marked % REPEATED, *operands)
+
+    fits = jnp.max(over[:1]) <= 0
 
     grad_table, slow_grad = lax.cond(
         fits, fast, slow, plan, back,
-        section, all_ids, own_ids, embed_table, norm_gain, cotangent,
+        section, marked, own_ids, embed_table, norm_gain, cotangent,
     )
     grad_table, slow_grad, home = lax.optimization_barrier((grad_table, slow_grad, home))
     (fast_grad,) = call(

time: 107 us -> 103 us (0.963)
  other arithmetic: 3.34 us -> 0.63 us
  starting transfers between devices: 49.1 us -> 47.9 us
    ppermute x2, waiting for transfers between devices: 0.5 us -> 2.75 us  [to_sibling(): return lax.ppermute(array, CORES, [(0, 1), (1, 0)])]
    all_to_all x1, waiting for transfers between devices: 3.93 us -> 2.46 us  [on_device(): back = lax.all_to_all(by_column, 'dp', 0, 0, tiled=True)]
    reduce_sum x2 -> x0, other arithmetic: 1.29 us -> none  [the longest x1 1.15 us: on_device(): jnp.sum(new_in_section, axis=1)]
  transfers between devices with their start and end apart: 10 -> 10, of which waited for: 4 -> 6; matrix products, arithmetic and copies ran while one was open for 3% -> 1% of each run, Pallas kernels for 6% -> 7%
where the time goes in v8:
time: 103 us; the launch traced here: 102 us
  starting transfers between devices  47.9 us (47%)
  blocking collectives  22.8 us (22%)
  Pallas kernels  16.5 us (16%)
  waiting for transfers between devices  12.2 us (12%)
  between operations  1.48 us (1%)
    ppermute x6, starting transfers between devices, to_chip(): return lax.ppermute(array, CHIPS, [(i, i ^ k) for i in range(chips)])  25.3 us
    all_to_all x1, blocking collectives, on_device(): marked = lax.all_to_all(marked, 'dp', 0, 0, tiled=True)  22.8 us
    pallas_call x9, Pallas kernels, call(): pl.pallas_call(kernel, in_specs=[whole(o.shape, s) for o, s in zip(operan...  16.5 us
    all_to_all x1, starting transfers between devices, on_device(): back = lax.all_to_all(by_column, 'dp', 0, 0, tiled=True)  12.6 us
    ppermute x6, waiting for transfers between devices, to_chip(): return lax.ppermute(array, CHIPS, [(i, i ^ k) for i in range(chips)])  6.9 us
    all_to_all x1, starting transfers between devices, on_device(): full_rows = lax.all_to_all(rows, 'dp', 0, 0, tiled=True)  6.01 us
    ppermute x2, starting transfers between devices, to_sibling(): return lax.ppermute(array, CORES, [(0, 1), (1, 0)])  4.01 us
    ppermute x2, waiting for transfers between devices, to_sibling(): return lax.ppermute(array, CORES, [(0, 1), (1, 0)])  2.75 us
  transfers between devices with their start and end apart: 10, of which 6 were waited for; matrix products, arithmetic and copies ran while one was open for 1% of the time, Pallas kernels for 7%

profile of v8, /device:TPU:6, one launch (start us, length us, event | category | flops | bytes accessed | tf_op | source)
XLA Modules:
  0.0 101.6 jit_solution(4501133452052469520)
XLA Ops:
  0.6 1.5 %shard_map.60 = (bf16[72,1024]{1,0:T(8,128)(2,1)S(1)}, bf16[72,1024]{1,0:T(8,128)(2,1)S(1)}, bf16[72,1024]{1,0:T(8,128)(2,1)S(1)}, bf16[72,1024]{1,0:T(8,128)(2,...) custom-call(s32[1]{0:T(128)} %bitcast.1.section_ref, s32[1,128]{1,0:T(1,128)} %bitcast.8, ...), custom_call_target="tpu_custom_call" | custom-call | tf_op jit(solution)/shard_map/pallas_call | solution.py:180
  2.1 7.7 %collective-permute-start = (bf16[72,1024]{1,0:T(8,128)(2,1)S(1)}, bf16[72,1024]{1,0:T(8,128)(2,1)S(1)}, u32[]{:S(2)}, u32[]{:S(2)}) collective-permute-start(bf16[72,1024]{1,0:T(8,128)(2,1)S(1)} %get-tuple-element.59), channel_id=1, source_target_pairs={{0,256},{128,384},{256,0},{384,128},{1,257},{129,385},{257,1},{385... | collective-permute-start | bytes 442376 | tf_op jit(solution)/shard_map/ppermute | solution.py:525
  9.8 0.8 shard_map.59
  10.6 22.8 %all_to_all.33 = s32[64,1,128]{2,1,0:T(1,128)S(1)} all-to-all(s32[64,1,128]{2,1,0:T(1,128)S(1)} %shard_map.59), channel_id=1, replica_groups=mesh['section_0'=4,'section_1'=2,'dp'=64] {'dp'}, dimensions={0} | all-to-all | bytes 65536 | tf_op jit(solution)/shard_map/all_to_all | solution.py:519
  33.4 0.0 collective-permute-done.refs_2_
  33.4 0.0 copy-start.5
  33.4 5.6 %shard_map.61 = (bf16[64,32,128]{2,1,0:T(8,128)(2,1)}, s32[40,128]{1,0:T(8,128)S(1)}, s32[8,128]{1,0:T(8,128)S(1)}) custom-call(s32[1]{0:T(128)} %bitcast.1.section_ref, s32[64,128]{1,0:T(8,128)S(1)} %bitcast.5, bf16[8192,128]{1,0:T(8,128)(2,1)} %table_ref.1), custom_call_target="tpu_custom_call" | custom-call | tf_op jit(solution)/shard_map/pallas_call | solution.py:180
  39.0 6.0 %all-to-all-start.5 = ((bf16[64,32,128]{2,1,0:T(8,128)(2,1)}), bf16[64,32,128]{2,1,0:T(8,128)(2,1)S(1)}, u32[]{:S(2)}, u32[]{:S(2)}) async-start(bf16[64,32,128]{2,1,0:T(8,128)(2,1)} %get-tuple-element.64), calls=%async_computation.5 | async-start | bytes 1048576 | tf_op jit(solution)/shard_map/all_to_all | solution.py:549
  45.0 3.0 %collective-permute-start.1 = (bf16[72,1024]{1,0:T(8,128)(2,1)S(1)}, bf16[72,1024]{1,0:T(8,128)(2,1)S(1)}, u32[]{:S(2)}, u32[]{:S(2)}) collective-permute-start(bf16[72,1024]{1,0:T(8,128)(2,1)S(1)} %get-tuple-element.67), channel_id=1, source_target_pairs={{0,128},{128,0},{256,384},{384,256},{1,129},{129,1},{257,385},{385... | collective-permute-start | bytes 442376 | tf_op jit(solution)/shard_map/ppermute | solution.py:525
  48.0 2.3 %collective-permute-start.2 = (bf16[72,1024]{1,0:T(8,128)(2,1)S(1)}, bf16[72,1024]{1,0:T(8,128)(2,1)S(1)}, u32[]{:S(2)}, u32[]{:S(2)}) collective-permute-start(bf16[72,1024]{1,0:T(8,128)(2,1)S(1)} %get-tuple-element.69), channel_id=1, source_target_pairs={{0,384},{128,256},{256,128},{384,0},{1,385},{129,257},{257,129},{3... | collective-permute-start | bytes 442376 | tf_op jit(solution)/shard_map/ppermute | solution.py:525
  50.4 4.0 %collective-permute-done.1.refs_1_ = bf16[72,1024]{1,0:T(8,128)(2,1)S(1)} collective-permute-done((bf16[72,1024]{1,0:T(8,128)(2,1)S(1)}, bf16[72,1024]{1,0:T(8,128)(2,1)S(1)}, u32[]{:S(2)}, u32[]{:S(2)}) %collective-permute-start.1) | collective-permute-done | bytes 147488 | tf_op jit(solution)/shard_map/ppermute | solution.py:525
  54.3 2.9 %collective-permute-done.2.refs_3_ = bf16[72,1024]{1,0:T(8,128)(2,1)S(1)} collective-permute-done((bf16[72,1024]{1,0:T(8,128)(2,1)S(1)}, bf16[72,1024]{1,0:T(8,128)(2,1)S(1)}, u32[]{:S(2)}, u32[]{:S(2)}) %collective-permute-start.2) | collective-permute-done | bytes 147488 | tf_op jit(solution)/shard_map/ppermute | solution.py:525
  57.3 1.9 %collective-permute-start.3 = (bf16[4,72,1024]{2,1,0:T(8,128)(2,1)S(1)}, bf16[4,72,1024]{2,1,0:T(8,128)(2,1)S(1)}, u32[]{:S(2)}, u32[]{:S(2)}) collective-permute-start(bf16[4,72,1024]{2,1,0:T(8,128)(2,1)S(1)} %shard_map.62), channel_id=1, source_target_pairs={{0,64},{64,0},{1,65},{65,1},{2,66},{66,2},{3,67},{67,3},{4,68},{68... | collective-permute-start | bytes 1769480 | tf_op jit(solution)/shard_map/ppermute | solution.py:528
  59.2 0.0 copy-done.5
  59.3 1.9 %collective-permute-done.3.got_ref = bf16[4,72,1024]{2,1,0:T(8,128)(2,1)S(1)} collective-permute-done((bf16[4,72,1024]{2,1,0:T(8,128)(2,1)S(1)}, bf16[4,72,1024]{2,1,0:T(8,128)(2,1)S(1)}, u32[]{:S(2)}, u32[]{:S(2)}) %collective-permute-start.3) | collective-permute-done | bytes 589856 | tf_op jit(solution)/shard_map/ppermute | solution.py:528
  61.2 0.1 all-to-all-done.5.rows_ref
  61.3 1.2 %shard_map.63 = (bf16[4,72,1024]{2,1,0:T(8,128)(2,1)S(1)}, bf16[4,72,1024]{2,1,0:T(8,128)(2,1)S(1)}) custom-call(s32[1]{0:T(128)} %bitcast.1.section_ref, bf16[64,32,128]{2,1,0:T(8,128)(2,1)S(1)} %all-to-all-done.5.rows_ref, f32[8,1024]{1,0:T(8,128)S(1)} %reshape.25.gain_ref, bf16[72,32]{1,0:T(8,128)(2,1)S(1)} %get-tuple-element.65.expand_ref, ...), custom_call_target="tpu_custom_call" | custom-call | tf_op jit(solution)/shard_map/pallas_call | solution.py:180
  62.5 0.0 copy-start.4
  62.5 0.0 copy-start.6
  62.5 2.1 %collective-permute-start.4 = (bf16[4,72,1024]{2,1,0:T(8,128)(2,1)S(1)}, bf16[4,72,1024]{2,1,0:T(8,128)(2,1)S(1)}, u32[]{:S(2)}, u32[]{:S(2)}) collective-permute-start(bf16[4,72,1024]{2,1,0:T(8,128)(2,1)S(1)} %get-tuple-element.71.give_ref), channel_id=1, source_target_pairs={{0,64},{64,0},{1,65},{65,1},{2,66},{66,2},{3,67},{67,3},{4,68},{68... | collective-permute-start | bytes 1769480 | tf_op jit(solution)/shard_map/ppermute | solution.py:528
  64.6 1.1 %shard_map.64 = bf16[64,32,128]{2,1,0:T(8,128)(2,1)} custom-call(s32[1]{0:T(128)} %bitcast.1.section_ref, bf16[32,72]{1,0:T(8,128)(2,1)S(1)} %get-tuple-element.63.combine_ref, bf16[4,72,1024]{2,1,0:T(8,128)(2,1)S(1)} %get-tuple-element.70.keep_ref, bf16[4,72,1024]{2,1,0:T(8,128)(2,1)S(1)} %get-tuple-element.71.give_ref), custom_call_target="tpu_custom_call" | custom-call | tf_op jit(solution)/shard_map/pallas_call | solution.py:180
  65.7 0.8 collective-permute-done.4.got_ref
  66.5 0.2 shard_map.65
  66.7 12.6 %all-to-all-start.6 = ((bf16[64,32,128]{2,1,0:T(8,128)(2,1)}), bf16[64,32,128]{2,1,0:T(8,128)(2,1)S(1)}, u32[]{:S(2)}, u32[]{:S(2)}) async-start(bf16[64,32,128]{2,1,0:T(8,128)(2,1)} %shard_map.64), calls=%async_computation.6 | async-start | bytes 1048576 | tf_op jit(solution)/shard_map/all_to_all | solution.py:564
  79.3 4.6 %collective-permute-start.5 = (bf16[72,1024]{1,0:T(8,128)(2,1)S(1)}, bf16[72,1024]{1,0:T(8,128)(2,1)S(1)}, u32[]{:S(2)}, u32[]{:S(2)}) collective-permute-start(bf16[72,1024]{1,0:T(8,128)(2,1)S(1)} %get-tuple-element.79), channel_id=1, source_target_pairs={{0,256},{128,384},{256,0},{384,128},{1,257},{129,385},{257,1},{385... | collective-permute-start | bytes 442376 | tf_op jit(solution)/shard_map/ppermute | solution.py:525
  83.9 2.9 %collective-permute-start.6 = (bf16[72,1024]{1,0:T(8,128)(2,1)S(1)}, bf16[72,1024]{1,0:T(8,128)(2,1)S(1)}, u32[]{:S(2)}, u32[]{:S(2)}) collective-permute-start(bf16[72,1024]{1,0:T(8,128)(2,1)S(1)} %get-tuple-element.80), channel_id=1, source_target_pairs={{0,128},{128,0},{256,384},{384,256},{1,129},{129,1},{257,385},{385... | collective-permute-start | bytes 442376 | tf_op jit(solution)/shard_map/ppermute | solution.py:525
  86.8 4.8 %collective-permute-start.7 = (bf16[72,1024]{1,0:T(8,128)(2,1)S(1)}, bf16[72,1024]{1,0:T(8,128)(2,1)S(1)}, u32[]{:S(2)}, u32[]{:S(2)}) collective-permute-start(bf16[72,1024]{1,0:T(8,128)(2,1)S(1)} %get-tuple-element.81), channel_id=1, source_target_pairs={{0,384},{128,256},{256,128},{384,0},{1,385},{129,257},{257,129},{3... | collective-permute-start | bytes 442376 | tf_op jit(solution)/shard_map/ppermute | solution.py:525
  91.5 0.6 slice_reduce_fusion
  92.8 2.5 %all-to-all-done.6 = bf16[64,32,128]{2,1,0:T(8,128)(2,1)S(1)} async-done(((bf16[64,32,128]{2,1,0:T(8,128)(2,1)}), bf16[64,32,128]{2,1,0:T(8,128)(2,1)S(1)}, u32[]{:S(2)}, u32[]{:S(2)}) %all-to-all-start.6) | async-done | bytes 524320 | tf_op jit(solution)/shard_map/all_to_all | solution.py:564
  95.3 0.0 copy-done.4
  95.3 0.0 copy-done.6
  95.3 4.9 %conditional.1 = (bf16[8192,128]{1,0:T(8,128)(2,1)S(1)}, bf16[128,1024]{1,0:T(8,128)(2,1)S(1)}) conditional(s32[]{:T(128)} %convert_element_type.4, (s32[64,128]{1,0:T(8,128)S(1)}, s32[1]{0:T(128)}, bf16[8192,128]{1,0:T(8,128)(2,1)}, s32[1,128]{1,0:T(1,128)S(1)}, bf16[128,1024]{1,0:T(8,128)(2,1)S(1)}, /*index=5*/f32[8192]{0:T(1024)S(1)}) %tuple.30, ...), branch_computations={%region_1.2_spmd, %region_2.3_spmd} | conditional | flops 90112 | bytes 46203044 | solution.py:578
  95.3 4.8 %branch_1_fun.1 = bf16[8192,128]{1,0:T(8,128)(2,1)S(1)} custom-call(s32[40,128]{1,0:T(8,128)S(1)} %get-tuple-element.26.plan_ref, bf16[64,32,128]{2,1,0:T(8,128)(2,1)S(1)} %get-tuple-element.27.grads_ref), custom_call_target="tpu_custom_call" | custom-call | tf_op jit(solution)/shard_map/cond/branch_1_fun/pallas_call | solution.py:180
  100.2 0.0 copy-start.3
  100.2 0.0 collective-permute-done.5.refs_2_
  100.2 0.0 collective-permute-done.6.refs_1_
  100.2 0.0 collective-permute-done.7.refs_3_
  100.2 1.4 %shard_map.66.fast_ref = bf16[128,1024]{1,0:T(8,128)(2,1)} custom-call(s32[1]{0:T(128)} %bitcast.1.section_ref, s32[1,128]{1,0:T(1,128)S(1)} %bitcast.11, bf16[72,1024]{1,0:T(8,128)(2,1)S(1)} %get-tuple-element.83.refs_0_, bf16[72,1024]{1,0:T(8,128)(2,1)S(1)} %collective-permute-done.6.refs_1_, bf16[72,1024]{1,0:T(8,128)(2,1)S(1)} %collective-permute-done.5.refs_2_, ...), custom_call_target="tpu_custom_call" | custom-call | tf_op jit(solution)/shard_map/pallas_call | solution.py:180
  101.5 0.0 copy-done.3
  (4 shorter events, 0.1 us)
Async XLA Ops:
  2.1 31.3 %collective-permute-start = (bf16[72,1024]{1,0:T(8,128)(2,1)S(1)}, bf16[72,1024]{1,0:T(8,128)(2,1)S(1)}, u32[]{:S(2)}, u32[]{:S(2)}) collective-permute-start(bf16[72,1024]{1,0:T(8,128)(2,1)S(1)} %get-tuple-element.59), channel_id=1, source_target_pairs={{0,256},{128,384},{256,0},{384,128},{1,257},{129,385},{257,1},{385... | collective-permute-start | bytes 442376 | tf_op jit(solution)/shard_map/ppermute | solution.py:525
  33.4 25.8 %copy-start.5 = (f32[8192]{0:T(1024)S(1)}, f32[8192]{0:T(1024)}, u32[]{:S(2)}) copy-start(f32[8192]{0:T(1024)} %param.8) | copy-start | bytes 98308
  39.0 22.3 %all-to-all-start.5 = ((bf16[64,32,128]{2,1,0:T(8,128)(2,1)}), bf16[64,32,128]{2,1,0:T(8,128)(2,1)S(1)}, u32[]{:S(2)}, u32[]{:S(2)}) async-start(bf16[64,32,128]{2,1,0:T(8,128)(2,1)} %get-tuple-element.64), calls=%async_computation.5 | async-start | bytes 1048576 | tf_op jit(solution)/shard_map/all_to_all | solution.py:549
  45.0 9.4 %collective-permute-start.1 = (bf16[72,1024]{1,0:T(8,128)(2,1)S(1)}, bf16[72,1024]{1,0:T(8,128)(2,1)S(1)}, u32[]{:S(2)}, u32[]{:S(2)}) collective-permute-start(bf16[72,1024]{1,0:T(8,128)(2,1)S(1)} %get-tuple-element.67), channel_id=1, source_target_pairs={{0,128},{128,0},{256,384},{384,256},{1,129},{129,1},{257,385},{385... | collective-permute-start | bytes 442376 | tf_op jit(solution)/shard_map/ppermute | solution.py:525
  48.0 9.2 %collective-permute-start.2 = (bf16[72,1024]{1,0:T(8,128)(2,1)S(1)}, bf16[72,1024]{1,0:T(8,128)(2,1)S(1)}, u32[]{:S(2)}, u32[]{:S(2)}) collective-permute-start(bf16[72,1024]{1,0:T(8,128)(2,1)S(1)} %get-tuple-element.69), channel_id=1, source_target_pairs={{0,384},{128,256},{256,128},{384,0},{1,385},{129,257},{257,129},{3... | collective-permute-start | bytes 442376 | tf_op jit(solution)/shard_map/ppermute | solution.py:525
  57.3 3.9 %collective-permute-start.3 = (bf16[4,72,1024]{2,1,0:T(8,128)(2,1)S(1)}, bf16[4,72,1024]{2,1,0:T(8,128)(2,1)S(1)}, u32[]{:S(2)}, u32[]{:S(2)}) collective-permute-start(bf16[4,72,1024]{2,1,0:T(8,128)(2,1)S(1)} %shard_map.62), channel_id=1, source_target_pairs={{0,64},{64,0},{1,65},{65,1},{2,66},{66,2},{3,67},{67,3},{4,68},{68... | collective-permute-start | bytes 1769480 | tf_op jit(solution)/shard_map/ppermute | solution.py:528
  62.5 32.8 %copy-start.4 = (bf16[128,1024]{1,0:T(8,128)(2,1)S(1)}, bf16[128,1024]{1,0:T(8,128)(2,1)}, u32[]{:S(2)}) copy-start(bf16[128,1024]{1,0:T(8,128)(2,1)} %cotangent_ref.1) | copy-start | bytes 786436
  62.5 32.8 %copy-start.6 = (s32[128]{0:T(128)S(1)}, s32[128]{0:T(128)}, u32[]{:S(2)}) copy-start(s32[128]{0:T(128)} %param.6) | copy-start | bytes 1540
  62.5 4.0 %collective-permute-start.4 = (bf16[4,72,1024]{2,1,0:T(8,128)(2,1)S(1)}, bf16[4,72,1024]{2,1,0:T(8,128)(2,1)S(1)}, u32[]{:S(2)}, u32[]{:S(2)}) collective-permute-start(bf16[4,72,1024]{2,1,0:T(8,128)(2,1)S(1)} %get-tuple-element.71.give_ref), channel_id=1, source_target_pairs={{0,64},{64,0},{1,65},{65,1},{2,66},{66,2},{3,67},{67,3},{4,68},{68... | collective-permute-start | bytes 1769480 | tf_op jit(solution)/shard_map/ppermute | solution.py:528
  66.7 28.6 %all-to-all-start.6 = ((bf16[64,32,128]{2,1,0:T(8,128)(2,1)}), bf16[64,32,128]{2,1,0:T(8,128)(2,1)S(1)}, u32[]{:S(2)}, u32[]{:S(2)}) async-start(bf16[64,32,128]{2,1,0:T(8,128)(2,1)} %shard_map.64), calls=%async_computation.6 | async-start | bytes 1048576 | tf_op jit(solution)/shard_map/all_to_all | solution.py:564
  79.3 20.9 %collective-permute-start.5 = (bf16[72,1024]{1,0:T(8,128)(2,1)S(1)}, bf16[72,1024]{1,0:T(8,128)(2,1)S(1)}, u32[]{:S(2)}, u32[]{:S(2)}) collective-permute-start(bf16[72,1024]{1,0:T(8,128)(2,1)S(1)} %get-tuple-element.79), channel_id=1, source_target_pairs={{0,256},{128,384},{256,0},{384,128},{1,257},{129,385},{257,1},{385... | collective-permute-start | bytes 442376 | tf_op jit(solution)/shard_map/ppermute | solution.py:525
  83.9 16.3 %collective-permute-start.6 = (bf16[72,1024]{1,0:T(8,128)(2,1)S(1)}, bf16[72,1024]{1,0:T(8,128)(2,1)S(1)}, u32[]{:S(2)}, u32[]{:S(2)}) collective-permute-start(bf16[72,1024]{1,0:T(8,128)(2,1)S(1)} %get-tuple-element.80), channel_id=1, source_target_pairs={{0,128},{128,0},{256,384},{384,256},{1,129},{129,1},{257,385},{385... | collective-permute-start | bytes 442376 | tf_op jit(solution)/shard_map/ppermute | solution.py:525
  86.8 13.4 %collective-permute-start.7 = (bf16[72,1024]{1,0:T(8,128)(2,1)S(1)}, bf16[72,1024]{1,0:T(8,128)(2,1)S(1)}, u32[]{:S(2)}, u32[]{:S(2)}) collective-permute-start(bf16[72,1024]{1,0:T(8,128)(2,1)S(1)} %get-tuple-element.81), channel_id=1, source_target_pairs={{0,384},{128,256},{256,128},{384,0},{1,385},{129,257},{257,129},{3... | collective-permute-start | bytes 442376 | tf_op jit(solution)/shard_map/ppermute | solution.py:525
  100.2 1.4 %copy-start.3 = (bf16[8192,128]{1,0:T(8,128)(2,1)}, bf16[8192,128]{1,0:T(8,128)(2,1)S(1)}, u32[]{:S(2)}) copy-start(bf16[8192,128]{1,0:T(8,128)(2,1)S(1)} %get-tuple-element.57) | copy-start | bytes 6291460

commit v9 on v8

--- a/solution.py
+++ b/solution.py
@@ -13,6 +13,7 @@
 TOKEN_SLOTS = 72
 ROW_SLOTS = 32
 CHUNK = 8
+ALWAYS = 2
 FAR_FIRST = (2, 1, 3)
 EARLY = 1
 REPEATED = 1 << 16
@@ -301,13 +302,17 @@
     plan_copy.wait()
 
     def group(g, carry):
+        def copy_row(c):
+            picked_ref[pl.ds(c, 1), :] = wide_ref[pl.ds(steps_ref[c, g], 1), :]
+
         def chunk(i, carry):
             for j in range(CHUNK):
-                c = i * CHUNK + j
-                picked_ref[pl.ds(c, 1), :] = wide_ref[pl.ds(steps_ref[c, g], 1), :]
+                copy_row(i * CHUNK + j)
             return carry
 
-        lax.fori_loop(0, steps_ref[slots, g], chunk, 0)
+        for c in range(ALWAYS * CHUNK):
+            copy_row(c)
+        lax.fori_loop(ALWAYS, steps_ref[slots, g], chunk, 0)
         rows_ref[g] = picked_ref[...].astype(jnp.bfloat16)
         return carry
 
@@ -329,17 +334,18 @@
     def group(g, carry):
         wide_ref[...] = grads_ref[g].astype(jnp.float32)
 
-        def chunk(i, carry):
-            rows = [pl.ds(plan_ref[i * CHUNK + j, g], 1) for j in range(CHUNK)]
-            sums = [
-                total_ref[row, :] + wide_ref[pl.ds(i * CHUNK + j, 1), :]
-                for j, row in enumerate(rows)
-            ]
+        def add_rows(slots_here):
+            rows = [pl.ds(plan_ref[c, g], 1) for c in slots_here]
+            sums = [total_ref[row, :] + wide_ref[pl.ds(c, 1), :] for c, row in zip(slots_here, rows)]
             for row, value in zip(rows, sums):
                 total_ref[row, :] = value
+
+        def chunk(i, carry):
+            add_rows([i * CHUNK + j for j in range(CHUNK)])
             return carry
 
-        lax.fori_loop(0, plan_ref[slots, g], chunk, 0)
+        add_rows(list(range(ALWAYS * CHUNK)))
+        lax.fori_loop(ALWAYS, plan_ref[slots, g], chunk, 0)
         return carry
 
     lax.fori_loop(0, groups, group, 0)

time: 103 us -> 102 us (level)
  Pallas kernels: 16.5 us -> 14.3 us
    pallas_call x9, Pallas kernels: 16.5 us -> 14.3 us  [call(): pl.pallas_call(kernel, in_specs=[whole(o.shape, s) for o, s in zip(operan...]
  transfers between devices with their start and end apart: 10 -> 10, of which waited for: 6 -> 7; matrix products, arithmetic and copies ran while one was open for 1% -> 1% of each run, Pallas kernels for 7% -> 6%
where the time goes in v9:
time: 102 us; the launch traced here: 99.9 us
  starting transfers between devices  47.9 us (47%)
  blocking collectives  22.8 us (22%)
  Pallas kernels  14.3 us (14%)
  waiting for transfers between devices  12.7 us (12%)
  between operations  1.47 us (1%)
    ppermute x6, starting transfers between devices, to_chip(): return lax.ppermute(array, CHIPS, [(i, i ^ k) for i in range(chips)])  25.2 us
    all_to_all x1, blocking collectives, on_device(): marked = lax.all_to_all(marked, 'dp', 0, 0, tiled=True)  22.8 us
    pallas_call x9, Pallas kernels, call(): pl.pallas_call(kernel, in_specs=[whole(o.shape, s) for o, s in zip(operan...  14.3 us
    all_to_all x1, starting transfers between devices, on_device(): back = lax.all_to_all(by_column, 'dp', 0, 0, tiled=True)  12.6 us
    ppermute x6, waiting for transfers between devices, to_chip(): return lax.ppermute(array, CHIPS, [(i, i ^ k) for i in range(chips)])  7.26 us
    all_to_all x1, starting transfers between devices, on_device(): full_rows = lax.all_to_all(rows, 'dp', 0, 0, tiled=True)  6.01 us
    ppermute x2, starting transfers between devices, to_sibling(): return lax.ppermute(array, CORES, [(0, 1), (1, 0)])  4.04 us
    ppermute x2, waiting for transfers between devices, to_sibling(): return lax.ppermute(array, CORES, [(0, 1), (1, 0)])  2.72 us
  transfers between devices with their start and end apart: 10, of which 7 were waited for; matrix products, arithmetic and copies ran while one was open for 1% of the time, Pallas kernels for 6%

profile of v9, /device:TPU:6, one launch (start us, length us, event | category | flops | bytes accessed | tf_op | source)
XLA Modules:
  0.0 99.9 jit_solution(5317753952792760513)
XLA Ops:
  0.6 1.5 %shard_map.60 = (bf16[72,1024]{1,0:T(8,128)(2,1)S(1)}, bf16[72,1024]{1,0:T(8,128)(2,1)S(1)}, bf16[72,1024]{1,0:T(8,128)(2,1)S(1)}, bf16[72,1024]{1,0:T(8,128)(2,...) custom-call(s32[1]{0:T(128)} %bitcast.1.section_ref, s32[1,128]{1,0:T(1,128)} %bitcast.8, ...), custom_call_target="tpu_custom_call" | custom-call | tf_op jit(solution)/shard_map/pallas_call | solution.py:181
  2.1 7.7 %collective-permute-start = (bf16[72,1024]{1,0:T(8,128)(2,1)S(1)}, bf16[72,1024]{1,0:T(8,128)(2,1)S(1)}, u32[]{:S(2)}, u32[]{:S(2)}) collective-permute-start(bf16[72,1024]{1,0:T(8,128)(2,1)S(1)} %get-tuple-element.59), channel_id=1, source_target_pairs={{0,256},{128,384},{256,0},{384,128},{1,257},{129,385},{257,1},{385... | collective-permute-start | bytes 442376 | tf_op jit(solution)/shard_map/ppermute | solution.py:531
  9.8 0.8 shard_map.59
  10.6 22.8 %all_to_all.33 = s32[64,1,128]{2,1,0:T(1,128)S(1)} all-to-all(s32[64,1,128]{2,1,0:T(1,128)S(1)} %shard_map.59), channel_id=1, replica_groups=mesh['section_0'=4,'section_1'=2,'dp'=64] {'dp'}, dimensions={0} | all-to-all | bytes 65536 | tf_op jit(solution)/shard_map/all_to_all | solution.py:525
  33.4 0.0 collective-permute-done.refs_2_
  33.4 0.0 copy-start.5
  33.4 4.3 %shard_map.61 = (bf16[64,32,128]{2,1,0:T(8,128)(2,1)}, s32[40,128]{1,0:T(8,128)S(1)}, s32[8,128]{1,0:T(8,128)S(1)}) custom-call(s32[1]{0:T(128)} %bitcast.1.section_ref, s32[64,128]{1,0:T(8,128)S(1)} %bitcast.5, bf16[8192,128]{1,0:T(8,128)(2,1)} %table_ref.1), custom_call_target="tpu_custom_call" | custom-call | tf_op jit(solution)/shard_map/pallas_call | solution.py:181
  37.7 6.0 %all-to-all-start.5 = ((bf16[64,32,128]{2,1,0:T(8,128)(2,1)}), bf16[64,32,128]{2,1,0:T(8,128)(2,1)S(1)}, u32[]{:S(2)}, u32[]{:S(2)}) async-start(bf16[64,32,128]{2,1,0:T(8,128)(2,1)} %get-tuple-element.64), calls=%async_computation.5 | async-start | bytes 1048576 | tf_op jit(solution)/shard_map/all_to_all | solution.py:555
  43.8 2.9 %collective-permute-start.1 = (bf16[72,1024]{1,0:T(8,128)(2,1)S(1)}, bf16[72,1024]{1,0:T(8,128)(2,1)S(1)}, u32[]{:S(2)}, u32[]{:S(2)}) collective-permute-start(bf16[72,1024]{1,0:T(8,128)(2,1)S(1)} %get-tuple-element.67), channel_id=1, source_target_pairs={{0,128},{128,0},{256,384},{384,256},{1,129},{129,1},{257,385},{385... | collective-permute-start | bytes 442376 | tf_op jit(solution)/shard_map/ppermute | solution.py:531
  46.6 2.4 %collective-permute-start.2 = (bf16[72,1024]{1,0:T(8,128)(2,1)S(1)}, bf16[72,1024]{1,0:T(8,128)(2,1)S(1)}, u32[]{:S(2)}, u32[]{:S(2)}) collective-permute-start(bf16[72,1024]{1,0:T(8,128)(2,1)S(1)} %get-tuple-element.69), channel_id=1, source_target_pairs={{0,384},{128,256},{256,128},{384,0},{1,385},{129,257},{257,129},{3... | collective-permute-start | bytes 442376 | tf_op jit(solution)/shard_map/ppermute | solution.py:531
  49.1 3.8 %collective-permute-done.1.refs_1_ = bf16[72,1024]{1,0:T(8,128)(2,1)S(1)} collective-permute-done((bf16[72,1024]{1,0:T(8,128)(2,1)S(1)}, bf16[72,1024]{1,0:T(8,128)(2,1)S(1)}, u32[]{:S(2)}, u32[]{:S(2)}) %collective-permute-start.1) | collective-permute-done | bytes 147488 | tf_op jit(solution)/shard_map/ppermute | solution.py:531
  52.9 3.0 %collective-permute-done.2.refs_3_ = bf16[72,1024]{1,0:T(8,128)(2,1)S(1)} collective-permute-done((bf16[72,1024]{1,0:T(8,128)(2,1)S(1)}, bf16[72,1024]{1,0:T(8,128)(2,1)S(1)}, u32[]{:S(2)}, u32[]{:S(2)}) %collective-permute-start.2) | collective-permute-done | bytes 147488 | tf_op jit(solution)/shard_map/ppermute | solution.py:531
  55.9 1.9 %collective-permute-start.3 = (bf16[4,72,1024]{2,1,0:T(8,128)(2,1)S(1)}, bf16[4,72,1024]{2,1,0:T(8,128)(2,1)S(1)}, u32[]{:S(2)}, u32[]{:S(2)}) collective-permute-start(bf16[4,72,1024]{2,1,0:T(8,128)(2,1)S(1)} %shard_map.62), channel_id=1, source_target_pairs={{0,64},{64,0},{1,65},{65,1},{2,66},{66,2},{3,67},{67,3},{4,68},{68... | collective-permute-start | bytes 1769480 | tf_op jit(solution)/shard_map/ppermute | solution.py:534
  57.9 0.0 copy-done.5
  57.9 1.9 %collective-permute-done.3.got_ref = bf16[4,72,1024]{2,1,0:T(8,128)(2,1)S(1)} collective-permute-done((bf16[4,72,1024]{2,1,0:T(8,128)(2,1)S(1)}, bf16[4,72,1024]{2,1,0:T(8,128)(2,1)S(1)}, u32[]{:S(2)}, u32[]{:S(2)}) %collective-permute-start.3) | collective-permute-done | bytes 589856 | tf_op jit(solution)/shard_map/ppermute | solution.py:534
  59.8 0.1 all-to-all-done.5.rows_ref
  59.9 1.2 %shard_map.63 = (bf16[4,72,1024]{2,1,0:T(8,128)(2,1)S(1)}, bf16[4,72,1024]{2,1,0:T(8,128)(2,1)S(1)}) custom-call(s32[1]{0:T(128)} %bitcast.1.section_ref, bf16[64,32,128]{2,1,0:T(8,128)(2,1)S(1)} %all-to-all-done.5.rows_ref, f32[8,1024]{1,0:T(8,128)S(1)} %reshape.25.gain_ref, bf16[72,32]{1,0:T(8,128)(2,1)S(1)} %get-tuple-element.65.expand_ref, ...), custom_call_target="tpu_custom_call" | custom-call | tf_op jit(solution)/shard_map/pallas_call | solution.py:181
  61.1 0.0 copy-start.4
  61.1 0.0 copy-start.6
  61.1 2.1 %collective-permute-start.4 = (bf16[4,72,1024]{2,1,0:T(8,128)(2,1)S(1)}, bf16[4,72,1024]{2,1,0:T(8,128)(2,1)S(1)}, u32[]{:S(2)}, u32[]{:S(2)}) collective-permute-start(bf16[4,72,1024]{2,1,0:T(8,128)(2,1)S(1)} %get-tuple-element.71.give_ref), channel_id=1, source_target_pairs={{0,64},{64,0},{1,65},{65,1},{2,66},{66,2},{3,67},{67,3},{4,68},{68... | collective-permute-start | bytes 1769480 | tf_op jit(solution)/shard_map/ppermute | solution.py:534
  63.3 1.1 %shard_map.64 = bf16[64,32,128]{2,1,0:T(8,128)(2,1)} custom-call(s32[1]{0:T(128)} %bitcast.1.section_ref, bf16[32,72]{1,0:T(8,128)(2,1)S(1)} %get-tuple-element.63.combine_ref, bf16[4,72,1024]{2,1,0:T(8,128)(2,1)S(1)} %get-tuple-element.70.keep_ref, bf16[4,72,1024]{2,1,0:T(8,128)(2,1)S(1)} %get-tuple-element.71.give_ref), custom_call_target="tpu_custom_call" | custom-call | tf_op jit(solution)/shard_map/pallas_call | solution.py:181
  64.4 0.8 collective-permute-done.4.got_ref
  65.2 0.2 shard_map.65
  65.3 12.6 %all-to-all-start.6 = ((bf16[64,32,128]{2,1,0:T(8,128)(2,1)}), bf16[64,32,128]{2,1,0:T(8,128)(2,1)S(1)}, u32[]{:S(2)}, u32[]{:S(2)}) async-start(bf16[64,32,128]{2,1,0:T(8,128)(2,1)} %shard_map.64), calls=%async_computation.6 | async-start | bytes 1048576 | tf_op jit(solution)/shard_map/all_to_all | solution.py:570
  77.9 4.6 %collective-permute-start.5 = (bf16[72,1024]{1,0:T(8,128)(2,1)S(1)}, bf16[72,1024]{1,0:T(8,128)(2,1)S(1)}, u32[]{:S(2)}, u32[]{:S(2)}) collective-permute-start(bf16[72,1024]{1,0:T(8,128)(2,1)S(1)} %get-tuple-element.79), channel_id=1, source_target_pairs={{0,256},{128,384},{256,0},{384,128},{1,257},{129,385},{257,1},{385... | collective-permute-start | bytes 442376 | tf_op jit(solution)/shard_map/ppermute | solution.py:531
  82.5 2.8 %collective-permute-start.6 = (bf16[72,1024]{1,0:T(8,128)(2,1)S(1)}, bf16[72,1024]{1,0:T(8,128)(2,1)S(1)}, u32[]{:S(2)}, u32[]{:S(2)}) collective-permute-start(bf16[72,1024]{1,0:T(8,128)(2,1)S(1)} %get-tuple-element.80), channel_id=1, source_target_pairs={{0,128},{128,0},{256,384},{384,256},{1,129},{129,1},{257,385},{385... | collective-permute-start | bytes 442376 | tf_op jit(solution)/shard_map/ppermute | solution.py:531
  85.4 4.8 %collective-permute-start.7 = (bf16[72,1024]{1,0:T(8,128)(2,1)S(1)}, bf16[72,1024]{1,0:T(8,128)(2,1)S(1)}, u32[]{:S(2)}, u32[]{:S(2)}) collective-permute-start(bf16[72,1024]{1,0:T(8,128)(2,1)S(1)} %get-tuple-element.81), channel_id=1, source_target_pairs={{0,384},{128,256},{256,128},{384,0},{1,385},{129,257},{257,129},{3... | collective-permute-start | bytes 442376 | tf_op jit(solution)/shard_map/ppermute | solution.py:531
  90.2 0.6 slice_reduce_fusion
  91.5 2.7 %all-to-all-done.6 = bf16[64,32,128]{2,1,0:T(8,128)(2,1)S(1)} async-done(((bf16[64,32,128]{2,1,0:T(8,128)(2,1)}), bf16[64,32,128]{2,1,0:T(8,128)(2,1)S(1)}, u32[]{:S(2)}, u32[]{:S(2)}) %all-to-all-start.6) | async-done | bytes 524320 | tf_op jit(solution)/shard_map/all_to_all | solution.py:570
  94.1 0.0 copy-done.4
  94.2 0.0 copy-done.6
  94.2 3.9 %conditional.1 = (bf16[8192,128]{1,0:T(8,128)(2,1)S(1)}, bf16[128,1024]{1,0:T(8,128)(2,1)S(1)}) conditional(s32[]{:T(128)} %convert_element_type.4, (s32[64,128]{1,0:T(8,128)S(1)}, s32[1]{0:T(128)}, bf16[8192,128]{1,0:T(8,128)(2,1)}, s32[1,128]{1,0:T(1,128)S(1)}, bf16[128,1024]{1,0:T(8,128)(2,1)S(1)}, /*index=5*/f32[8192]{0:T(1024)S(1)}) %tuple.30, ...), branch_computations={%region_1.2_spmd, %region_2.3_spmd} | conditional | flops 90112 | bytes 46203044 | solution.py:584
  94.2 3.9 %branch_1_fun.1 = bf16[8192,128]{1,0:T(8,128)(2,1)S(1)} custom-call(s32[40,128]{1,0:T(8,128)S(1)} %get-tuple-element.26.plan_ref, bf16[64,32,128]{2,1,0:T(8,128)(2,1)S(1)} %get-tuple-element.27.grads_ref), custom_call_target="tpu_custom_call" | custom-call | tf_op jit(solution)/shard_map/cond/branch_1_fun/pallas_call | solution.py:181
  98.1 0.0 copy-start.3
  98.1 0.0 collective-permute-done.5.refs_2_
  98.1 0.4 collective-permute-done.6.refs_1_
  98.5 0.0 collective-permute-done.7.refs_3_
  98.5 1.3 %shard_map.66.fast_ref = bf16[128,1024]{1,0:T(8,128)(2,1)} custom-call(s32[1]{0:T(128)} %bitcast.1.section_ref, s32[1,128]{1,0:T(1,128)S(1)} %bitcast.11, bf16[72,1024]{1,0:T(8,128)(2,1)S(1)} %get-tuple-element.83.refs_0_, bf16[72,1024]{1,0:T(8,128)(2,1)S(1)} %collective-permute-done.6.refs_1_, bf16[72,1024]{1,0:T(8,128)(2,1)S(1)} %collective-permute-done.5.refs_2_, ...), custom_call_target="tpu_custom_call" | custom-call | tf_op jit(solution)/shard_map/pallas_call | solution.py:181
  99.8 0.0 copy-done.3
  (4 shorter events, 0.1 us)
Async XLA Ops:
  2.1 31.3 %collective-permute-start = (bf16[72,1024]{1,0:T(8,128)(2,1)S(1)}, bf16[72,1024]{1,0:T(8,128)(2,1)S(1)}, u32[]{:S(2)}, u32[]{:S(2)}) collective-permute-start(bf16[72,1024]{1,0:T(8,128)(2,1)S(1)} %get-tuple-element.59), channel_id=1, source_target_pairs={{0,256},{128,384},{256,0},{384,128},{1,257},{129,385},{257,1},{385... | collective-permute-start | bytes 442376 | tf_op jit(solution)/shard_map/ppermute | solution.py:531
  33.4 24.5 %copy-start.5 = (f32[8192]{0:T(1024)S(1)}, f32[8192]{0:T(1024)}, u32[]{:S(2)}) copy-start(f32[8192]{0:T(1024)} %param.8) | copy-start | bytes 98308
  37.7 22.1 %all-to-all-start.5 = ((bf16[64,32,128]{2,1,0:T(8,128)(2,1)}), bf16[64,32,128]{2,1,0:T(8,128)(2,1)S(1)}, u32[]{:S(2)}, u32[]{:S(2)}) async-start(bf16[64,32,128]{2,1,0:T(8,128)(2,1)} %get-tuple-element.64), calls=%async_computation.5 | async-start | bytes 1048576 | tf_op jit(solution)/shard_map/all_to_all | solution.py:555
  43.8 9.1 %collective-permute-start.1 = (bf16[72,1024]{1,0:T(8,128)(2,1)S(1)}, bf16[72,1024]{1,0:T(8,128)(2,1)S(1)}, u32[]{:S(2)}, u32[]{:S(2)}) collective-permute-start(bf16[72,1024]{1,0:T(8,128)(2,1)S(1)} %get-tuple-element.67), channel_id=1, source_target_pairs={{0,128},{128,0},{256,384},{384,256},{1,129},{129,1},{257,385},{385... | collective-permute-start | bytes 442376 | tf_op jit(solution)/shard_map/ppermute | solution.py:531
  46.6 9.2 %collective-permute-start.2 = (bf16[72,1024]{1,0:T(8,128)(2,1)S(1)}, bf16[72,1024]{1,0:T(8,128)(2,1)S(1)}, u32[]{:S(2)}, u32[]{:S(2)}) collective-permute-start(bf16[72,1024]{1,0:T(8,128)(2,1)S(1)} %get-tuple-element.69), channel_id=1, source_target_pairs={{0,384},{128,256},{256,128},{384,0},{1,385},{129,257},{257,129},{3... | collective-permute-start | bytes 442376 | tf_op jit(solution)/shard_map/ppermute | solution.py:531
  55.9 3.9 %collective-permute-start.3 = (bf16[4,72,1024]{2,1,0:T(8,128)(2,1)S(1)}, bf16[4,72,1024]{2,1,0:T(8,128)(2,1)S(1)}, u32[]{:S(2)}, u32[]{:S(2)}) collective-permute-start(bf16[4,72,1024]{2,1,0:T(8,128)(2,1)S(1)} %shard_map.62), channel_id=1, source_target_pairs={{0,64},{64,0},{1,65},{65,1},{2,66},{66,2},{3,67},{67,3},{4,68},{68... | collective-permute-start | bytes 1769480 | tf_op jit(solution)/shard_map/ppermute | solution.py:534
  61.1 33.0 %copy-start.4 = (bf16[128,1024]{1,0:T(8,128)(2,1)S(1)}, bf16[128,1024]{1,0:T(8,128)(2,1)}, u32[]{:S(2)}) copy-start(bf16[128,1024]{1,0:T(8,128)(2,1)} %cotangent_ref.1) | copy-start | bytes 786436
  61.1 33.0 %copy-start.6 = (s32[128]{0:T(128)S(1)}, s32[128]{0:T(128)}, u32[]{:S(2)}) copy-start(s32[128]{0:T(128)} %param.6) | copy-start | bytes 1540
  61.1 4.0 %collective-permute-start.4 = (bf16[4,72,1024]{2,1,0:T(8,128)(2,1)S(1)}, bf16[4,72,1024]{2,1,0:T(8,128)(2,1)S(1)}, u32[]{:S(2)}, u32[]{:S(2)}) collective-permute-start(bf16[4,72,1024]{2,1,0:T(8,128)(2,1)S(1)} %get-tuple-element.71.give_ref), channel_id=1, source_target_pairs={{0,64},{64,0},{1,65},{65,1},{2,66},{66,2},{3,67},{67,3},{4,68},{68... | collective-permute-start | bytes 1769480 | tf_op jit(solution)/shard_map/ppermute | solution.py:534
  65.3 28.8 %all-to-all-start.6 = ((bf16[64,32,128]{2,1,0:T(8,128)(2,1)}), bf16[64,32,128]{2,1,0:T(8,128)(2,1)S(1)}, u32[]{:S(2)}, u32[]{:S(2)}) async-start(bf16[64,32,128]{2,1,0:T(8,128)(2,1)} %shard_map.64), calls=%async_computation.6 | async-start | bytes 1048576 | tf_op jit(solution)/shard_map/all_to_all | solution.py:570
  77.9 20.2 %collective-permute-start.5 = (bf16[72,1024]{1,0:T(8,128)(2,1)S(1)}, bf16[72,1024]{1,0:T(8,128)(2,1)S(1)}, u32[]{:S(2)}, u32[]{:S(2)}) collective-permute-start(bf16[72,1024]{1,0:T(8,128)(2,1)S(1)} %get-tuple-element.79), channel_id=1, source_target_pairs={{0,256},{128,384},{256,0},{384,128},{1,257},{129,385},{257,1},{385... | collective-permute-start | bytes 442376 | tf_op jit(solution)/shard_map/ppermute | solution.py:531
  82.5 16.0 %collective-permute-start.6 = (bf16[72,1024]{1,0:T(8,128)(2,1)S(1)}, bf16[72,1024]{1,0:T(8,128)(2,1)S(1)}, u32[]{:S(2)}, u32[]{:S(2)}) collective-permute-start(bf16[72,1024]{1,0:T(8,128)(2,1)S(1)} %get-tuple-element.80), channel_id=1, source_target_pairs={{0,128},{128,0},{256,384},{384,256},{1,129},{129,1},{257,385},{385... | collective-permute-start | bytes 442376 | tf_op jit(solution)/shard_map/ppermute | solution.py:531
  85.4 13.2 %collective-permute-start.7 = (bf16[72,1024]{1,0:T(8,128)(2,1)S(1)}, bf16[72,1024]{1,0:T(8,128)(2,1)S(1)}, u32[]{:S(2)}, u32[]{:S(2)}) collective-permute-start(bf16[72,1024]{1,0:T(8,128)(2,1)S(1)} %get-tuple-element.81), channel_id=1, source_target_pairs={{0,384},{128,256},{256,128},{384,0},{1,385},{129,257},{257,129},{3... | collective-permute-start | bytes 442376 | tf_op jit(solution)/shard_map/ppermute | solution.py:531
  98.1 1.8 %copy-start.3 = (bf16[8192,128]{1,0:T(8,128)(2,1)}, bf16[8192,128]{1,0:T(8,128)(2,1)S(1)}, u32[]{:S(2)}) copy-start(bf16[8192,128]{1,0:T(8,128)(2,1)S(1)} %get-tuple-element.57) | copy-start | bytes 6291460

commit v10 on v9

--- a/solution.py
+++ b/solution.py
@@ -15,7 +15,7 @@
 CHUNK = 8
 ALWAYS = 2
 FAR_FIRST = (2, 1, 3)
-EARLY = 1
+EARLY = 2
 REPEATED = 1 << 16
 CHIPS = "section_0"
 CORES = "section_1"

time: 102 us -> 103 us (level)
  waiting for transfers between devices: 12.7 us -> 15 us
    all_to_all x1, waiting for transfers between devices: 0.06 us -> 2.14 us  [on_device(): full_rows = lax.all_to_all(rows, 'dp', 0, 0, tiled=True)]
    all_to_all x1, starting transfers between devices: 12.6 us -> 11.5 us  [on_device(): back = lax.all_to_all(by_column, 'dp', 0, 0, tiled=True)]
  transfers between devices with their start and end apart: 10 -> 10, of which waited for: 7 -> 6; matrix products, arithmetic and copies ran while one was open for 1% -> 1% of each run, Pallas kernels for 6% -> 6%
where the time goes in v10:
time: 103 us; the launch traced here: 101 us
  starting transfers between devices  46.9 us (46%)
  blocking collectives  22.8 us (22%)
  waiting for transfers between devices  15 us (15%)
  Pallas kernels  14.2 us (14%)
  between operations  1.47 us (1%)
    ppermute x6, starting transfers between devices, to_chip(): return lax.ppermute(array, CHIPS, [(i, i ^ k) for i in range(chips)])  25.4 us
    all_to_all x1, blocking collectives, on_device(): marked = lax.all_to_all(marked, 'dp', 0, 0, tiled=True)  22.8 us
    pallas_call x9, Pallas kernels, call(): pl.pallas_call(kernel, in_specs=[whole(o.shape, s) for o, s in zip(operan...  14.1 us
    all_to_all x1, starting transfers between devices, on_device(): back = lax.all_to_all(by_column, 'dp', 0, 0, tiled=True)  11.5 us
    ppermute x6, waiting for transfers between devices, to_chip(): return lax.ppermute(array, CHIPS, [(i, i ^ k) for i in range(chips)])  7.42 us
    all_to_all x1, starting transfers between devices, on_device(): full_rows = lax.all_to_all(rows, 'dp', 0, 0, tiled=True)  6.01 us
    ppermute x2, starting transfers between devices, to_sibling(): return lax.ppermute(array, CORES, [(0, 1), (1, 0)])  3.97 us
    ppermute x2, waiting for transfers between devices, to_sibling(): return lax.ppermute(array, CORES, [(0, 1), (1, 0)])  2.79 us
  transfers between devices with their start and end apart: 10, of which 6 were waited for; matrix products, arithmetic and copies ran while one was open for 1% of the time, Pallas kernels for 6%

profile of v10, /device:TPU:6, one launch (start us, length us, event | category | flops | bytes accessed | tf_op | source)
XLA Modules:
  0.0 101.0 jit_solution(4796118724293532064)
XLA Ops:
  0.6 1.5 %shard_map.60 = (bf16[72,1024]{1,0:T(8,128)(2,1)S(1)}, bf16[72,1024]{1,0:T(8,128)(2,1)S(1)}, bf16[72,1024]{1,0:T(8,128)(2,1)S(1)}, bf16[72,1024]{1,0:T(8,128)(2,...) custom-call(s32[1]{0:T(128)} %bitcast.1.section_ref, s32[1,128]{1,0:T(1,128)} %bitcast.8, ...), custom_call_target="tpu_custom_call" | custom-call | tf_op jit(solution)/shard_map/pallas_call | solution.py:181
  2.1 7.7 %collective-permute-start = (bf16[72,1024]{1,0:T(8,128)(2,1)S(1)}, bf16[72,1024]{1,0:T(8,128)(2,1)S(1)}, u32[]{:S(2)}, u32[]{:S(2)}) collective-permute-start(bf16[72,1024]{1,0:T(8,128)(2,1)S(1)} %get-tuple-element.60), channel_id=1, source_target_pairs={{0,256},{128,384},{256,0},{384,128},{1,257},{129,385},{257,1},{385... | collective-permute-start | bytes 442376 | tf_op jit(solution)/shard_map/ppermute | solution.py:531
  9.8 2.7 %collective-permute-start.1 = (bf16[72,1024]{1,0:T(8,128)(2,1)S(1)}, bf16[72,1024]{1,0:T(8,128)(2,1)S(1)}, u32[]{:S(2)}, u32[]{:S(2)}) collective-permute-start(bf16[72,1024]{1,0:T(8,128)(2,1)S(1)} %get-tuple-element.61), channel_id=1, source_target_pairs={{0,128},{128,0},{256,384},{384,256},{1,129},{129,1},{257,385},{385... | collective-permute-start | bytes 442376 | tf_op jit(solution)/shard_map/ppermute | solution.py:531
  12.5 0.8 shard_map.59
  13.3 22.8 %all_to_all.33 = s32[64,1,128]{2,1,0:T(1,128)S(1)} all-to-all(s32[64,1,128]{2,1,0:T(1,128)S(1)} %shard_map.59), channel_id=1, replica_groups=mesh['section_0'=4,'section_1'=2,'dp'=64] {'dp'}, dimensions={0} | all-to-all | bytes 65536 | tf_op jit(solution)/shard_map/all_to_all | solution.py:525
  36.1 0.0 collective-permute-done.refs_2_
  36.1 0.0 collective-permute-done.1.refs_1_
  36.1 0.0 copy-start.5
  36.1 4.3 %shard_map.61 = (bf16[64,32,128]{2,1,0:T(8,128)(2,1)}, s32[40,128]{1,0:T(8,128)S(1)}, s32[8,128]{1,0:T(8,128)S(1)}) custom-call(s32[1]{0:T(128)} %bitcast.1.section_ref, s32[64,128]{1,0:T(8,128)S(1)} %bitcast.5, bf16[8192,128]{1,0:T(8,128)(2,1)} %table_ref.1), custom_call_target="tpu_custom_call" | custom-call | tf_op jit(solution)/shard_map/pallas_call | solution.py:181
  40.4 6.0 %all-to-all-start.5 = ((bf16[64,32,128]{2,1,0:T(8,128)(2,1)}), bf16[64,32,128]{2,1,0:T(8,128)(2,1)S(1)}, u32[]{:S(2)}, u32[]{:S(2)}) async-start(bf16[64,32,128]{2,1,0:T(8,128)(2,1)} %get-tuple-element.66), calls=%async_computation.5 | async-start | bytes 1048576 | tf_op jit(solution)/shard_map/all_to_all | solution.py:555
  46.4 2.8 %collective-permute-start.2 = (bf16[72,1024]{1,0:T(8,128)(2,1)S(1)}, bf16[72,1024]{1,0:T(8,128)(2,1)S(1)}, u32[]{:S(2)}, u32[]{:S(2)}) collective-permute-start(bf16[72,1024]{1,0:T(8,128)(2,1)S(1)} %get-tuple-element.71), channel_id=1, source_target_pairs={{0,384},{128,256},{256,128},{384,0},{1,385},{129,257},{257,129},{3... | collective-permute-start | bytes 442376 | tf_op jit(solution)/shard_map/ppermute | solution.py:531
  49.2 6.4 %collective-permute-done.2.refs_3_ = bf16[72,1024]{1,0:T(8,128)(2,1)S(1)} collective-permute-done((bf16[72,1024]{1,0:T(8,128)(2,1)S(1)}, bf16[72,1024]{1,0:T(8,128)(2,1)S(1)}, u32[]{:S(2)}, u32[]{:S(2)}) %collective-permute-start.2) | collective-permute-done | bytes 147488 | tf_op jit(solution)/shard_map/ppermute | solution.py:531
  55.6 1.9 %collective-permute-start.3 = (bf16[4,72,1024]{2,1,0:T(8,128)(2,1)S(1)}, bf16[4,72,1024]{2,1,0:T(8,128)(2,1)S(1)}, u32[]{:S(2)}, u32[]{:S(2)}) collective-permute-start(bf16[4,72,1024]{2,1,0:T(8,128)(2,1)S(1)} %shard_map.62), channel_id=1, source_target_pairs={{0,64},{64,0},{1,65},{65,1},{2,66},{66,2},{3,67},{67,3},{4,68},{68... | collective-permute-start | bytes 1769480 | tf_op jit(solution)/shard_map/ppermute | solution.py:534
  57.5 0.0 copy-done.5
  57.6 1.9 %collective-permute-done.3.got_ref = bf16[4,72,1024]{2,1,0:T(8,128)(2,1)S(1)} collective-permute-done((bf16[4,72,1024]{2,1,0:T(8,128)(2,1)S(1)}, bf16[4,72,1024]{2,1,0:T(8,128)(2,1)S(1)}, u32[]{:S(2)}, u32[]{:S(2)}) %collective-permute-start.3) | collective-permute-done | bytes 589856 | tf_op jit(solution)/shard_map/ppermute | solution.py:534
  59.5 2.1 %all-to-all-done.5.rows_ref = bf16[64,32,128]{2,1,0:T(8,128)(2,1)S(1)} async-done(((bf16[64,32,128]{2,1,0:T(8,128)(2,1)}), bf16[64,32,128]{2,1,0:T(8,128)(2,1)S(1)}, u32[]{:S(2)}, u32[]{:S(2)}) %all-to-all-start.5) | async-done | bytes 524320 | tf_op jit(solution)/shard_map/all_to_all | solution.py:555
  61.6 1.2 %shard_map.63 = (bf16[4,72,1024]{2,1,0:T(8,128)(2,1)S(1)}, bf16[4,72,1024]{2,1,0:T(8,128)(2,1)S(1)}) custom-call(s32[1]{0:T(128)} %bitcast.1.section_ref, bf16[64,32,128]{2,1,0:T(8,128)(2,1)S(1)} %all-to-all-done.5.rows_ref, f32[8,1024]{1,0:T(8,128)S(1)} %reshape.25.gain_ref, bf16[72,32]{1,0:T(8,128)(2,1)S(1)} %get-tuple-element.67.expand_ref, ...), custom_call_target="tpu_custom_call" | custom-call | tf_op jit(solution)/shard_map/pallas_call | solution.py:181
  62.8 0.0 copy-start.4
  62.9 0.0 copy-start.6
  62.9 2.1 %collective-permute-start.4 = (bf16[4,72,1024]{2,1,0:T(8,128)(2,1)S(1)}, bf16[4,72,1024]{2,1,0:T(8,128)(2,1)S(1)}, u32[]{:S(2)}, u32[]{:S(2)}) collective-permute-start(bf16[4,72,1024]{2,1,0:T(8,128)(2,1)S(1)} %get-tuple-element.73.give_ref), channel_id=1, source_target_pairs={{0,64},{64,0},{1,65},{65,1},{2,66},{66,2},{3,67},{67,3},{4,68},{68... | collective-permute-start | bytes 1769480 | tf_op jit(solution)/shard_map/ppermute | solution.py:534
  64.9 1.1 %shard_map.64 = bf16[64,32,128]{2,1,0:T(8,128)(2,1)} custom-call(s32[1]{0:T(128)} %bitcast.1.section_ref, bf16[32,72]{1,0:T(8,128)(2,1)S(1)} %get-tuple-element.65.combine_ref, bf16[4,72,1024]{2,1,0:T(8,128)(2,1)S(1)} %get-tuple-element.72.keep_ref, bf16[4,72,1024]{2,1,0:T(8,128)(2,1)S(1)} %get-tuple-element.73.give_ref), custom_call_target="tpu_custom_call" | custom-call | tf_op jit(solution)/shard_map/pallas_call | solution.py:181
  66.0 0.8 collective-permute-done.4.got_ref
  66.9 0.2 shard_map.65
  67.1 11.5 %all-to-all-start.6 = ((bf16[64,32,128]{2,1,0:T(8,128)(2,1)}), bf16[64,32,128]{2,1,0:T(8,128)(2,1)S(1)}, u32[]{:S(2)}, u32[]{:S(2)}) async-start(bf16[64,32,128]{2,1,0:T(8,128)(2,1)} %shard_map.64), calls=%async_computation.6 | async-start | bytes 1048576 | tf_op jit(solution)/shard_map/all_to_all | solution.py:570
  78.6 5.1 %collective-permute-start.5 = (bf16[72,1024]{1,0:T(8,128)(2,1)S(1)}, bf16[72,1024]{1,0:T(8,128)(2,1)S(1)}, u32[]{:S(2)}, u32[]{:S(2)}) collective-permute-start(bf16[72,1024]{1,0:T(8,128)(2,1)S(1)} %get-tuple-element.81), channel_id=1, source_target_pairs={{0,256},{128,384},{256,0},{384,128},{1,257},{129,385},{257,1},{385... | collective-permute-start | bytes 442376 | tf_op jit(solution)/shard_map/ppermute | solution.py:531
  83.7 1.9 %collective-permute-start.6 = (bf16[72,1024]{1,0:T(8,128)(2,1)S(1)}, bf16[72,1024]{1,0:T(8,128)(2,1)S(1)}, u32[]{:S(2)}, u32[]{:S(2)}) collective-permute-start(bf16[72,1024]{1,0:T(8,128)(2,1)S(1)} %get-tuple-element.82), channel_id=1, source_target_pairs={{0,128},{128,0},{256,384},{384,256},{1,129},{129,1},{257,385},{385... | collective-permute-start | bytes 442376 | tf_op jit(solution)/shard_map/ppermute | solution.py:531
  85.6 5.2 %collective-permute-start.7 = (bf16[72,1024]{1,0:T(8,128)(2,1)S(1)}, bf16[72,1024]{1,0:T(8,128)(2,1)S(1)}, u32[]{:S(2)}, u32[]{:S(2)}) collective-permute-start(bf16[72,1024]{1,0:T(8,128)(2,1)S(1)} %get-tuple-element.83), channel_id=1, source_target_pairs={{0,384},{128,256},{256,128},{384,0},{1,385},{129,257},{257,129},{3... | collective-permute-start | bytes 442376 | tf_op jit(solution)/shard_map/ppermute | solution.py:531
  90.8 0.6 slice_reduce_fusion
  92.1 2.6 %all-to-all-done.6 = bf16[64,32,128]{2,1,0:T(8,128)(2,1)S(1)} async-done(((bf16[64,32,128]{2,1,0:T(8,128)(2,1)}), bf16[64,32,128]{2,1,0:T(8,128)(2,1)S(1)}, u32[]{:S(2)}, u32[]{:S(2)}) %all-to-all-start.6) | async-done | bytes 524320 | tf_op jit(solution)/shard_map/all_to_all | solution.py:570
  94.7 0.0 copy-done.4
  94.7 0.0 copy-done.6
  94.7 3.8 %conditional.1 = (bf16[8192,128]{1,0:T(8,128)(2,1)S(1)}, bf16[128,1024]{1,0:T(8,128)(2,1)S(1)}) conditional(s32[]{:T(128)} %convert_element_type.4, (s32[64,128]{1,0:T(8,128)S(1)}, s32[1]{0:T(128)}, bf16[8192,128]{1,0:T(8,128)(2,1)}, s32[1,128]{1,0:T(1,128)S(1)}, bf16[128,1024]{1,0:T(8,128)(2,1)S(1)}, /*index=5*/f32[8192]{0:T(1024)S(1)}) %tuple.30, ...), branch_computations={%region_1.2_spmd, %region_2.3_spmd} | conditional | flops 90112 | bytes 46203044 | solution.py:584
  94.7 3.8 %branch_1_fun.1 = bf16[8192,128]{1,0:T(8,128)(2,1)S(1)} custom-call(s32[40,128]{1,0:T(8,128)S(1)} %get-tuple-element.26.plan_ref, bf16[64,32,128]{2,1,0:T(8,128)(2,1)S(1)} %get-tuple-element.27.grads_ref), custom_call_target="tpu_custom_call" | custom-call | tf_op jit(solution)/shard_map/cond/branch_1_fun/pallas_call | solution.py:181
  98.6 0.0 copy-start.3
  98.6 0.0 collective-permute-done.5.refs_2_
  98.6 1.1 %collective-permute-done.6.refs_1_ = bf16[72,1024]{1,0:T(8,128)(2,1)S(1)} collective-permute-done((bf16[72,1024]{1,0:T(8,128)(2,1)S(1)}, bf16[72,1024]{1,0:T(8,128)(2,1)S(1)}, u32[]{:S(2)}, u32[]{:S(2)}) %collective-permute-start.6) | collective-permute-done | bytes 147488 | tf_op jit(solution)/shard_map/ppermute | solution.py:531
  99.6 0.0 collective-permute-done.7.refs_3_
  99.7 1.3 %shard_map.66.fast_ref = bf16[128,1024]{1,0:T(8,128)(2,1)} custom-call(s32[1]{0:T(128)} %bitcast.1.section_ref, s32[1,128]{1,0:T(1,128)S(1)} %bitcast.11, bf16[72,1024]{1,0:T(8,128)(2,1)S(1)} %get-tuple-element.85.refs_0_, bf16[72,1024]{1,0:T(8,128)(2,1)S(1)} %collective-permute-done.6.refs_1_, bf16[72,1024]{1,0:T(8,128)(2,1)S(1)} %collective-permute-done.5.refs_2_, ...), custom_call_target="tpu_custom_call" | custom-call | tf_op jit(solution)/shard_map/pallas_call | solution.py:181
  101.0 0.0 copy-done.3
  (4 shorter events, 0.1 us)
Async XLA Ops:
  2.1 34.0 %collective-permute-start = (bf16[72,1024]{1,0:T(8,128)(2,1)S(1)}, bf16[72,1024]{1,0:T(8,128)(2,1)S(1)}, u32[]{:S(2)}, u32[]{:S(2)}) collective-permute-start(bf16[72,1024]{1,0:T(8,128)(2,1)S(1)} %get-tuple-element.60), channel_id=1, source_target_pairs={{0,256},{128,384},{256,0},{384,128},{1,257},{129,385},{257,1},{385... | collective-permute-start | bytes 442376 | tf_op jit(solution)/shard_map/ppermute | solution.py:531
  9.8 26.3 %collective-permute-start.1 = (bf16[72,1024]{1,0:T(8,128)(2,1)S(1)}, bf16[72,1024]{1,0:T(8,128)(2,1)S(1)}, u32[]{:S(2)}, u32[]{:S(2)}) collective-permute-start(bf16[72,1024]{1,0:T(8,128)(2,1)S(1)} %get-tuple-element.61), channel_id=1, source_target_pairs={{0,128},{128,0},{256,384},{384,256},{1,129},{129,1},{257,385},{385... | collective-permute-start | bytes 442376 | tf_op jit(solution)/shard_map/ppermute | solution.py:531
  36.1 21.4 %copy-start.5 = (f32[8192]{0:T(1024)S(1)}, f32[8192]{0:T(1024)}, u32[]{:S(2)}) copy-start(f32[8192]{0:T(1024)} %param.8) | copy-start | bytes 98308
  40.4 21.2 %all-to-all-start.5 = ((bf16[64,32,128]{2,1,0:T(8,128)(2,1)}), bf16[64,32,128]{2,1,0:T(8,128)(2,1)S(1)}, u32[]{:S(2)}, u32[]{:S(2)}) async-start(bf16[64,32,128]{2,1,0:T(8,128)(2,1)} %get-tuple-element.66), calls=%async_computation.5 | async-start | bytes 1048576 | tf_op jit(solution)/shard_map/all_to_all | solution.py:555
  46.4 9.1 %collective-permute-start.2 = (bf16[72,1024]{1,0:T(8,128)(2,1)S(1)}, bf16[72,1024]{1,0:T(8,128)(2,1)S(1)}, u32[]{:S(2)}, u32[]{:S(2)}) collective-permute-start(bf16[72,1024]{1,0:T(8,128)(2,1)S(1)} %get-tuple-element.71), channel_id=1, source_target_pairs={{0,384},{128,256},{256,128},{384,0},{1,385},{129,257},{257,129},{3... | collective-permute-start | bytes 442376 | tf_op jit(solution)/shard_map/ppermute | solution.py:531
  55.6 3.9 %collective-permute-start.3 = (bf16[4,72,1024]{2,1,0:T(8,128)(2,1)S(1)}, bf16[4,72,1024]{2,1,0:T(8,128)(2,1)S(1)}, u32[]{:S(2)}, u32[]{:S(2)}) collective-permute-start(bf16[4,72,1024]{2,1,0:T(8,128)(2,1)S(1)} %shard_map.62), channel_id=1, source_target_pairs={{0,64},{64,0},{1,65},{65,1},{2,66},{66,2},{3,67},{67,3},{4,68},{68... | collective-permute-start | bytes 1769480 | tf_op jit(solution)/shard_map/ppermute | solution.py:534
  62.8 31.9 %copy-start.4 = (bf16[128,1024]{1,0:T(8,128)(2,1)S(1)}, bf16[128,1024]{1,0:T(8,128)(2,1)}, u32[]{:S(2)}) copy-start(bf16[128,1024]{1,0:T(8,128)(2,1)} %cotangent_ref.1) | copy-start | bytes 786436
  62.9 31.9 %copy-start.6 = (s32[128]{0:T(128)S(1)}, s32[128]{0:T(128)}, u32[]{:S(2)}) copy-start(s32[128]{0:T(128)} %param.6) | copy-start | bytes 1540
  62.9 4.0 %collective-permute-start.4 = (bf16[4,72,1024]{2,1,0:T(8,128)(2,1)S(1)}, bf16[4,72,1024]{2,1,0:T(8,128)(2,1)S(1)}, u32[]{:S(2)}, u32[]{:S(2)}) collective-permute-start(bf16[4,72,1024]{2,1,0:T(8,128)(2,1)S(1)} %get-tuple-element.73.give_ref), channel_id=1, source_target_pairs={{0,64},{64,0},{1,65},{65,1},{2,66},{66,2},{3,67},{67,3},{4,68},{68... | collective-permute-start | bytes 1769480 | tf_op jit(solution)/shard_map/ppermute | solution.py:534
  67.1 27.7 %all-to-all-start.6 = ((bf16[64,32,128]{2,1,0:T(8,128)(2,1)}), bf16[64,32,128]{2,1,0:T(8,128)(2,1)S(1)}, u32[]{:S(2)}, u32[]{:S(2)}) async-start(bf16[64,32,128]{2,1,0:T(8,128)(2,1)} %shard_map.64), calls=%async_computation.6 | async-start | bytes 1048576 | tf_op jit(solution)/shard_map/all_to_all | solution.py:570
  78.6 20.0 %collective-permute-start.5 = (bf16[72,1024]{1,0:T(8,128)(2,1)S(1)}, bf16[72,1024]{1,0:T(8,128)(2,1)S(1)}, u32[]{:S(2)}, u32[]{:S(2)}) collective-permute-start(bf16[72,1024]{1,0:T(8,128)(2,1)S(1)} %get-tuple-element.81), channel_id=1, source_target_pairs={{0,256},{128,384},{256,0},{384,128},{1,257},{129,385},{257,1},{385... | collective-permute-start | bytes 442376 | tf_op jit(solution)/shard_map/ppermute | solution.py:531
  83.7 16.0 %collective-permute-start.6 = (bf16[72,1024]{1,0:T(8,128)(2,1)S(1)}, bf16[72,1024]{1,0:T(8,128)(2,1)S(1)}, u32[]{:S(2)}, u32[]{:S(2)}) collective-permute-start(bf16[72,1024]{1,0:T(8,128)(2,1)S(1)} %get-tuple-element.82), channel_id=1, source_target_pairs={{0,128},{128,0},{256,384},{384,256},{1,129},{129,1},{257,385},{385... | collective-permute-start | bytes 442376 | tf_op jit(solution)/shard_map/ppermute | solution.py:531
  85.6 14.0 %collective-permute-start.7 = (bf16[72,1024]{1,0:T(8,128)(2,1)S(1)}, bf16[72,1024]{1,0:T(8,128)(2,1)S(1)}, u32[]{:S(2)}, u32[]{:S(2)}) collective-permute-start(bf16[72,1024]{1,0:T(8,128)(2,1)S(1)} %get-tuple-element.83), channel_id=1, source_target_pairs={{0,384},{128,256},{256,128},{384,0},{1,385},{129,257},{257,129},{3... | collective-permute-start | bytes 442376 | tf_op jit(solution)/shard_map/ppermute | solution.py:531
  98.6 2.4 %copy-start.3 = (bf16[8192,128]{1,0:T(8,128)(2,1)}, bf16[8192,128]{1,0:T(8,128)(2,1)S(1)}, u32[]{:S(2)}) copy-start(bf16[8192,128]{1,0:T(8,128)(2,1)S(1)} %get-tuple-element.58) | copy-start | bytes 6291460
